TPU v7x, 256 devices: a whole 4x4x8 slice. The times are simulated.
256 devices in a mesh: owner: 16 (over z, core), helper: 16 (over y, x).
Axes of the slice: x: 4, y: 4, z: 8, core: 2. Of those that a mesh axis runs over, the one named last changes fastest.
Arguments:
- points: bfloat16 [1024, 64, 512], P(('owner', 'helper')), may hold values from -1.5 to 1.5
- weights: bfloat16 [1024, 16, 512], P(('owner', 'helper')), may hold values from -6 to 6
- neighbours: int32 [1024, 48], P(('owner', 'helper')), may hold values from -1 to 1023, as said below
- counts: int32 [1024], P(('owner', 'helper')), may hold values from 1 to 48, as said below
Outputs:
- potential: float32 [1024, 16, 512], P(('owner', 'helper'))
Inputs may be any that keep to these rules, and one draw needn't show every extreme that they name: `neighbours`: slot 0 of a leaf's list holds the leaf itself; slots 0 to counts - 1 hold distinct leaves, each in the same group of 64 consecutive leaves as the listed leaf or in the group just before or just after it; all other slots hold -1. `counts`: some leaf has a full list in every draw.
All inputs are finite; a program needn't handle non-finite values.
Results may differ from a plain program's by a relative error of at most 0.0028.
Values may be sent and summed in bfloat16 or wider, within the bound.
No kernel may reach another device: no remote copies, remote signals or barrier semaphores. Data moves between devices by JAX's collectives and lax.ppermute only.
A program may use at most 64 MiB of HBM per device.

v0:
```python
import functools

import jax
import jax.numpy as jnp
from jax import lax
from jax.experimental import pallas as pl
from jax.experimental.pallas import tpu as pltpu
from jax.sharding import PartitionSpec as P


LOG2E = 1.4426950408889634
SIDE = 4
LOCAL = 4
GROUP = LOCAL * SIDE * SIDE
UNROLL = 4
CHUNK = 128
PRE = 128
AT_ONCE = 4
TILE = 16
LISTS = 12
UNUSED = 255


def moved(value, step, along):
    pairs = []
    for h in range(SIDE * SIDE):
        r, c = divmod(h, SIDE)
        if along == 0:
            to = ((r + step) % SIDE) * SIDE + c
        else:
            to = r * SIDE + (c + step) % SIDE
        pairs.append((h, to))
    return lax.ppermute(value, "helper", pairs)


def nn(a, b):
    return lax.dot_general(
        a, b, (((1,), (0,)), ((), ())), preferred_element_type=jnp.float32
    )


def tn(a, b):
    return lax.dot_general(
        a, b, (((0,), (0,)), ((), ())), preferred_element_type=jnp.float32
    )


def pack_kernel(first_ref, points, weights, lists, counts, s_out, t_out, tile):
    dims = points.shape[1]
    slots = lists.shape[1]
    top = LOCAL * dims
    for i in range(LOCAL):
        coords = points[i]
        s_out[i * dims : (i + 1) * dims] = coords
        t_out[i * dims : (i + 1) * dims] = coords
        wide = coords.astype(jnp.float32)
        n = jnp.sum(wide * wide, axis=0, keepdims=True)
        high = n.astype(jnp.bfloat16).astype(jnp.float32)
        rest = n - high
        middle = rest.astype(jnp.bfloat16).astype(jnp.float32)
        tile[3 * i : 3 * i + 1] = high
        tile[3 * i + 1 : 3 * i + 2] = middle
        tile[3 * i + 2 : 3 * i + 3] = rest - middle
        at = top + TILE + i * weights.shape[1]
        s_out[at : at + weights.shape[1]] = weights[i]
    tile[LISTS : LISTS + 3] = jnp.ones((3, tile.shape[1]), jnp.float32)
    tile[LISTS + 3 :] = jnp.zeros((1, tile.shape[1]), jnp.float32)
    s_out[top : top + TILE] = tile[...].astype(jnp.bfloat16)
    tile[LISTS:] = jnp.zeros((LOCAL, tile.shape[1]), jnp.float32)
    slot = lax.broadcasted_iota(jnp.int32, (LOCAL, slots), 1)
    size = counts[...]
    near = jnp.where(slot < size, lists[...] - first_ref[0], UNUSED)
    tile[LISTS:, :slots] = near.astype(jnp.float32)
    tile[LISTS:, slots : slots + 1] = size.astype(jnp.float32)
    t_out[top:] = tile[...].astype(jnp.bfloat16)


def target_kernel(slots, me_ref, *refs):
    blocks, refs = refs[:SIDE], refs[SIDE:]
    tgt, own_ref, far_ref, count_ref, tile, norm, keys, keys_s, sem = refs
    dims = tgt.shape[1] - TILE
    top = LOCAL * dims
    norm[...] = jnp.zeros_like(norm)
    for b, ref in enumerate(blocks):
        tile[...] = ref[top:].astype(jnp.float32)
        keys[b * LOCAL : (b + 1) * LOCAL] = tile[LISTS:, :128].astype(jnp.int32)
    s = keys[...]
    g, h, i = s >> 6, (s >> 2) & 15, s & 3
    used = s < UNUSED
    lane = lax.broadcasted_iota(jnp.int32, s.shape, 1)
    t = lax.broadcasted_iota(jnp.int32, s.shape, 0)
    block = ((me_ref[0] - (h >> 2)) & 3) * LOCAL + i
    slot = jnp.where(used, block + jnp.where(g == 2, SIDE * LOCAL, 0), 0)
    mine = used & ((h & 3) == me_ref[1])
    kind = jnp.where(mine, jnp.where(g == 1, 0, 1), 2)
    key = (kind << 24) | (t << 16) | (t << 8) | slot
    keys[...] = jnp.where(lane == slots, s, key)
    copy = pltpu.make_async_copy(keys, keys_s, sem)
    copy.start()
    for b, ref in enumerate(blocks):
        tile[...] = ref[top:].astype(jnp.float32)
        for j in range(LOCAL):
            tgt[b * LOCAL + j, :dims] = ref[j * dims : (j + 1) * dims]
            norm[LISTS : LISTS + 3] = -0.5 * tile[3 * j : 3 * j + 3]
            tgt[b * LOCAL + j, dims:] = norm[...].astype(jnp.bfloat16)
    copy.wait()

    def per_target(t, carry):
        def some(q, carry):
            own, far = carry
            for u in range(AT_ONCE):
                key = keys_s[t, AT_ONCE * q + u]
                kind = key >> 24
                own_ref[own] = key & 0xFFFFFF
                far_ref[far] = key & 0xFFFFFF
                own = own + jnp.where(kind == 0, 1, 0)
                far = far + jnp.where(kind == 1, 1, 0)
            return own, far

        turns = (keys_s[t, slots] + (AT_ONCE - 1)) >> 2
        return lax.fori_loop(0, turns, some, carry)

    targets = SIDE * LOCAL
    own, far = lax.fori_loop(0, targets, per_target, (jnp.int32(0), jnp.int32(0)))
    count_ref[0] = own
    count_ref[1] = far
    for u in range(UNROLL + 2):
        own_ref[own + u] = jnp.int32(targets << 16)
        far_ref[far + u] = jnp.int32(targets << 16)


def pair_kernel(which, places, last, count_ref, keys_ref, *refs):
    n_refs = 1 + max(p[0] for p in places)
    source_refs, refs = refs[:n_refs], refs[n_refs:]
    tgt, refs = refs[0], refs[1:]
    if last:
        start_ref, refs = refs[0], refs[1:]
    out_refs, refs = refs[: SIDE if last else 1], refs[SIDE if last else 1 :]
    src, acc, sel, k0, k1, s0, s1 = refs
    dims = tgt.shape[1] - TILE
    width = tgt.shape[2]
    targets = tgt.shape[0]
    top = LOCAL * dims
    rows_of_block = src.shape[1]
    vectors = acc.shape[1]
    kb, sb = (k0, k1), (s0, s1)

    for b, (operand, at) in enumerate(places):
        src[b] = source_refs[operand][at : at + rows_of_block]
    row = lax.broadcasted_iota(jnp.int32, (TILE, width), 0)
    for i in range(LOCAL):
        on = (row >= 3 * i) & (row < 3 * i + 3)
        sel[i] = jnp.where(on, jnp.float32(-0.5), jnp.float32(0.0)).astype(jnp.bfloat16)
    if last:
        acc[:targets] = start_ref[...]
    else:
        acc[:targets] = jnp.zeros((targets,) + acc.shape[1:], jnp.float32)
    acc[targets] = jnp.zeros(acc.shape[1:], jnp.float32)
    k1[...] = jnp.zeros_like(k1)

    def picked(p):
        key = keys_ref[p]
        return (key >> 2) & 63, key & 3, (key >> 8) & 255, key >> 16

    def left(b, i, lo, hi):
        at = pl.multiple_of(i * dims, dims)
        return jnp.concatenate(
            [src[b, pl.ds(at, dims), lo:hi], src[b, top : top + TILE, lo:hi]], axis=0
        )

    def right(i, t):
        return jnp.concatenate([tgt[t, :dims], tgt[t, dims:] + sel[i]], axis=0)

    def ahead(p, buffer):
        b, i, t, _ = picked(p)
        rows = right(i, t)
        for lo in range(0, PRE, CHUNK):
            buffer[lo : lo + CHUNK] = tn(left(b, i, lo, lo + CHUNK), rows)

    def gauss(e):
        return jnp.exp2(e * LOG2E).astype(jnp.bfloat16)

    def step(p, k_in, k_out, s_now, s_next):
        b, i, t, _ = picked(p)
        rows = right(i, t)
        for lo in range(0, PRE, CHUNK):
            k_out[lo : lo + CHUNK] = gauss(s_now[lo : lo + CHUNK])
        for lo in range(PRE, width, CHUNK):
            k_out[lo : lo + CHUNK] = gauss(tn(left(b, i, lo, lo + CHUNK), rows))
        ahead(p + 1, s_next)
        b, i, _, a = picked(jnp.maximum(p - 1, 0))
        at = pl.multiple_of(top + TILE + i * vectors, vectors)
        acc[a] += nn(src[b, pl.ds(at, vectors)], k_in[...])

    ahead(0, s0)

    def body(h, carry):
        for u in range(UNROLL):
            step(
                UNROLL * h + u,
                kb[(u + 1) % 2],
                kb[u % 2],
                sb[u % 2],
                sb[(u + 1) % 2],
            )
        return carry

    lax.fori_loop(0, (count_ref[which] + UNROLL) // UNROLL, body, 0)
    if last:
        for d, ref in enumerate(out_refs):
            ref[...] = acc[d * LOCAL : (d + 1) * LOCAL].astype(ref.dtype)
    else:
        out_refs[0][...] = acc[:targets]


SMEM = pl.BlockSpec(memory_space=pltpu.SMEM)
VMEM = pl.BlockSpec(memory_space=pltpu.VMEM)


def pair_sums(which, count, keys, operands, places, tgt, vectors, start=None):
    targets, deep, width = tgt.shape
    dims = deep - TILE
    rows = LOCAL * (dims + vectors) + TILE
    last = start is not None
    if last:
        part = (LOCAL, vectors, width)
        out = [jax.ShapeDtypeStruct(part, jnp.float32)]
        out += [jax.ShapeDtypeStruct(part, jnp.bfloat16)] * (SIDE - 1)
    else:
        out = [jax.ShapeDtypeStruct((targets, vectors, width), jnp.float32)]
    pairs = 40
    return pl.pallas_call(
        functools.partial(pair_kernel, which, places, last),
        out_shape=out,
        in_specs=[SMEM, SMEM] + [VMEM] * (len(operands) + 1 + last),
        out_specs=[VMEM] * len(out),
        scratch_shapes=[
            pltpu.VMEM((len(places), rows, width), jnp.bfloat16),
            pltpu.VMEM((targets + 1, vectors, width), jnp.float32),
            pltpu.VMEM((LOCAL, TILE, width), jnp.bfloat16),
            pltpu.VMEM((width, width), jnp.bfloat16),
            pltpu.VMEM((width, width), jnp.bfloat16),
            pltpu.VMEM((PRE, width), jnp.float32),
            pltpu.VMEM((PRE, width), jnp.float32),
        ],
        compiler_params=pltpu.CompilerParams(vmem_limit_bytes=28 << 20),
        cost_estimate=pl.CostEstimate(
            flops=2 * pairs * width * width * deep,
            transcendentals=pairs * width * width,
            bytes_accessed=len(places) * rows * width * 2,
        ),
        name="pairs_far" if last else "pairs_own",
    )(count, keys, *operands, tgt, *((start,) if last else ()))


def potentials(points, weights, neighbours, counts):
    local, dims, width = points.shape
    vectors = weights.shape[1]
    slots = neighbours.shape[1]
    owners = lax.axis_size("owner")
    helper = lax.axis_index("helper")
    first_leaf = (lax.axis_index("owner") - 1) * GROUP
    up = [(i, (i + 1) % owners) for i in range(owners)]
    down = [(j, i) for i, j in up]

    rows = local * (dims + vectors) + TILE
    source, target = pl.pallas_call(
        pack_kernel,
        out_shape=(
            jax.ShapeDtypeStruct((rows, width), jnp.bfloat16),
            jax.ShapeDtypeStruct((local * dims + TILE, width), jnp.bfloat16),
        ),
        in_specs=[SMEM] + [VMEM] * 4,
        out_specs=(VMEM, VMEM),
        scratch_shapes=[pltpu.VMEM((TILE, width), jnp.float32)],
        compiler_params=pltpu.CompilerParams(vmem_limit_bytes=4 << 20),
        name="pack",
    )(first_leaf[None], points, weights, neighbours, counts[:, None])

    order = (1, 3, 2)
    row = {0: target}
    for d in order:
        row[d] = moved(target, d, 1)
    column = {0: source}
    for d in order:
        column[d] = moved(source, d, 0)
    sides = []
    for ring in (up, down):
        sides.append([lax.ppermute(source, "owner", ring)])
    near = jnp.concatenate([column[1], column[3]], axis=0)
    for ring, side in zip((up, down), sides):
        side.append(lax.ppermute(near, "owner", ring))

    room = SIDE * local * slots + 8
    me = jnp.stack([helper // SIDE, helper % SIDE]).astype(jnp.int32)
    tgt, own, far, count = pl.pallas_call(
        functools.partial(target_kernel, slots),
        out_shape=(
            jax.ShapeDtypeStruct((SIDE * local, dims + TILE, width), jnp.bfloat16),
            jax.ShapeDtypeStruct((room,), jnp.int32),
            jax.ShapeDtypeStruct((room,), jnp.int32),
            jax.ShapeDtypeStruct((2,), jnp.int32),
        ),
        in_specs=[SMEM] + [VMEM] * SIDE,
        out_specs=(VMEM, SMEM, SMEM, SMEM),
        scratch_shapes=[
            pltpu.VMEM((TILE, width), jnp.float32),
            pltpu.VMEM((TILE, width), jnp.float32),
            pltpu.VMEM((SIDE * local, 128), jnp.int32),
            pltpu.SMEM((SIDE * local, 128), jnp.int32),
            pltpu.SemaphoreType.DMA,
        ],
        compiler_params=pltpu.CompilerParams(vmem_limit_bytes=8 << 20),
        name="targets",
    )(me, *[row[d] for d in range(SIDE)])
    opposite, tgt, own, far, count = lax.optimization_barrier(
        (column[2], tgt, own, far, count)
    )
    for ring, side in zip((up, down), sides):
        side.append(lax.ppermute(opposite, "owner", ring))

    (total,) = pair_sums(
        0,
        count,
        own,
        [source, column[1], opposite, column[3]],
        tuple((d, 0) for d in range(SIDE)),
        tgt,
        vectors,
    )
    places = []
    for s in range(2):
        places += [(3 * s, 0), (3 * s + 1, 0), (3 * s + 2, 0), (3 * s + 1, rows)]
    parts = pair_sums(
        1, count, far, sides[0] + sides[1], tuple(places), tgt, vectors, total
    )
    result = parts[0]
    for d in order:
        result = result + moved(parts[d], -d, 1).astype(jnp.float32)
    return result


def solution(mesh):
    placed = (
        P(("owner", "helper"), None, None),
        P(("owner", "helper"), None, None),
        P(("owner", "helper"), None),
        P(("owner", "helper")),
    )
    return jax.shard_map(
        potentials,
        mesh=mesh,
        in_specs=placed,
        out_specs=P(("owner", "helper"), None, None),
        check_vma=False,
    )
```

profile of v0, /device:TPU:16, one launch (start us, length us, event | category | flops | bytes accessed | tf_op | source)
XLA Modules:
  0.0 76.3 jit_solution(17616629746667233483)
XLA Ops:
  0.0 0.7 copy.5.counts
  0.7 0.0 copy-start
  0.7 0.9 %copy-done = bf16[4,64,512]{2,1,0:T(8,128)(2,1)S(1)} copy-done((bf16[4,64,512]{2,1,0:T(8,128)(2,1)S(1)}, bf16[4,64,512]{2,1,0:T(8,128)(2,1)}, u32[]{:S(2)}) %copy-start) | copy-done | bytes 262168
  1.7 0.0 copy-start.1
  1.7 0.8 %copy-done.1 = bf16[4,16,512]{2,1,0:T(8,128)(2,1)S(1)} copy-done((bf16[4,16,512]{2,1,0:T(8,128)(2,1)S(1)}, bf16[4,16,512]{2,1,0:T(8,128)(2,1)}, u32[]{:S(2)}) %copy-start.1) | copy-done | bytes 65560
  2.5 0.0 copy-start.2
  2.5 0.7 copy-done.2
  3.2 0.1 pack.1
  3.3 1.4 %collective-permute-start.5 = (bf16[336,512]{1,0:T(8,128)(2,1)S(1)}, bf16[336,512]{1,0:T(8,128)(2,1)S(1)}, u32[]{:S(2)}, u32[]{:S(2)}) collective-permute-start(bf16[336,512]{1,0:T(8,128)(2,1)S(1)} %get-tuple-element.20.refs_0_), channel_id=1, source_target_pairs={{0,4},{1,5},{2,6},{3,7},{4,8},{5,9},{6,10},{7,11},{8,12},{9,13},{1... | collective-permute-start | bytes 1032200 | tf_op jit(solution)/shard_map/ppermute | solution.py:33
  4.7 0.7 collective-permute-start.6
  5.4 1.5 %collective-permute-start.1 = (bf16[272,512]{1,0:T(8,128)(2,1)S(1)}, bf16[272,512]{1,0:T(8,128)(2,1)S(1)}, u32[]{:S(2)}, u32[]{:S(2)}) collective-permute-start(bf16[272,512]{1,0:T(8,128)(2,1)S(1)} %get-tuple-element.21.refs_0_), channel_id=1, source_target_pairs={{0,1},{1,2},{2,3},{3,0},{4,5},{5,6},{6,7},{7,4},{8,9},{9,10},{10,1... | collective-permute-start | bytes 835592 | tf_op jit(solution)/shard_map/ppermute | solution.py:33
  6.9 2.7 %collective-permute-start.2 = (bf16[272,512]{1,0:T(8,128)(2,1)S(1)}, bf16[272,512]{1,0:T(8,128)(2,1)S(1)}, u32[]{:S(2)}, u32[]{:S(2)}) collective-permute-start(bf16[272,512]{1,0:T(8,128)(2,1)S(1)} %get-tuple-element.21.refs_0_), channel_id=1, source_target_pairs={{0,2},{1,3},{2,0},{3,1},{4,6},{5,7},{6,4},{7,5},{8,10},{9,11},{10,... | collective-permute-start | bytes 835592 | tf_op jit(solution)/shard_map/ppermute | solution.py:33
  9.6 1.5 %collective-permute-start = (bf16[336,512]{1,0:T(8,128)(2,1)S(1)}, bf16[336,512]{1,0:T(8,128)(2,1)}, u32[]{:S(2)}, u32[]{:S(2)}) collective-permute-start(bf16[336,512]{1,0:T(8,128)(2,1)S(1)} %get-tuple-element.20.refs_0_), channel_id=1, source_target_pairs={{0,8},{1,9},{2,10},{3,11},{4,12},{5,13},{6,14},{7,15},{8,0},{9,1},... | collective-permute-start | bytes 1032200 | tf_op jit(solution)/shard_map/ppermute | solution.py:33
  11.2 9.4 %collective-permute-done.5.refs_1_ = bf16[336,512]{1,0:T(8,128)(2,1)S(1)} collective-permute-done((bf16[336,512]{1,0:T(8,128)(2,1)S(1)}, bf16[336,512]{1,0:T(8,128)(2,1)S(1)}, u32[]{:S(2)}, u32[]{:S(2)}) %collective-permute-start.5) | collective-permute-done | bytes 344096 | tf_op jit(solution)/shard_map/ppermute | solution.py:33
  20.6 0.0 collective-permute-start.4
  20.6 0.8 constant_dynamic-update-slice_fusion.1
  21.3 0.0 collective-permute-done.6.refs_3_
  21.3 0.8 %constant_dynamic-update-slice_fusion = bf16[672,512]{1,0:T(8,128)(2,1)} fusion(bf16[672,512]{1,0:T(8,128)(2,1)} %constant_dynamic-update-slice_fusion.1, bf16[336,512]{1,0:T(8,128)(2,1)S(1)} %collective-permute-done.6.refs_3_), kind=kLoop, calls=%fused_computation.1 | loop fusion | bytes 688128 | tf_op jit(solution)/shard_map/concatenate | solution.py:290
  22.1 3.0 %collective-permute-start.10 = (bf16[672,512]{1,0:T(8,128)(2,1)}, bf16[672,512]{1,0:T(8,128)(2,1)S(1)}, u32[]{:S(2)}, u32[]{:S(2)}) collective-permute-start(bf16[672,512]{1,0:T(8,128)(2,1)} %constant_dynamic-update-slice_fusion), channel_id=1, source_target_pairs={{16,0},{32,16},{48,32},{64,48},{80,64},{96,80},{112,96},{128,112},... | collective-permute-start | bytes 2064392 | tf_op jit(solution)/shard_map/ppermute | solution.py:292
  25.0 0.0 collective-permute-done.1.refs_1_
  25.0 0.0 collective-permute-start.7
  25.0 0.0 collective-permute-done.2.refs_2_
  25.1 2.8 %collective-permute-start.3 = (bf16[272,512]{1,0:T(8,128)(2,1)S(1)}, bf16[272,512]{1,0:T(8,128)(2,1)S(1)}, u32[]{:S(2)}, u32[]{:S(2)}) collective-permute-start(bf16[272,512]{1,0:T(8,128)(2,1)S(1)} %get-tuple-element.21.refs_0_), channel_id=1, source_target_pairs={{0,3},{1,0},{2,1},{3,2},{4,7},{5,4},{6,5},{7,6},{8,11},{9,8},{10,9... | collective-permute-start | bytes 835592 | tf_op jit(solution)/shard_map/ppermute | solution.py:33
  27.9 0.1 pad_add_fusion.me_ref
  28.0 6.7 %collective-permute-done.3.refs_3_ = bf16[272,512]{1,0:T(8,128)(2,1)S(1)} collective-permute-done((bf16[272,512]{1,0:T(8,128)(2,1)S(1)}, bf16[272,512]{1,0:T(8,128)(2,1)S(1)}, u32[]{:S(2)}, u32[]{:S(2)}) %collective-permute-start.3) | collective-permute-done | bytes 278560 | tf_op jit(solution)/shard_map/ppermute | solution.py:33
  34.7 0.2 collective-permute-start.9
  34.9 4.0 %targets.1 = (bf16[16,80,512]{2,1,0:T(8,128)(2,1)S(1)}, s32[776]{0:T(1024)S(1)}, s32[776]{0:T(1024)S(1)}, s32[2]{0:T(128)S(1)}) custom-call(s32[2]{0:T(128)S(1)} %pad_add_fusion.me_ref, bf16[272,512]{1,0:T(8,128)(2,1)S(1)} %get-tuple-element.21.refs_0_, bf16[272,512]{1,0:T(8,128)(2,1)S(1)} %collective-permute-done.1.refs_1_, ...), custom_call_target="tpu_custom_call" | custom-call | tf_op jit(solution)/shard_map/targets/pallas_call | solution.py:296
  38.9 0.0 collective-permute-done.refs_2_
  38.9 2.8 %collective-permute-start.11 = (bf16[336,512]{1,0:T(8,128)(2,1)}, bf16[336,512]{1,0:T(8,128)(2,1)S(1)}, u32[]{:S(2)}, u32[]{:S(2)}) collective-permute-start(bf16[336,512]{1,0:T(8,128)(2,1)} %collective-permute-done.refs_2_), channel_id=1, source_target_pairs={{16,0},{32,16},{48,32},{64,48},{80,64},{96,80},{112,96},{128,112},... | collective-permute-start | bytes 1032200 | tf_op jit(solution)/shard_map/ppermute | solution.py:320
  41.8 0.0 collective-permute-done.4.refs_0_
  41.8 0.0 collective-permute-start.8
  41.8 9.0 %pairs_own.1.refs_7_ = f32[16,16,512]{2,1,0:T(8,128)S(1)} custom-call(s32[2]{0:T(128)S(1)} %get-tuple-element.26.count_ref, s32[776]{0:T(1024)S(1)} %get-tuple-element.30.keys_ref, bf16[336,512]{1,0:T(8,128)(2,1)S(1)} %get-tuple-element.20.refs_0_, bf16[336,512]{1,0:T(8,128)(2,1)S(1)} %collective-permute-done.5.refs_1_, ...), custom_call_target="tpu_custom_call" | custom-call | flops 1677721600 | bytes 1376256 | tf_op jit(solution)/shard_map/pairs_own/pallas_call | solution.py:232
  50.8 0.0 collective-permute-done.9.refs_3_
  50.8 0.0 collective-permute-done.11.refs_5_
  50.8 0.0 collective-permute-done.8.refs_2_
  50.8 0.0 collective-permute-done.10.refs_4_
  50.8 0.0 collective-permute-done.7.refs_1_
  50.8 9.1 %pairs_far.1 = (f32[4,16,512]{2,1,0:T(8,128)S(1)}, bf16[4,16,512]{2,1,0:T(8,128)(2,1)S(1)}, bf16[4,16,512]{2,1,0:T(8,128)(2,1)S(1)}, bf16[4,16,512]{2,1,0:T(8,128)(2,1)S(1)}) custom-call(s32[2]{0:T(128)S(1)} %get-tuple-element.26.count_ref, s32[776]{0:T(1024)S(1)} %get-tuple-element.27.keys_ref, bf16[336,512]{1,0:T(8,128)(2,1)} %collective-permute-done.4.refs_0_, ...), custom_call_target="tpu_custom_call" | custom-call | flops 1677721600 | bytes 2752512 | tf_op jit(solution)/shard_map/pairs_far/pallas_call | solution.py:232
  59.9 9.5 %collective-permute-start.12 = (bf16[4,16,512]{2,1,0:T(8,128)(2,1)S(1)}, bf16[4,16,512]{2,1,0:T(8,128)(2,1)S(1)}, u32[]{:S(2)}, u32[]{:S(2)}) collective-permute-start(bf16[4,16,512]{2,1,0:T(8,128)(2,1)S(1)} %get-tuple-element.32), channel_id=1, source_target_pairs={{0,3},{1,0},{2,1},{3,2},{4,7},{5,4},{6,5},{7,6},{8,11},{9,8},{10,9... | collective-permute-start | bytes 196616 | tf_op jit(solution)/shard_map/ppermute | solution.py:33
  69.4 0.0 collective-permute-start.13
  69.4 1.6 %collective-permute-start.14 = (bf16[4,16,512]{2,1,0:T(8,128)(2,1)S(1)}, bf16[4,16,512]{2,1,0:T(8,128)(2,1)S(1)}, u32[]{:S(2)}, u32[]{:S(2)}) collective-permute-start(bf16[4,16,512]{2,1,0:T(8,128)(2,1)S(1)} %get-tuple-element.34), channel_id=1, source_target_pairs={{0,2},{1,3},{2,0},{3,1},{4,6},{5,7},{6,4},{7,5},{8,10},{9,11},{10,... | collective-permute-start | bytes 196616 | tf_op jit(solution)/shard_map/ppermute | solution.py:33
  71.0 0.4 collective-permute-done.12
  71.3 4.3 %collective-permute-done.13 = bf16[4,16,512]{2,1,0:T(8,128)(2,1)S(1)} collective-permute-done((bf16[4,16,512]{2,1,0:T(8,128)(2,1)S(1)}, bf16[4,16,512]{2,1,0:T(8,128)(2,1)S(1)}, u32[]{:S(2)}, u32[]{:S(2)}) %collective-permute-start.13) | collective-permute-done | bytes 65568 | tf_op jit(solution)/shard_map/ppermute | solution.py:33
  75.6 0.0 collective-permute-done.14
  75.6 0.7 convert_add_fusion
Async XLA Ops:
  0.7 0.9 %copy-start = (bf16[4,64,512]{2,1,0:T(8,128)(2,1)S(1)}, bf16[4,64,512]{2,1,0:T(8,128)(2,1)}, u32[]{:S(2)}) copy-start(bf16[4,64,512]{2,1,0:T(8,128)(2,1)} %points.1) | copy-start | bytes 786436
  1.7 0.8 %copy-start.1 = (bf16[4,16,512]{2,1,0:T(8,128)(2,1)S(1)}, bf16[4,16,512]{2,1,0:T(8,128)(2,1)}, u32[]{:S(2)}) copy-start(bf16[4,16,512]{2,1,0:T(8,128)(2,1)} %weights.1) | copy-start | bytes 196612
  2.5 0.7 copy-start.2
  3.3 17.2 %collective-permute-start.5 = (bf16[336,512]{1,0:T(8,128)(2,1)S(1)}, bf16[336,512]{1,0:T(8,128)(2,1)S(1)}, u32[]{:S(2)}, u32[]{:S(2)}) collective-permute-start(bf16[336,512]{1,0:T(8,128)(2,1)S(1)} %get-tuple-element.20.refs_0_), channel_id=1, source_target_pairs={{0,4},{1,5},{2,6},{3,7},{4,8},{5,9},{6,10},{7,11},{8,12},{9,13},{1... | collective-permute-start | bytes 1032200 | tf_op jit(solution)/shard_map/ppermute | solution.py:33
  4.7 16.7 %collective-permute-start.6 = (bf16[336,512]{1,0:T(8,128)(2,1)S(1)}, bf16[336,512]{1,0:T(8,128)(2,1)S(1)}, u32[]{:S(2)}, u32[]{:S(2)}) collective-permute-start(bf16[336,512]{1,0:T(8,128)(2,1)S(1)} %get-tuple-element.20.refs_0_), channel_id=1, source_target_pairs={{0,12},{1,13},{2,14},{3,15},{4,0},{5,1},{6,2},{7,3},{8,4},{9,5},{1... | collective-permute-start | bytes 1032200 | tf_op jit(solution)/shard_map/ppermute | solution.py:33
  5.4 19.6 %collective-permute-start.1 = (bf16[272,512]{1,0:T(8,128)(2,1)S(1)}, bf16[272,512]{1,0:T(8,128)(2,1)S(1)}, u32[]{:S(2)}, u32[]{:S(2)}) collective-permute-start(bf16[272,512]{1,0:T(8,128)(2,1)S(1)} %get-tuple-element.21.refs_0_), channel_id=1, source_target_pairs={{0,1},{1,2},{2,3},{3,0},{4,5},{5,6},{6,7},{7,4},{8,9},{9,10},{10,1... | collective-permute-start | bytes 835592 | tf_op jit(solution)/shard_map/ppermute | solution.py:33
  6.9 18.2 %collective-permute-start.2 = (bf16[272,512]{1,0:T(8,128)(2,1)S(1)}, bf16[272,512]{1,0:T(8,128)(2,1)S(1)}, u32[]{:S(2)}, u32[]{:S(2)}) collective-permute-start(bf16[272,512]{1,0:T(8,128)(2,1)S(1)} %get-tuple-element.21.refs_0_), channel_id=1, source_target_pairs={{0,2},{1,3},{2,0},{3,1},{4,6},{5,7},{6,4},{7,5},{8,10},{9,11},{10,... | collective-permute-start | bytes 835592 | tf_op jit(solution)/shard_map/ppermute | solution.py:33
  9.6 29.3 %collective-permute-start = (bf16[336,512]{1,0:T(8,128)(2,1)S(1)}, bf16[336,512]{1,0:T(8,128)(2,1)}, u32[]{:S(2)}, u32[]{:S(2)}) collective-permute-start(bf16[336,512]{1,0:T(8,128)(2,1)S(1)} %get-tuple-element.20.refs_0_), channel_id=1, source_target_pairs={{0,8},{1,9},{2,10},{3,11},{4,12},{5,13},{6,14},{7,15},{8,0},{9,1},... | collective-permute-start | bytes 1032200 | tf_op jit(solution)/shard_map/ppermute | solution.py:33
  20.6 21.2 %collective-permute-start.4 = (bf16[336,512]{1,0:T(8,128)(2,1)S(1)}, bf16[336,512]{1,0:T(8,128)(2,1)}, u32[]{:S(2)}, u32[]{:S(2)}) collective-permute-start(bf16[336,512]{1,0:T(8,128)(2,1)S(1)} %get-tuple-element.20.refs_0_), channel_id=1, source_target_pairs={{0,16},{16,32},{32,48},{48,64},{64,80},{80,96},{96,112},{112,128},... | collective-permute-start | bytes 1032200 | tf_op jit(solution)/shard_map/ppermute | solution.py:289
  22.1 28.7 %collective-permute-start.10 = (bf16[672,512]{1,0:T(8,128)(2,1)}, bf16[672,512]{1,0:T(8,128)(2,1)S(1)}, u32[]{:S(2)}, u32[]{:S(2)}) collective-permute-start(bf16[672,512]{1,0:T(8,128)(2,1)} %constant_dynamic-update-slice_fusion), channel_id=1, source_target_pairs={{16,0},{32,16},{48,32},{64,48},{80,64},{96,80},{112,96},{128,112},... | collective-permute-start | bytes 2064392 | tf_op jit(solution)/shard_map/ppermute | solution.py:292
  25.0 25.8 %collective-permute-start.7 = (bf16[672,512]{1,0:T(8,128)(2,1)}, bf16[672,512]{1,0:T(8,128)(2,1)S(1)}, u32[]{:S(2)}, u32[]{:S(2)}) collective-permute-start(bf16[672,512]{1,0:T(8,128)(2,1)} %constant_dynamic-update-slice_fusion), channel_id=1, source_target_pairs={{0,16},{16,32},{32,48},{48,64},{64,80},{80,96},{96,112},{112,128},... | collective-permute-start | bytes 2064392 | tf_op jit(solution)/shard_map/ppermute | solution.py:292
  25.1 9.7 %collective-permute-start.3 = (bf16[272,512]{1,0:T(8,128)(2,1)S(1)}, bf16[272,512]{1,0:T(8,128)(2,1)S(1)}, u32[]{:S(2)}, u32[]{:S(2)}) collective-permute-start(bf16[272,512]{1,0:T(8,128)(2,1)S(1)} %get-tuple-element.21.refs_0_), channel_id=1, source_target_pairs={{0,3},{1,0},{2,1},{3,2},{4,7},{5,4},{6,5},{7,6},{8,11},{9,8},{10,9... | collective-permute-start | bytes 835592 | tf_op jit(solution)/shard_map/ppermute | solution.py:33
  34.7 16.1 %collective-permute-start.9 = (bf16[336,512]{1,0:T(8,128)(2,1)S(1)}, bf16[336,512]{1,0:T(8,128)(2,1)S(1)}, u32[]{:S(2)}, u32[]{:S(2)}) collective-permute-start(bf16[336,512]{1,0:T(8,128)(2,1)S(1)} %get-tuple-element.20.refs_0_), channel_id=1, source_target_pairs={{16,0},{32,16},{48,32},{64,48},{80,64},{96,80},{112,96},{128,112},... | collective-permute-start | bytes 1032200 | tf_op jit(solution)/shard_map/ppermute | solution.py:289
  38.9 11.9 %collective-permute-start.11 = (bf16[336,512]{1,0:T(8,128)(2,1)}, bf16[336,512]{1,0:T(8,128)(2,1)S(1)}, u32[]{:S(2)}, u32[]{:S(2)}) collective-permute-start(bf16[336,512]{1,0:T(8,128)(2,1)} %collective-permute-done.refs_2_), channel_id=1, source_target_pairs={{16,0},{32,16},{48,32},{64,48},{80,64},{96,80},{112,96},{128,112},... | collective-permute-start | bytes 1032200 | tf_op jit(solution)/shard_map/ppermute | solution.py:320
  41.8 9.1 %collective-permute-start.8 = (bf16[336,512]{1,0:T(8,128)(2,1)}, bf16[336,512]{1,0:T(8,128)(2,1)S(1)}, u32[]{:S(2)}, u32[]{:S(2)}) collective-permute-start(bf16[336,512]{1,0:T(8,128)(2,1)} %collective-permute-done.refs_2_), channel_id=1, source_target_pairs={{0,16},{16,32},{32,48},{48,64},{64,80},{80,96},{96,112},{112,128},... | collective-permute-start | bytes 1032200 | tf_op jit(solution)/shard_map/ppermute | solution.py:320
  59.9 11.4 %collective-permute-start.12 = (bf16[4,16,512]{2,1,0:T(8,128)(2,1)S(1)}, bf16[4,16,512]{2,1,0:T(8,128)(2,1)S(1)}, u32[]{:S(2)}, u32[]{:S(2)}) collective-permute-start(bf16[4,16,512]{2,1,0:T(8,128)(2,1)S(1)} %get-tuple-element.32), channel_id=1, source_target_pairs={{0,3},{1,0},{2,1},{3,2},{4,7},{5,4},{6,5},{7,6},{8,11},{9,8},{10,9... | collective-permute-start | bytes 196616 | tf_op jit(solution)/shard_map/ppermute | solution.py:33
  69.4 6.2 %collective-permute-start.13 = (bf16[4,16,512]{2,1,0:T(8,128)(2,1)S(1)}, bf16[4,16,512]{2,1,0:T(8,128)(2,1)S(1)}, u32[]{:S(2)}, u32[]{:S(2)}) collective-permute-start(bf16[4,16,512]{2,1,0:T(8,128)(2,1)S(1)} %get-tuple-element.33), channel_id=1, source_target_pairs={{0,1},{1,2},{2,3},{3,0},{4,5},{5,6},{6,7},{7,4},{8,9},{9,10},{10,1... | collective-permute-start | bytes 196616 | tf_op jit(solution)/shard_map/ppermute | solution.py:33
  69.4 6.2 %collective-permute-start.14 = (bf16[4,16,512]{2,1,0:T(8,128)(2,1)S(1)}, bf16[4,16,512]{2,1,0:T(8,128)(2,1)S(1)}, u32[]{:S(2)}, u32[]{:S(2)}) collective-permute-start(bf16[4,16,512]{2,1,0:T(8,128)(2,1)S(1)} %get-tuple-element.34), channel_id=1, source_target_pairs={{0,2},{1,3},{2,0},{3,1},{4,6},{5,7},{6,4},{7,5},{8,10},{9,11},{10,... | collective-permute-start | bytes 196616 | tf_op jit(solution)/shard_map/ppermute | solution.py:33
where the time goes:
time: 76.6 us; the launch traced here: 76.3 us
  starting transfers between devices  27.7 us (36%)
  Pallas kernels  22.2 us (29%)
  waiting for transfers between devices  20.8 us (27%)
  local copies, waits for them, and re-layouts  4.74 us (6%)
    ppermute x9, starting transfers between devices, moved(): return lax.ppermute(value, 'helper', pairs)  21.7 us
    ppermute x9, waiting for transfers between devices, moved(): return lax.ppermute(value, 'helper', pairs)  20.8 us
    pallas_call x2, Pallas kernels, pair_sums(): pl.pallas_call(functools.partial(pair_kernel, which, places, last), out_s...  18.1 us
    pallas_call x1, Pallas kernels, potentials(): pl.pallas_call(functools.partial(target_kernel, slots), out_shape=(jax.Sh...  4.03 us
    unnamed x7, local copies, waits for them, and re-layouts  3.23 us
    ppermute x2, starting transfers between devices, potentials(): side.append(lax.ppermute(near, 'owner', ring))  2.96 us
    ppermute x2, starting transfers between devices, potentials(): side.append(lax.ppermute(opposite, 'owner', ring))  2.81 us
  transfers between devices with their start and end apart: 15, of which 4 were waited for; matrix products, arithmetic and copies ran while one was open for 2% of the time, Pallas kernels for 17%

commit v1 on v0

--- a/solution.py
+++ b/solution.py
@@ -12,7 +12,8 @@
 SIDE = 4
 LOCAL = 4
 GROUP = LOCAL * SIDE * SIDE
-UNROLL = 4
+UNROLL = 8
+TAIL = 2
 CHUNK = 128
 PRE = 128
 AT_ONCE = 4
@@ -45,13 +46,25 @@
     )
 
 
-def pack_kernel(first_ref, points, weights, lists, counts, s_out, t_out, tile):
+def pack_kernel(first_ref, counts, points, weights, lists, s_out, t_out, tile, near, sems):
     dims = points.shape[1]
+    vectors = weights.shape[1]
     slots = lists.shape[1]
     top = LOCAL * dims
+    copies = []
     for i in range(LOCAL):
-        coords = points[i]
-        s_out[i * dims : (i + 1) * dims] = coords
+        here = s_out.at[i * dims : (i + 1) * dims]
+        copies.append(pltpu.make_async_copy(points.at[i], here, sems.at[i]))
+    for i in range(LOCAL):
+        at = top + TILE + i * vectors
+        here = s_out.at[at : at + vectors]
+        copies.append(pltpu.make_async_copy(weights.at[i], here, sems.at[LOCAL + i]))
+    copies.append(pltpu.make_async_copy(lists, near, sems.at[2 * LOCAL]))
+    for copy in copies:
+        copy.start()
+    for i in range(LOCAL):
+        copies[i].wait()
+        coords = s_out[i * dims : (i + 1) * dims]
         t_out[i * dims : (i + 1) * dims] = coords
         wide = coords.astype(jnp.float32)
         n = jnp.sum(wide * wide, axis=0, keepdims=True)
@@ -61,18 +74,22 @@
         tile[3 * i : 3 * i + 1] = high
         tile[3 * i + 1 : 3 * i + 2] = middle
         tile[3 * i + 2 : 3 * i + 3] = rest - middle
-        at = top + TILE + i * weights.shape[1]
-        s_out[at : at + weights.shape[1]] = weights[i]
     tile[LISTS : LISTS + 3] = jnp.ones((3, tile.shape[1]), jnp.float32)
     tile[LISTS + 3 :] = jnp.zeros((1, tile.shape[1]), jnp.float32)
     s_out[top : top + TILE] = tile[...].astype(jnp.bfloat16)
     tile[LISTS:] = jnp.zeros((LOCAL, tile.shape[1]), jnp.float32)
-    slot = lax.broadcasted_iota(jnp.int32, (LOCAL, slots), 1)
-    size = counts[...]
-    near = jnp.where(slot < size, lists[...] - first_ref[0], UNUSED)
-    tile[LISTS:, :slots] = near.astype(jnp.float32)
-    tile[LISTS:, slots : slots + 1] = size.astype(jnp.float32)
+    copies[2 * LOCAL].wait()
+    slot = lax.broadcasted_iota(jnp.int32, (1, slots), 1)
+    for i in range(LOCAL):
+        size = counts[i]
+        place = jnp.where(slot < size, near[i : i + 1] - first_ref[0], UNUSED)
+        tile[LISTS + i : LISTS + i + 1, :slots] = place.astype(jnp.float32)
+        tile[LISTS + i : LISTS + i + 1, slots : slots + 1] = jnp.full(
+            (1, 1), size, jnp.int32
+        ).astype(jnp.float32)
     t_out[top:] = tile[...].astype(jnp.bfloat16)
+    for copy in copies[LOCAL : 2 * LOCAL]:
+        copy.wait()
 
 
 def target_kernel(slots, me_ref, *refs):
@@ -80,7 +97,8 @@
     tgt, own_ref, far_ref, count_ref, tile, norm, keys, keys_s, sem = refs
     dims = tgt.shape[1] - TILE
     top = LOCAL * dims
-    norm[...] = jnp.zeros_like(norm)
+    norm[...] = jnp.full(norm.shape, -0.5, jnp.float32)
+    norm[LISTS + 3 :] = jnp.zeros((1, norm.shape[1]), jnp.float32)
     for b, ref in enumerate(blocks):
         tile[...] = ref[top:].astype(jnp.float32)
         keys[b * LOCAL : (b + 1) * LOCAL] = tile[LISTS:, :128].astype(jnp.int32)
@@ -136,21 +154,25 @@
     if last:
         start_ref, refs = refs[0], refs[1:]
     out_refs, refs = refs[: SIDE if last else 1], refs[SIDE if last else 1 :]
-    src, acc, sel, k0, k1, s0, s1 = refs
+    src, wts, acc, k0, k1, s0, s1 = refs
     dims = tgt.shape[1] - TILE
     width = tgt.shape[2]
     targets = tgt.shape[0]
     top = LOCAL * dims
-    rows_of_block = src.shape[1]
     vectors = acc.shape[1]
     kb, sb = (k0, k1), (s0, s1)
 
+    row = lax.broadcasted_iota(jnp.int32, (TILE, width), 0)
     for b, (operand, at) in enumerate(places):
-        src[b] = source_refs[operand][at : at + rows_of_block]
-    row = lax.broadcasted_iota(jnp.int32, (TILE, width), 0)
-    for i in range(LOCAL):
-        on = (row >= 3 * i) & (row < 3 * i + 3)
-        sel[i] = jnp.where(on, jnp.float32(-0.5), jnp.float32(0.0)).astype(jnp.bfloat16)
+        block = source_refs[operand]
+        tile = block[at + top : at + top + TILE].astype(jnp.float32)
+        for i in range(LOCAL):
+            on = ((row >= 3 * i) & (row < 3 * i + 3)) | (row >= LISTS)
+            slot = b * LOCAL + i
+            src[slot, :dims] = block[at + i * dims : at + (i + 1) * dims]
+            src[slot, dims:] = jnp.where(on, tile, 0.0).astype(jnp.bfloat16)
+            first = at + top + TILE + i * vectors
+            wts[slot] = block[first : first + vectors]
     if last:
         acc[:targets] = start_ref[...]
     else:
@@ -160,52 +182,53 @@
 
     def picked(p):
         key = keys_ref[p]
-        return (key >> 2) & 63, key & 3, (key >> 8) & 255, key >> 16
-
-    def left(b, i, lo, hi):
-        at = pl.multiple_of(i * dims, dims)
-        return jnp.concatenate(
-            [src[b, pl.ds(at, dims), lo:hi], src[b, top : top + TILE, lo:hi]], axis=0
-        )
-
-    def right(i, t):
-        return jnp.concatenate([tgt[t, :dims], tgt[t, dims:] + sel[i]], axis=0)
+        return key & 255, (key >> 8) & 255, key >> 16
 
     def ahead(p, buffer):
-        b, i, t, _ = picked(p)
-        rows = right(i, t)
+        s, t, _ = picked(p)
+        rows = tgt[t]
         for lo in range(0, PRE, CHUNK):
-            buffer[lo : lo + CHUNK] = tn(left(b, i, lo, lo + CHUNK), rows)
+            buffer[lo : lo + CHUNK] = tn(src[s, :, lo : lo + CHUNK], rows)
 
     def gauss(e):
         return jnp.exp2(e * LOG2E).astype(jnp.bfloat16)
 
     def step(p, k_in, k_out, s_now, s_next):
-        b, i, t, _ = picked(p)
-        rows = right(i, t)
+        s, t, _ = picked(p)
+        rows = tgt[t]
         for lo in range(0, PRE, CHUNK):
             k_out[lo : lo + CHUNK] = gauss(s_now[lo : lo + CHUNK])
         for lo in range(PRE, width, CHUNK):
-            k_out[lo : lo + CHUNK] = gauss(tn(left(b, i, lo, lo + CHUNK), rows))
+            k_out[lo : lo + CHUNK] = gauss(tn(src[s, :, lo : lo + CHUNK], rows))
         ahead(p + 1, s_next)
-        b, i, _, a = picked(jnp.maximum(p - 1, 0))
-        at = pl.multiple_of(top + TILE + i * vectors, vectors)
-        acc[a] += nn(src[b, pl.ds(at, vectors)], k_in[...])
+        s, _, a = picked(jnp.maximum(p - 1, 0))
+        acc[a] += nn(wts[s], k_in[...])
 
     ahead(0, s0)
 
-    def body(h, carry):
-        for u in range(UNROLL):
+    def turn(first, steps):
+        for u in range(steps):
             step(
-                UNROLL * h + u,
+                first + u,
                 kb[(u + 1) % 2],
                 kb[u % 2],
                 sb[u % 2],
                 sb[(u + 1) % 2],
             )
+
+    def body(h, carry):
+        turn(UNROLL * h, UNROLL)
         return carry
 
-    lax.fori_loop(0, (count_ref[which] + UNROLL) // UNROLL, body, 0)
+    def tail(h, carry):
+        turn(whole + TAIL * h, TAIL)
+        return carry
+
+    steps = count_ref[which] + 1
+    turns = steps // UNROLL
+    whole = turns * UNROLL
+    lax.fori_loop(0, turns, body, 0)
+    lax.fori_loop(0, (steps - whole + TAIL - 1) // TAIL, tail, 0)
     if last:
         for d, ref in enumerate(out_refs):
             ref[...] = acc[d * LOCAL : (d + 1) * LOCAL].astype(ref.dtype)
@@ -215,6 +238,7 @@
 
 SMEM = pl.BlockSpec(memory_space=pltpu.SMEM)
 VMEM = pl.BlockSpec(memory_space=pltpu.VMEM)
+HBM = pl.BlockSpec(memory_space=pltpu.HBM)
 
 
 def pair_sums(which, count, keys, operands, places, tgt, vectors, start=None):
@@ -235,9 +259,9 @@
         in_specs=[SMEM, SMEM] + [VMEM] * (len(operands) + 1 + last),
         out_specs=[VMEM] * len(out),
         scratch_shapes=[
-            pltpu.VMEM((len(places), rows, width), jnp.bfloat16),
+            pltpu.VMEM((len(places) * LOCAL, deep, width), jnp.bfloat16),
+            pltpu.VMEM((len(places) * LOCAL, vectors, width), jnp.bfloat16),
             pltpu.VMEM((targets + 1, vectors, width), jnp.float32),
-            pltpu.VMEM((LOCAL, TILE, width), jnp.bfloat16),
             pltpu.VMEM((width, width), jnp.bfloat16),
             pltpu.VMEM((width, width), jnp.bfloat16),
             pltpu.VMEM((PRE, width), jnp.float32),
@@ -270,12 +294,23 @@
             jax.ShapeDtypeStruct((rows, width), jnp.bfloat16),
             jax.ShapeDtypeStruct((local * dims + TILE, width), jnp.bfloat16),
         ),
-        in_specs=[SMEM] + [VMEM] * 4,
+        in_specs=[SMEM, SMEM] + [HBM] * 3,
         out_specs=(VMEM, VMEM),
-        scratch_shapes=[pltpu.VMEM((TILE, width), jnp.float32)],
+        scratch_shapes=[
+            pltpu.VMEM((TILE, width), jnp.float32),
+            pltpu.VMEM((local, slots), jnp.int32),
+            pltpu.SemaphoreType.DMA((2 * local + 1,)),
+        ],
         compiler_params=pltpu.CompilerParams(vmem_limit_bytes=4 << 20),
         name="pack",
-    )(first_leaf[None], points, weights, neighbours, counts[:, None])
+    )(
+        first_leaf[None],
+        counts,
+        *[
+            pltpu.with_memory_space_constraint(a, pltpu.HBM)
+            for a in (points, weights, neighbours)
+        ],
+    )
 
     order = (1, 3, 2)
     row = {0: target}
@@ -287,13 +322,13 @@
     sides = []
     for ring in (up, down):
         sides.append([lax.ppermute(source, "owner", ring)])
-    near = jnp.concatenate([column[1], column[3]], axis=0)
-    for ring, side in zip((up, down), sides):
-        side.append(lax.ppermute(near, "owner", ring))
+    for d in order[:2]:
+        for ring, side in zip((up, down), sides):
+            side.append(lax.ppermute(column[d], "owner", ring))
 
     room = SIDE * local * slots + 8
     me = jnp.stack([helper // SIDE, helper % SIDE]).astype(jnp.int32)
-    tgt, own, far, count = pl.pallas_call(
+    make_targets = pl.pallas_call(
         functools.partial(target_kernel, slots),
         out_shape=(
             jax.ShapeDtypeStruct((SIDE * local, dims + TILE, width), jnp.bfloat16),
@@ -312,7 +347,8 @@
         ],
         compiler_params=pltpu.CompilerParams(vmem_limit_bytes=8 << 20),
         name="targets",
-    )(me, *[row[d] for d in range(SIDE)])
+    )
+    tgt, own, far, count = make_targets(me, *[row[d] for d in range(SIDE)])
     opposite, tgt, own, far, count = lax.optimization_barrier(
         (column[2], tgt, own, far, count)
     )
@@ -330,7 +366,7 @@
     )
     places = []
     for s in range(2):
-        places += [(3 * s, 0), (3 * s + 1, 0), (3 * s + 2, 0), (3 * s + 1, rows)]
+        places += [(4 * s, 0), (4 * s + 1, 0), (4 * s + 3, 0), (4 * s + 2, 0)]
     parts = pair_sums(
         1, count, far, sides[0] + sides[1], tuple(places), tgt, vectors, total
     )

time: 76.6 us -> 64.6 us (0.84)
  waiting for transfers between devices: 20.8 us -> 12.2 us
  local copies, waits for them, and re-layouts: 4.74 us -> 0.65 us
  starting transfers between devices: 27.7 us -> 29.2 us
    ppermute x9, waiting for transfers between devices: 20.8 us -> 10.8 us  [moved(): return lax.ppermute(value, 'helper', pairs)]
    ppermute x9, starting transfers between devices: 21.7 us -> 15.9 us  [moved(): return lax.ppermute(value, 'helper', pairs)]
    ppermute x2, starting transfers between devices: 0.19 us -> 4.19 us  [potentials(): sides.append([lax.ppermute(source, 'owner', ring)])]
    ppermute x2 -> x4, starting transfers between devices: 2.96 us -> 5.91 us  [potentials(): side.append(lax.ppermute(column[d], 'owner', ring))]
    unnamed x7 -> x2, local copies, waits for them, and re-layouts: 3.23 us -> 0.65 us
    pallas_call x2, Pallas kernels: 18.1 us -> 15.9 us  [pair_sums(): pl.pallas_call(functools.partial(pair_kernel, which, places, last), out_s...]
    pallas_call x1, Pallas kernels: 0.1 us -> 1.61 us  [potentials(): pl.pallas_call(pack_kernel, out_shape=(jax.ShapeDtypeStruct((rows, width)...]
    ppermute x2 -> x4, waiting for transfers between devices: 0.01 us -> 1.37 us  [potentials(): side.append(lax.ppermute(column[d], 'owner', ring))]
  transfers between devices with their start and end apart: 15 -> 17, of which waited for: 4 -> 5; matrix products, arithmetic and copies ran while one was open for 2% -> 0% of each run, Pallas kernels for 17% -> 19%
where the time goes in v1:
time: 64.6 us; the launch traced here: 64.5 us
  starting transfers between devices  29.2 us (45%)
  Pallas kernels  21.5 us (33%)
  waiting for transfers between devices  12.2 us (19%)
  other arithmetic  0.76 us (1%)
  local copies, waits for them, and re-layouts  0.65 us (1%)
    ppermute x9, starting transfers between devices, moved(): return lax.ppermute(value, 'helper', pairs)  15.9 us
    pallas_call x2, Pallas kernels, pair_sums(): pl.pallas_call(functools.partial(pair_kernel, which, places, last), out_s...  15.9 us
    ppermute x9, waiting for transfers between devices, moved(): return lax.ppermute(value, 'helper', pairs)  10.8 us
    ppermute x4, starting transfers between devices, potentials(): side.append(lax.ppermute(column[d], 'owner', ring))  5.91 us
    ppermute x2, starting transfers between devices, potentials(): sides.append([lax.ppermute(source, 'owner', ring)])  4.19 us
    pallas_call x1, Pallas kernels, potentials(): tgt, own, far, count = make_targets(me, *[row[d] for d in range(SIDE)])  4.04 us
    ppermute x2, starting transfers between devices, potentials(): side.append(lax.ppermute(opposite, 'owner', ring))  3.16 us
    pallas_call x1, Pallas kernels, potentials(): pl.pallas_call(pack_kernel, out_shape=(jax.ShapeDtypeStruct((rows, width)...  1.61 us
  transfers between devices with their start and end apart: 17, of which 5 were waited for; matrix products, arithmetic and copies ran while one was open for 0% of the time, Pallas kernels for 19%

profile of v1, /device:TPU:16, one launch (start us, length us, event | category | flops | bytes accessed | tf_op | source)
XLA Modules:
  0.0 64.5 jit_solution(3534400800264017077)
XLA Ops:
  0.0 0.0 copy-start
  0.0 0.7 %copy-done = s32[4]{0:T(128)S(1)} copy-done((s32[4]{0:T(128)S(1)}, s32[4]{0:T(128)}, u32[]{:S(2)}) %copy-start) | copy-done | bytes 40
  0.7 1.6 %pack.1 = (bf16[336,512]{1,0:T(8,128)(2,1)S(1)}, bf16[272,512]{1,0:T(8,128)(2,1)S(1)}) custom-call(s32[1]{0:T(128)} %bitcast.first_ref, s32[4]{0:T(128)S(1)} %copy-done, bf16[4,64,512]{2,1,0:T(8,128)(2,1)} %points.1, bf16[4,16,512]{2,1,0:T(8,128)(2,1)} %weights.1, s32[4,48]{1,0:T(4,128)} %lists.1), custom_call_target="tpu_custom_call" | custom-call | tf_op jit(solution)/shard_map/pack/pallas_call | solution.py:291
  2.3 2.1 %collective-permute-start = (bf16[336,512]{1,0:T(8,128)(2,1)S(1)}, bf16[336,512]{1,0:T(8,128)(2,1)S(1)}, u32[]{:S(2)}, u32[]{:S(2)}) collective-permute-start(bf16[336,512]{1,0:T(8,128)(2,1)S(1)} %get-tuple-element.20.refs_0_), channel_id=1, source_target_pairs={{0,8},{1,9},{2,10},{3,11},{4,12},{5,13},{6,14},{7,15},{8,0},{9,1},... | collective-permute-start | bytes 1032200 | tf_op jit(solution)/shard_map/ppermute | solution.py:34
  4.4 0.0 collective-permute-start.1
  4.4 2.5 %collective-permute-start.2 = (bf16[272,512]{1,0:T(8,128)(2,1)S(1)}, bf16[272,512]{1,0:T(8,128)(2,1)S(1)}, u32[]{:S(2)}, u32[]{:S(2)}) collective-permute-start(bf16[272,512]{1,0:T(8,128)(2,1)S(1)} %get-tuple-element.21.refs_0_), channel_id=1, source_target_pairs={{0,2},{1,3},{2,0},{3,1},{4,6},{5,7},{6,4},{7,5},{8,10},{9,11},{10,... | collective-permute-start | bytes 835592 | tf_op jit(solution)/shard_map/ppermute | solution.py:34
  6.9 1.4 %collective-permute-start.3 = (bf16[272,512]{1,0:T(8,128)(2,1)S(1)}, bf16[272,512]{1,0:T(8,128)(2,1)S(1)}, u32[]{:S(2)}, u32[]{:S(2)}) collective-permute-start(bf16[272,512]{1,0:T(8,128)(2,1)S(1)} %get-tuple-element.21.refs_0_), channel_id=1, source_target_pairs={{0,3},{1,0},{2,1},{3,2},{4,7},{5,4},{6,5},{7,6},{8,11},{9,8},{10,9... | collective-permute-start | bytes 835592 | tf_op jit(solution)/shard_map/ppermute | solution.py:34
  8.4 2.2 %collective-permute-start.5 = (bf16[336,512]{1,0:T(8,128)(2,1)S(1)}, bf16[336,512]{1,0:T(8,128)(2,1)S(1)}, u32[]{:S(2)}, u32[]{:S(2)}) collective-permute-start(bf16[336,512]{1,0:T(8,128)(2,1)S(1)} %get-tuple-element.20.refs_0_), channel_id=1, source_target_pairs={{0,4},{1,5},{2,6},{3,7},{4,8},{5,9},{6,10},{7,11},{8,12},{9,13},{1... | collective-permute-start | bytes 1032200 | tf_op jit(solution)/shard_map/ppermute | solution.py:34
  10.5 0.1 pad_add_fusion.me_ref
  10.6 2.0 %collective-permute-done.1.refs_1_ = bf16[272,512]{1,0:T(8,128)(2,1)S(1)} collective-permute-done((bf16[272,512]{1,0:T(8,128)(2,1)S(1)}, bf16[272,512]{1,0:T(8,128)(2,1)S(1)}, u32[]{:S(2)}, u32[]{:S(2)}) %collective-permute-start.1) | collective-permute-done | bytes 278560 | tf_op jit(solution)/shard_map/ppermute | solution.py:34
  12.7 2.2 %collective-permute-start.7 = (bf16[336,512]{1,0:T(8,128)(2,1)S(1)}, bf16[336,512]{1,0:T(8,128)(2,1)S(1)}, u32[]{:S(2)}, u32[]{:S(2)}) collective-permute-start(bf16[336,512]{1,0:T(8,128)(2,1)S(1)} %get-tuple-element.20.refs_0_), channel_id=1, source_target_pairs={{0,12},{1,13},{2,14},{3,15},{4,0},{5,1},{6,2},{7,3},{8,4},{9,5},{1... | collective-permute-start | bytes 1032200 | tf_op jit(solution)/shard_map/ppermute | solution.py:34
  14.9 4.2 %collective-permute-done.2.refs_2_ = bf16[272,512]{1,0:T(8,128)(2,1)S(1)} collective-permute-done((bf16[272,512]{1,0:T(8,128)(2,1)S(1)}, bf16[272,512]{1,0:T(8,128)(2,1)S(1)}, u32[]{:S(2)}, u32[]{:S(2)}) %collective-permute-start.2) | collective-permute-done | bytes 278560 | tf_op jit(solution)/shard_map/ppermute | solution.py:34
  19.0 4.2 %collective-permute-start.10 = (bf16[336,512]{1,0:T(8,128)(2,1)S(1)}, bf16[336,512]{1,0:T(8,128)(2,1)S(1)}, u32[]{:S(2)}, u32[]{:S(2)}) collective-permute-start(bf16[336,512]{1,0:T(8,128)(2,1)S(1)} %get-tuple-element.20.refs_0_), channel_id=1, source_target_pairs={{16,0},{32,16},{48,32},{64,48},{80,64},{96,80},{112,96},{128,112},... | collective-permute-start | bytes 1032200 | tf_op jit(solution)/shard_map/ppermute | solution.py:324
  23.2 0.0 collective-permute-done.3.refs_3_
  23.2 0.0 collective-permute-start.4
  23.2 4.0 %targets.1 = (bf16[16,80,512]{2,1,0:T(8,128)(2,1)S(1)}, s32[776]{0:T(1024)S(1)}, s32[776]{0:T(1024)S(1)}, s32[2]{0:T(128)S(1)}) custom-call(s32[2]{0:T(128)S(1)} %pad_add_fusion.me_ref, bf16[272,512]{1,0:T(8,128)(2,1)S(1)} %get-tuple-element.21.refs_0_, bf16[272,512]{1,0:T(8,128)(2,1)S(1)} %collective-permute-done.1.refs_1_, ...), custom_call_target="tpu_custom_call" | custom-call | tf_op jit(solution)/shard_map/targets/pallas_call | solution.py:351
  27.3 0.0 collective-permute-done.refs_2_
  27.3 3.2 %collective-permute-start.13 = (bf16[336,512]{1,0:T(8,128)(2,1)S(1)}, bf16[336,512]{1,0:T(8,128)(2,1)S(1)}, u32[]{:S(2)}, u32[]{:S(2)}) collective-permute-start(bf16[336,512]{1,0:T(8,128)(2,1)S(1)} %collective-permute-done.refs_2_), channel_id=1, source_target_pairs={{16,0},{32,16},{48,32},{64,48},{80,64},{96,80},{112,96},{128,112},... | collective-permute-start | bytes 1032200 | tf_op jit(solution)/shard_map/ppermute | solution.py:356
  30.4 0.0 collective-permute-done.5.refs_1_
  30.4 0.0 collective-permute-start.9
  30.4 0.0 collective-permute-done.7.refs_3_
  30.4 3.0 %collective-permute-start.11 = (bf16[336,512]{1,0:T(8,128)(2,1)S(1)}, bf16[336,512]{1,0:T(8,128)(2,1)S(1)}, u32[]{:S(2)}, u32[]{:S(2)}) collective-permute-start(bf16[336,512]{1,0:T(8,128)(2,1)S(1)} %collective-permute-done.5.refs_1_), channel_id=1, source_target_pairs={{16,0},{32,16},{48,32},{64,48},{80,64},{96,80},{112,96},{128,112},... | collective-permute-start | bytes 1032200 | tf_op jit(solution)/shard_map/ppermute | solution.py:327
  33.4 0.0 collective-permute-done.10.refs_4_
  33.4 0.0 collective-permute-start.6
  33.4 0.0 collective-permute-done.4.refs_0_
  33.4 3.0 %collective-permute-start.12 = (bf16[336,512]{1,0:T(8,128)(2,1)S(1)}, bf16[336,512]{1,0:T(8,128)(2,1)S(1)}, u32[]{:S(2)}, u32[]{:S(2)}) collective-permute-start(bf16[336,512]{1,0:T(8,128)(2,1)S(1)} %collective-permute-done.7.refs_3_), channel_id=1, source_target_pairs={{16,0},{32,16},{48,32},{64,48},{80,64},{96,80},{112,96},{128,112},... | collective-permute-start | bytes 1032200 | tf_op jit(solution)/shard_map/ppermute | solution.py:327
  36.4 0.0 collective-permute-done.13.refs_7_
  36.4 0.0 collective-permute-start.8
  36.4 7.9 %pairs_own.1.refs_9_ = f32[16,16,512]{2,1,0:T(8,128)S(1)} custom-call(s32[2]{0:T(128)S(1)} %get-tuple-element.26.count_ref, s32[776]{0:T(1024)S(1)} %get-tuple-element.30.keys_ref, bf16[336,512]{1,0:T(8,128)(2,1)S(1)} %get-tuple-element.20.refs_0_, bf16[336,512]{1,0:T(8,128)(2,1)S(1)} %collective-permute-done.5.refs_1_, ...), custom_call_target="tpu_custom_call" | custom-call | flops 1677721600 | bytes 1376256 | tf_op jit(solution)/shard_map/pairs_own/pallas_call | solution.py:256
  44.3 0.0 collective-permute-done.9.refs_3_
  44.3 0.0 collective-permute-done.11.refs_5_
  44.3 0.0 collective-permute-done.12.refs_6_
  44.3 0.0 collective-permute-done.6.refs_1_
  44.3 1.4 %collective-permute-done.8.refs_2_ = bf16[336,512]{1,0:T(8,128)(2,1)S(1)} collective-permute-done((bf16[336,512]{1,0:T(8,128)(2,1)S(1)}, bf16[336,512]{1,0:T(8,128)(2,1)S(1)}, u32[]{:S(2)}, u32[]{:S(2)}) %collective-permute-start.8) | collective-permute-done | bytes 344096 | tf_op jit(solution)/shard_map/ppermute | solution.py:327
  45.7 8.0 %pairs_far.1 = (f32[4,16,512]{2,1,0:T(8,128)S(1)}, bf16[4,16,512]{2,1,0:T(8,128)(2,1)S(1)}, bf16[4,16,512]{2,1,0:T(8,128)(2,1)S(1)}, bf16[4,16,512]{2,1,0:T(8,128)(2,1)S(1)}) custom-call(s32[2]{0:T(128)S(1)} %get-tuple-element.26.count_ref, s32[776]{0:T(1024)S(1)} %get-tuple-element.27.keys_ref, bf16[336,512]{1,0:T(8,128)(2,1)S(1)} %collective-permute-done.4.refs_0_, ...), custom_call_target="tpu_custom_call" | custom-call | flops 1677721600 | bytes 2752512 | tf_op jit(solution)/shard_map/pairs_far/pallas_call | solution.py:256
  53.7 3.9 %collective-permute-start.14 = (bf16[4,16,512]{2,1,0:T(8,128)(2,1)S(1)}, bf16[4,16,512]{2,1,0:T(8,128)(2,1)S(1)}, u32[]{:S(2)}, u32[]{:S(2)}) collective-permute-start(bf16[4,16,512]{2,1,0:T(8,128)(2,1)S(1)} %get-tuple-element.32), channel_id=1, source_target_pairs={{0,3},{1,0},{2,1},{3,2},{4,7},{5,4},{6,5},{7,6},{8,11},{9,8},{10,9... | collective-permute-start | bytes 196616 | tf_op jit(solution)/shard_map/ppermute | solution.py:34
  57.6 0.0 collective-permute-start.15
  57.6 1.6 %collective-permute-start.16 = (bf16[4,16,512]{2,1,0:T(8,128)(2,1)S(1)}, bf16[4,16,512]{2,1,0:T(8,128)(2,1)S(1)}, u32[]{:S(2)}, u32[]{:S(2)}) collective-permute-start(bf16[4,16,512]{2,1,0:T(8,128)(2,1)S(1)} %get-tuple-element.34), channel_id=1, source_target_pairs={{0,2},{1,3},{2,0},{3,1},{4,6},{5,7},{6,4},{7,5},{8,10},{9,11},{10,... | collective-permute-start | bytes 196616 | tf_op jit(solution)/shard_map/ppermute | solution.py:34
  59.1 0.4 collective-permute-done.14
  59.5 4.3 %collective-permute-done.15 = bf16[4,16,512]{2,1,0:T(8,128)(2,1)S(1)} collective-permute-done((bf16[4,16,512]{2,1,0:T(8,128)(2,1)S(1)}, bf16[4,16,512]{2,1,0:T(8,128)(2,1)S(1)}, u32[]{:S(2)}, u32[]{:S(2)}) %collective-permute-start.15) | collective-permute-done | bytes 65568 | tf_op jit(solution)/shard_map/ppermute | solution.py:34
  63.8 0.0 collective-permute-done.16
  63.8 0.7 %convert_add_fusion = f32[4,16,512]{2,1,0:T(8,128)} fusion(bf16[4,16,512]{2,1,0:T(8,128)(2,1)S(1)} %collective-permute-done.16, bf16[4,16,512]{2,1,0:T(8,128)(2,1)S(1)} %collective-permute-done.15, f32[4,16,512]{2,1,0:T(8,128)S(1)} %get-tuple-element.31, bf16[4,16,512]{2,1,0:T(8,128)(2,1)S(1)} %collective-permute-done.14), kind=kLoop, calls=%fused_computation | loop fusion | flops 196608 | bytes 458752 | tf_op jit(solution)/shard_map/add | solution.py:375
Async XLA Ops:
  0.0 0.7 %copy-start = (s32[4]{0:T(128)S(1)}, s32[4]{0:T(128)}, u32[]{:S(2)}) copy-start(s32[4]{0:T(128)} %counts.1) | copy-start | bytes 52
  2.3 25.0 %collective-permute-start = (bf16[336,512]{1,0:T(8,128)(2,1)S(1)}, bf16[336,512]{1,0:T(8,128)(2,1)S(1)}, u32[]{:S(2)}, u32[]{:S(2)}) collective-permute-start(bf16[336,512]{1,0:T(8,128)(2,1)S(1)} %get-tuple-element.20.refs_0_), channel_id=1, source_target_pairs={{0,8},{1,9},{2,10},{3,11},{4,12},{5,13},{6,14},{7,15},{8,0},{9,1},... | collective-permute-start | bytes 1032200 | tf_op jit(solution)/shard_map/ppermute | solution.py:34
  4.4 8.3 %collective-permute-start.1 = (bf16[272,512]{1,0:T(8,128)(2,1)S(1)}, bf16[272,512]{1,0:T(8,128)(2,1)S(1)}, u32[]{:S(2)}, u32[]{:S(2)}) collective-permute-start(bf16[272,512]{1,0:T(8,128)(2,1)S(1)} %get-tuple-element.21.refs_0_), channel_id=1, source_target_pairs={{0,1},{1,2},{2,3},{3,0},{4,5},{5,6},{6,7},{7,4},{8,9},{9,10},{10,1... | collective-permute-start | bytes 835592 | tf_op jit(solution)/shard_map/ppermute | solution.py:34
  4.4 14.6 %collective-permute-start.2 = (bf16[272,512]{1,0:T(8,128)(2,1)S(1)}, bf16[272,512]{1,0:T(8,128)(2,1)S(1)}, u32[]{:S(2)}, u32[]{:S(2)}) collective-permute-start(bf16[272,512]{1,0:T(8,128)(2,1)S(1)} %get-tuple-element.21.refs_0_), channel_id=1, source_target_pairs={{0,2},{1,3},{2,0},{3,1},{4,6},{5,7},{6,4},{7,5},{8,10},{9,11},{10,... | collective-permute-start | bytes 835592 | tf_op jit(solution)/shard_map/ppermute | solution.py:34
  6.9 16.3 %collective-permute-start.3 = (bf16[272,512]{1,0:T(8,128)(2,1)S(1)}, bf16[272,512]{1,0:T(8,128)(2,1)S(1)}, u32[]{:S(2)}, u32[]{:S(2)}) collective-permute-start(bf16[272,512]{1,0:T(8,128)(2,1)S(1)} %get-tuple-element.21.refs_0_), channel_id=1, source_target_pairs={{0,3},{1,0},{2,1},{3,2},{4,7},{5,4},{6,5},{7,6},{8,11},{9,8},{10,9... | collective-permute-start | bytes 835592 | tf_op jit(solution)/shard_map/ppermute | solution.py:34
  8.4 22.1 %collective-permute-start.5 = (bf16[336,512]{1,0:T(8,128)(2,1)S(1)}, bf16[336,512]{1,0:T(8,128)(2,1)S(1)}, u32[]{:S(2)}, u32[]{:S(2)}) collective-permute-start(bf16[336,512]{1,0:T(8,128)(2,1)S(1)} %get-tuple-element.20.refs_0_), channel_id=1, source_target_pairs={{0,4},{1,5},{2,6},{3,7},{4,8},{5,9},{6,10},{7,11},{8,12},{9,13},{1... | collective-permute-start | bytes 1032200 | tf_op jit(solution)/shard_map/ppermute | solution.py:34
  12.7 17.8 %collective-permute-start.7 = (bf16[336,512]{1,0:T(8,128)(2,1)S(1)}, bf16[336,512]{1,0:T(8,128)(2,1)S(1)}, u32[]{:S(2)}, u32[]{:S(2)}) collective-permute-start(bf16[336,512]{1,0:T(8,128)(2,1)S(1)} %get-tuple-element.20.refs_0_), channel_id=1, source_target_pairs={{0,12},{1,13},{2,14},{3,15},{4,0},{5,1},{6,2},{7,3},{8,4},{9,5},{1... | collective-permute-start | bytes 1032200 | tf_op jit(solution)/shard_map/ppermute | solution.py:34
  19.0 14.4 %collective-permute-start.10 = (bf16[336,512]{1,0:T(8,128)(2,1)S(1)}, bf16[336,512]{1,0:T(8,128)(2,1)S(1)}, u32[]{:S(2)}, u32[]{:S(2)}) collective-permute-start(bf16[336,512]{1,0:T(8,128)(2,1)S(1)} %get-tuple-element.20.refs_0_), channel_id=1, source_target_pairs={{16,0},{32,16},{48,32},{64,48},{80,64},{96,80},{112,96},{128,112},... | collective-permute-start | bytes 1032200 | tf_op jit(solution)/shard_map/ppermute | solution.py:324
  23.2 10.2 %collective-permute-start.4 = (bf16[336,512]{1,0:T(8,128)(2,1)S(1)}, bf16[336,512]{1,0:T(8,128)(2,1)S(1)}, u32[]{:S(2)}, u32[]{:S(2)}) collective-permute-start(bf16[336,512]{1,0:T(8,128)(2,1)S(1)} %get-tuple-element.20.refs_0_), channel_id=1, source_target_pairs={{0,16},{16,32},{32,48},{48,64},{64,80},{80,96},{96,112},{112,128},... | collective-permute-start | bytes 1032200 | tf_op jit(solution)/shard_map/ppermute | solution.py:324
  27.3 9.1 %collective-permute-start.13 = (bf16[336,512]{1,0:T(8,128)(2,1)S(1)}, bf16[336,512]{1,0:T(8,128)(2,1)S(1)}, u32[]{:S(2)}, u32[]{:S(2)}) collective-permute-start(bf16[336,512]{1,0:T(8,128)(2,1)S(1)} %collective-permute-done.refs_2_), channel_id=1, source_target_pairs={{16,0},{32,16},{48,32},{64,48},{80,64},{96,80},{112,96},{128,112},... | collective-permute-start | bytes 1032200 | tf_op jit(solution)/shard_map/ppermute | solution.py:356
  30.4 13.9 %collective-permute-start.9 = (bf16[336,512]{1,0:T(8,128)(2,1)S(1)}, bf16[336,512]{1,0:T(8,128)(2,1)S(1)}, u32[]{:S(2)}, u32[]{:S(2)}) collective-permute-start(bf16[336,512]{1,0:T(8,128)(2,1)S(1)} %collective-permute-done.refs_2_), channel_id=1, source_target_pairs={{0,16},{16,32},{32,48},{48,64},{64,80},{80,96},{96,112},{112,128},... | collective-permute-start | bytes 1032200 | tf_op jit(solution)/shard_map/ppermute | solution.py:356
  30.4 13.9 %collective-permute-start.11 = (bf16[336,512]{1,0:T(8,128)(2,1)S(1)}, bf16[336,512]{1,0:T(8,128)(2,1)S(1)}, u32[]{:S(2)}, u32[]{:S(2)}) collective-permute-start(bf16[336,512]{1,0:T(8,128)(2,1)S(1)} %collective-permute-done.5.refs_1_), channel_id=1, source_target_pairs={{16,0},{32,16},{48,32},{64,48},{80,64},{96,80},{112,96},{128,112},... | collective-permute-start | bytes 1032200 | tf_op jit(solution)/shard_map/ppermute | solution.py:327
  33.4 10.9 %collective-permute-start.6 = (bf16[336,512]{1,0:T(8,128)(2,1)S(1)}, bf16[336,512]{1,0:T(8,128)(2,1)S(1)}, u32[]{:S(2)}, u32[]{:S(2)}) collective-permute-start(bf16[336,512]{1,0:T(8,128)(2,1)S(1)} %collective-permute-done.5.refs_1_), channel_id=1, source_target_pairs={{0,16},{16,32},{32,48},{48,64},{64,80},{80,96},{96,112},{112,128},... | collective-permute-start | bytes 1032200 | tf_op jit(solution)/shard_map/ppermute | solution.py:327
  33.4 10.9 %collective-permute-start.12 = (bf16[336,512]{1,0:T(8,128)(2,1)S(1)}, bf16[336,512]{1,0:T(8,128)(2,1)S(1)}, u32[]{:S(2)}, u32[]{:S(2)}) collective-permute-start(bf16[336,512]{1,0:T(8,128)(2,1)S(1)} %collective-permute-done.7.refs_3_), channel_id=1, source_target_pairs={{16,0},{32,16},{48,32},{64,48},{80,64},{96,80},{112,96},{128,112},... | collective-permute-start | bytes 1032200 | tf_op jit(solution)/shard_map/ppermute | solution.py:327
  36.4 9.3 %collective-permute-start.8 = (bf16[336,512]{1,0:T(8,128)(2,1)S(1)}, bf16[336,512]{1,0:T(8,128)(2,1)S(1)}, u32[]{:S(2)}, u32[]{:S(2)}) collective-permute-start(bf16[336,512]{1,0:T(8,128)(2,1)S(1)} %collective-permute-done.7.refs_3_), channel_id=1, source_target_pairs={{0,16},{16,32},{32,48},{48,64},{64,80},{80,96},{96,112},{112,128},... | collective-permute-start | bytes 1032200 | tf_op jit(solution)/shard_map/ppermute | solution.py:327
  53.7 5.8 %collective-permute-start.14 = (bf16[4,16,512]{2,1,0:T(8,128)(2,1)S(1)}, bf16[4,16,512]{2,1,0:T(8,128)(2,1)S(1)}, u32[]{:S(2)}, u32[]{:S(2)}) collective-permute-start(bf16[4,16,512]{2,1,0:T(8,128)(2,1)S(1)} %get-tuple-element.32), channel_id=1, source_target_pairs={{0,3},{1,0},{2,1},{3,2},{4,7},{5,4},{6,5},{7,6},{8,11},{9,8},{10,9... | collective-permute-start | bytes 196616 | tf_op jit(solution)/shard_map/ppermute | solution.py:34
  57.6 6.2 %collective-permute-start.15 = (bf16[4,16,512]{2,1,0:T(8,128)(2,1)S(1)}, bf16[4,16,512]{2,1,0:T(8,128)(2,1)S(1)}, u32[]{:S(2)}, u32[]{:S(2)}) collective-permute-start(bf16[4,16,512]{2,1,0:T(8,128)(2,1)S(1)} %get-tuple-element.33), channel_id=1, source_target_pairs={{0,1},{1,2},{2,3},{3,0},{4,5},{5,6},{6,7},{7,4},{8,9},{9,10},{10,1... | collective-permute-start | bytes 196616 | tf_op jit(solution)/shard_map/ppermute | solution.py:34
  57.6 6.2 %collective-permute-start.16 = (bf16[4,16,512]{2,1,0:T(8,128)(2,1)S(1)}, bf16[4,16,512]{2,1,0:T(8,128)(2,1)S(1)}, u32[]{:S(2)}, u32[]{:S(2)}) collective-permute-start(bf16[4,16,512]{2,1,0:T(8,128)(2,1)S(1)} %get-tuple-element.34), channel_id=1, source_target_pairs={{0,2},{1,3},{2,0},{3,1},{4,6},{5,7},{6,4},{7,5},{8,10},{9,11},{10,... | collective-permute-start | bytes 196616 | tf_op jit(solution)/shard_map/ppermute | solution.py:34

commit v2 on v1

--- a/solution.py
+++ b/solution.py
@@ -46,7 +46,9 @@
     )
 
 
-def pack_kernel(first_ref, counts, points, weights, lists, s_out, t_out, tile, near, sems):
+def pack_kernel(
+    first_ref, counts_hbm, points, weights, lists, s_out, t_out, tile, near, counts, sems
+):
     dims = points.shape[1]
     vectors = weights.shape[1]
     slots = lists.shape[1]
@@ -60,6 +62,7 @@
         here = s_out.at[at : at + vectors]
         copies.append(pltpu.make_async_copy(weights.at[i], here, sems.at[LOCAL + i]))
     copies.append(pltpu.make_async_copy(lists, near, sems.at[2 * LOCAL]))
+    copies.append(pltpu.make_async_copy(counts_hbm, counts, sems.at[2 * LOCAL + 1]))
     for copy in copies:
         copy.start()
     for i in range(LOCAL):
@@ -79,6 +82,7 @@
     s_out[top : top + TILE] = tile[...].astype(jnp.bfloat16)
     tile[LISTS:] = jnp.zeros((LOCAL, tile.shape[1]), jnp.float32)
     copies[2 * LOCAL].wait()
+    copies[2 * LOCAL + 1].wait()
     slot = lax.broadcasted_iota(jnp.int32, (1, slots), 1)
     for i in range(LOCAL):
         size = counts[i]
@@ -92,9 +96,15 @@
         copy.wait()
 
 
+def join_kernel(a, b, c, out):
+    rows = a.shape[0]
+    for i, ref in enumerate((a, b, c)):
+        out[i * rows : (i + 1) * rows] = ref[...]
+
+
 def target_kernel(slots, me_ref, *refs):
     blocks, refs = refs[:SIDE], refs[SIDE:]
-    tgt, own_ref, far_ref, count_ref, tile, norm, keys, keys_s, sem = refs
+    tgt, own_ref, far_ref, tile, norm, keys, keys_s, sem = refs
     dims = tgt.shape[1] - TILE
     top = LOCAL * dims
     norm[...] = jnp.full(norm.shape, -0.5, jnp.float32)
@@ -129,8 +139,8 @@
             for u in range(AT_ONCE):
                 key = keys_s[t, AT_ONCE * q + u]
                 kind = key >> 24
-                own_ref[own] = key & 0xFFFFFF
-                far_ref[far] = key & 0xFFFFFF
+                own_ref[own + 1] = key & 0xFFFFFF
+                far_ref[far + 1] = key & 0xFFFFFF
                 own = own + jnp.where(kind == 0, 1, 0)
                 far = far + jnp.where(kind == 1, 1, 0)
             return own, far
@@ -140,14 +150,14 @@
 
     targets = SIDE * LOCAL
     own, far = lax.fori_loop(0, targets, per_target, (jnp.int32(0), jnp.int32(0)))
-    count_ref[0] = own
-    count_ref[1] = far
-    for u in range(UNROLL + 2):
+    own_ref[0] = own
+    far_ref[0] = far
+    for u in range(1, TAIL + 3):
         own_ref[own + u] = jnp.int32(targets << 16)
         far_ref[far + u] = jnp.int32(targets << 16)
 
 
-def pair_kernel(which, places, last, count_ref, keys_ref, *refs):
+def pair_kernel(places, last, keys_ref, *refs):
     n_refs = 1 + max(p[0] for p in places)
     source_refs, refs = refs[:n_refs], refs[n_refs:]
     tgt, refs = refs[0], refs[1:]
@@ -181,7 +191,7 @@
     k1[...] = jnp.zeros_like(k1)
 
     def picked(p):
-        key = keys_ref[p]
+        key = keys_ref[p + 1]
         return key & 255, (key >> 8) & 255, key >> 16
 
     def ahead(p, buffer):
@@ -224,7 +234,7 @@
         turn(whole + TAIL * h, TAIL)
         return carry
 
-    steps = count_ref[which] + 1
+    steps = keys_ref[0] + 1
     turns = steps // UNROLL
     whole = turns * UNROLL
     lax.fori_loop(0, turns, body, 0)
@@ -241,7 +251,7 @@
 HBM = pl.BlockSpec(memory_space=pltpu.HBM)
 
 
-def pair_sums(which, count, keys, operands, places, tgt, vectors, start=None):
+def pair_sums(keys, operands, places, tgt, vectors, start=None):
     targets, deep, width = tgt.shape
     dims = deep - TILE
     rows = LOCAL * (dims + vectors) + TILE
@@ -254,9 +264,9 @@
         out = [jax.ShapeDtypeStruct((targets, vectors, width), jnp.float32)]
     pairs = 40
     return pl.pallas_call(
-        functools.partial(pair_kernel, which, places, last),
+        functools.partial(pair_kernel, places, last),
         out_shape=out,
-        in_specs=[SMEM, SMEM] + [VMEM] * (len(operands) + 1 + last),
+        in_specs=[SMEM] + [VMEM] * (len(operands) + 1 + last),
         out_specs=[VMEM] * len(out),
         scratch_shapes=[
             pltpu.VMEM((len(places) * LOCAL, deep, width), jnp.bfloat16),
@@ -267,14 +277,14 @@
             pltpu.VMEM((PRE, width), jnp.float32),
             pltpu.VMEM((PRE, width), jnp.float32),
         ],
-        compiler_params=pltpu.CompilerParams(vmem_limit_bytes=28 << 20),
+        compiler_params=pltpu.CompilerParams(vmem_limit_bytes=14 << 20),
         cost_estimate=pl.CostEstimate(
             flops=2 * pairs * width * width * deep,
             transcendentals=pairs * width * width,
             bytes_accessed=len(places) * rows * width * 2,
         ),
         name="pairs_far" if last else "pairs_own",
-    )(count, keys, *operands, tgt, *((start,) if last else ()))
+    )(keys, *operands, tgt, *((start,) if last else ()))
 
 
 def potentials(points, weights, neighbours, counts):
@@ -294,21 +304,21 @@
             jax.ShapeDtypeStruct((rows, width), jnp.bfloat16),
             jax.ShapeDtypeStruct((local * dims + TILE, width), jnp.bfloat16),
         ),
-        in_specs=[SMEM, SMEM] + [HBM] * 3,
+        in_specs=[SMEM] + [HBM] * 4,
         out_specs=(VMEM, VMEM),
         scratch_shapes=[
             pltpu.VMEM((TILE, width), jnp.float32),
             pltpu.VMEM((local, slots), jnp.int32),
-            pltpu.SemaphoreType.DMA((2 * local + 1,)),
+            pltpu.SMEM((local,), jnp.int32),
+            pltpu.SemaphoreType.DMA((2 * local + 2,)),
         ],
         compiler_params=pltpu.CompilerParams(vmem_limit_bytes=4 << 20),
         name="pack",
     )(
         first_leaf[None],
-        counts,
         *[
             pltpu.with_memory_space_constraint(a, pltpu.HBM)
-            for a in (points, weights, neighbours)
+            for a in (counts, points, weights, neighbours)
         ],
     )
 
@@ -319,12 +329,18 @@
     column = {0: source}
     for d in order:
         column[d] = moved(source, d, 0)
+    join = pl.pallas_call(
+        join_kernel,
+        out_shape=jax.ShapeDtypeStruct((3 * rows, width), jnp.bfloat16),
+        in_specs=[VMEM] * 3,
+        out_specs=VMEM,
+        compiler_params=pltpu.CompilerParams(vmem_limit_bytes=4 << 20),
+        name="join",
+    )
+    near = join(source, column[1], column[3])
     sides = []
     for ring in (up, down):
-        sides.append([lax.ppermute(source, "owner", ring)])
-    for d in order[:2]:
-        for ring, side in zip((up, down), sides):
-            side.append(lax.ppermute(column[d], "owner", ring))
+        sides.append([lax.ppermute(near, "owner", ring)])
 
     room = SIDE * local * slots + 8
     me = jnp.stack([helper // SIDE, helper % SIDE]).astype(jnp.int32)
@@ -334,10 +350,9 @@
             jax.ShapeDtypeStruct((SIDE * local, dims + TILE, width), jnp.bfloat16),
             jax.ShapeDtypeStruct((room,), jnp.int32),
             jax.ShapeDtypeStruct((room,), jnp.int32),
-            jax.ShapeDtypeStruct((2,), jnp.int32),
         ),
         in_specs=[SMEM] + [VMEM] * SIDE,
-        out_specs=(VMEM, SMEM, SMEM, SMEM),
+        out_specs=(VMEM, SMEM, SMEM),
         scratch_shapes=[
             pltpu.VMEM((TILE, width), jnp.float32),
             pltpu.VMEM((TILE, width), jnp.float32),
@@ -348,16 +363,12 @@
         compiler_params=pltpu.CompilerParams(vmem_limit_bytes=8 << 20),
         name="targets",
     )
-    tgt, own, far, count = make_targets(me, *[row[d] for d in range(SIDE)])
-    opposite, tgt, own, far, count = lax.optimization_barrier(
-        (column[2], tgt, own, far, count)
-    )
+    tgt, own, far = make_targets(me, *[row[d] for d in range(SIDE)])
+    opposite, tgt, own, far = lax.optimization_barrier((column[2], tgt, own, far))
     for ring, side in zip((up, down), sides):
         side.append(lax.ppermute(opposite, "owner", ring))
 
     (total,) = pair_sums(
-        0,
-        count,
         own,
         [source, column[1], opposite, column[3]],
         tuple((d, 0) for d in range(SIDE)),
@@ -366,10 +377,8 @@
     )
     places = []
     for s in range(2):
-        places += [(4 * s, 0), (4 * s + 1, 0), (4 * s + 3, 0), (4 * s + 2, 0)]
-    parts = pair_sums(
-        1, count, far, sides[0] + sides[1], tuple(places), tgt, vectors, total
-    )
+        places += [(2 * s, 0), (2 * s, rows), (2 * s + 1, 0), (2 * s, 2 * rows)]
+    parts = pair_sums(far, sides[0] + sides[1], tuple(places), tgt, vectors, total)
     result = parts[0]
     for d in order:
         result = result + moved(parts[d], -d, 1).astype(jnp.float32)

time: 64.6 us -> 77.5 us (1.20)
  waiting for transfers between devices: 12.2 us -> 26 us
  starting transfers between devices: 29.2 us -> 28.2 us
  Pallas kernels: 21.5 us -> 22.3 us
    ppermute x9, waiting for transfers between devices: 10.8 us -> 25.9 us  [moved(): return lax.ppermute(value, 'helper', pairs)]
    ppermute x6 -> x2, starting transfers between devices: 10.1 us -> 4.29 us  [potentials(): sides.append([lax.ppermute(near, 'owner', ring)])]
    ppermute x2, starting transfers between devices: 3.16 us -> 6.55 us  [potentials(): side.append(lax.ppermute(opposite, 'owner', ring))]
    ppermute x9, starting transfers between devices: 15.9 us -> 17.4 us  [moved(): return lax.ppermute(value, 'helper', pairs)]
    ppermute x6 -> x2, waiting for transfers between devices: 1.37 us -> 0.01 us  [potentials(): sides.append([lax.ppermute(near, 'owner', ring)])]
    pallas_call x3 -> x4, Pallas kernels: 19.9 us -> 21.2 us  [the longest x2 17 us: pair_sums(): pl.pallas_call(functools.partial(pair_kernel, places, last), out_shape=ou...]
  transfers between devices with their start and end apart: 17 -> 13, of which waited for: 5 -> 7; matrix products, arithmetic and copies ran while one was open for 0% -> 0% of each run, Pallas kernels for 19% -> 16%
where the time goes in v2:
time: 77.5 us; the launch traced here: 77.3 us
  starting transfers between devices  28.2 us (36%)
  waiting for transfers between devices  26 us (34%)
  Pallas kernels  22.3 us (29%)
    ppermute x9, waiting for transfers between devices, moved(): return lax.ppermute(value, 'helper', pairs)  25.9 us
    ppermute x9, starting transfers between devices, moved(): return lax.ppermute(value, 'helper', pairs)  17.4 us
    pallas_call x2, Pallas kernels, pair_sums(): pl.pallas_call(functools.partial(pair_kernel, places, last), out_shape=ou...  17 us
    ppermute x2, starting transfers between devices, potentials(): side.append(lax.ppermute(opposite, 'owner', ring))  6.55 us
    ppermute x2, starting transfers between devices, potentials(): sides.append([lax.ppermute(near, 'owner', ring)])  4.29 us
    pallas_call x1, Pallas kernels, potentials(): tgt, own, far = make_targets(me, *[row[d] for d in range(SIDE)])  4.13 us
  transfers between devices with their start and end apart: 13, of which 7 were waited for; matrix products, arithmetic and copies ran while one was open for 0% of the time, Pallas kernels for 16%

profile of v2, /device:TPU:16, one launch (start us, length us, event | category | flops | bytes accessed | tf_op | source)
XLA Modules:
  0.0 77.3 jit_solution(18098252047053512656)
XLA Ops:
  0.0 1.1 %pack.1 = (bf16[336,512]{1,0:T(8,128)(2,1)S(1)}, bf16[272,512]{1,0:T(8,128)(2,1)S(1)}) custom-call(s32[1]{0:T(128)} %bitcast.first_ref, s32[4]{0:T(128)} %counts_hbm.1, bf16[4,64,512]{2,1,0:T(8,128)(2,1)} %points.1, bf16[4,16,512]{2,1,0:T(8,128)(2,1)} %weights.1, s32[4,48]{1,0:T(4,128)} %lists.1), custom_call_target="tpu_custom_call" | custom-call | tf_op jit(solution)/shard_map/pack/pallas_call | solution.py:301
  1.1 0.5 collective-permute-start.5
  1.6 1.6 %collective-permute-start.4 = (bf16[336,512]{1,0:T(8,128)(2,1)S(1)}, bf16[336,512]{1,0:T(8,128)(2,1)S(1)}, u32[]{:S(2)}, u32[]{:S(2)}) collective-permute-start(bf16[336,512]{1,0:T(8,128)(2,1)S(1)} %get-tuple-element.18.a.refs_0_), channel_id=1, source_target_pairs={{0,4},{1,5},{2,6},{3,7},{4,8},{5,9},{6,10},{7,11},{8,12},{9,13},{1... | collective-permute-start | bytes 1032200 | tf_op jit(solution)/shard_map/ppermute | solution.py:34
  3.2 7.8 %collective-permute-done.5.c.refs_3_ = bf16[336,512]{1,0:T(8,128)(2,1)S(1)} collective-permute-done((bf16[336,512]{1,0:T(8,128)(2,1)S(1)}, bf16[336,512]{1,0:T(8,128)(2,1)S(1)}, u32[]{:S(2)}, u32[]{:S(2)}) %collective-permute-start.5) | collective-permute-done | bytes 344096 | tf_op jit(solution)/shard_map/ppermute | solution.py:34
  11.0 0.2 collective-permute-done.4.b.refs_1_
  11.1 0.1 join.1
  11.2 4.3 %collective-permute-start.8 = (bf16[1008,512]{1,0:T(8,128)(2,1)S(1)}, bf16[1008,512]{1,0:T(8,128)(2,1)}, u32[]{:S(2)}, u32[]{:S(2)}) collective-permute-start(bf16[1008,512]{1,0:T(8,128)(2,1)S(1)} %join.1), channel_id=1, source_target_pairs={{16,0},{32,16},{48,32},{64,48},{80,64},{96,80},{112,96},{128,112},... | collective-permute-start | bytes 3096584 | tf_op jit(solution)/shard_map/ppermute | solution.py:343
  15.5 0.0 collective-permute-start.6
  15.5 2.8 %collective-permute-start.3 = (bf16[272,512]{1,0:T(8,128)(2,1)S(1)}, bf16[272,512]{1,0:T(8,128)(2,1)S(1)}, u32[]{:S(2)}, u32[]{:S(2)}) collective-permute-start(bf16[272,512]{1,0:T(8,128)(2,1)S(1)} %get-tuple-element.19.refs_0_), channel_id=1, source_target_pairs={{0,3},{1,0},{2,1},{3,2},{4,7},{5,4},{6,5},{7,6},{8,11},{9,8},{10,9... | collective-permute-start | bytes 835592 | tf_op jit(solution)/shard_map/ppermute | solution.py:34
  18.3 4.0 %collective-permute-start = (bf16[336,512]{1,0:T(8,128)(2,1)S(1)}, bf16[336,512]{1,0:T(8,128)(2,1)S(1)}, u32[]{:S(2)}, u32[]{:S(2)}) collective-permute-start(bf16[336,512]{1,0:T(8,128)(2,1)S(1)} %get-tuple-element.18.a.refs_0_), channel_id=1, source_target_pairs={{0,8},{1,9},{2,10},{3,11},{4,12},{5,13},{6,14},{7,15},{8,0},{9,1},... | collective-permute-start | bytes 1032200 | tf_op jit(solution)/shard_map/ppermute | solution.py:34
  22.3 0.8 %collective-permute-start.2 = (bf16[272,512]{1,0:T(8,128)(2,1)S(1)}, bf16[272,512]{1,0:T(8,128)(2,1)S(1)}, u32[]{:S(2)}, u32[]{:S(2)}) collective-permute-start(bf16[272,512]{1,0:T(8,128)(2,1)S(1)} %get-tuple-element.19.refs_0_), channel_id=1, source_target_pairs={{0,2},{1,3},{2,0},{3,1},{4,6},{5,7},{6,4},{7,5},{8,10},{9,11},{10,... | collective-permute-start | bytes 835592 | tf_op jit(solution)/shard_map/ppermute | solution.py:34
  23.1 5.3 %collective-permute-done.3.refs_3_ = bf16[272,512]{1,0:T(8,128)(2,1)S(1)} collective-permute-done((bf16[272,512]{1,0:T(8,128)(2,1)S(1)}, bf16[272,512]{1,0:T(8,128)(2,1)S(1)}, u32[]{:S(2)}, u32[]{:S(2)}) %collective-permute-start.3) | collective-permute-done | bytes 278560 | tf_op jit(solution)/shard_map/ppermute | solution.py:34
  28.3 0.0 collective-permute-start.1
  28.3 0.1 pad_add_fusion.me_ref
  28.4 4.3 %collective-permute-done.2.refs_2_ = bf16[272,512]{1,0:T(8,128)(2,1)S(1)} collective-permute-done((bf16[272,512]{1,0:T(8,128)(2,1)S(1)}, bf16[272,512]{1,0:T(8,128)(2,1)S(1)}, u32[]{:S(2)}, u32[]{:S(2)}) %collective-permute-start.2) | collective-permute-done | bytes 278560 | tf_op jit(solution)/shard_map/ppermute | solution.py:34
  32.7 3.8 %collective-permute-done.1.refs_1_ = bf16[272,512]{1,0:T(8,128)(2,1)S(1)} collective-permute-done((bf16[272,512]{1,0:T(8,128)(2,1)S(1)}, bf16[272,512]{1,0:T(8,128)(2,1)S(1)}, u32[]{:S(2)}, u32[]{:S(2)}) %collective-permute-start.1) | collective-permute-done | bytes 278560 | tf_op jit(solution)/shard_map/ppermute | solution.py:34
  36.5 4.1 %targets.1 = (bf16[16,80,512]{2,1,0:T(8,128)(2,1)S(1)}, s32[776]{0:T(1024)S(1)}, s32[776]{0:T(1024)S(1)}) custom-call(s32[2]{0:T(128)S(1)} %pad_add_fusion.me_ref, bf16[272,512]{1,0:T(8,128)(2,1)S(1)} %get-tuple-element.19.refs_0_, bf16[272,512]{1,0:T(8,128)(2,1)S(1)} %collective-permute-done.1.refs_1_, bf16[272,512]{1,0:T(8,128)(2,1)S(1)} %collective-permute-done.2.refs_2_, ...), custom_call_target="tpu_custom_call" | custom-call | tf_op jit(solution)/shard_map/targets/pallas_call | solution.py:366
  40.7 0.0 collective-permute-done.refs_2_
  40.7 6.6 %collective-permute-start.9 = (bf16[336,512]{1,0:T(8,128)(2,1)S(1)}, bf16[336,512]{1,0:T(8,128)(2,1)S(1)}, u32[]{:S(2)}, u32[]{:S(2)}) collective-permute-start(bf16[336,512]{1,0:T(8,128)(2,1)S(1)} %collective-permute-done.refs_2_), channel_id=1, source_target_pairs={{16,0},{32,16},{48,32},{64,48},{80,64},{96,80},{112,96},{128,112},... | collective-permute-start | bytes 1032200 | tf_op jit(solution)/shard_map/ppermute | solution.py:369
  47.2 0.0 collective-permute-start.7
  47.2 8.0 %pairs_own.1.refs_5_ = f32[16,16,512]{2,1,0:T(8,128)S(1)} custom-call(s32[776]{0:T(1024)S(1)} %get-tuple-element.26.keys_ref, bf16[336,512]{1,0:T(8,128)(2,1)S(1)} %get-tuple-element.18.a.refs_0_, bf16[336,512]{1,0:T(8,128)(2,1)S(1)} %collective-permute-done.4.b.refs_1_, bf16[336,512]{1,0:T(8,128)(2,1)S(1)} %collective-permute-done.refs_2_, ...), custom_call_target="tpu_custom_call" | custom-call | flops 1677721600 | bytes 1376256 | tf_op jit(solution)/shard_map/pairs_own/pallas_call | solution.py:266
  55.2 0.0 collective-permute-done.9.refs_3_
  55.2 0.0 collective-permute-done.7.refs_1_
  55.2 0.0 collective-permute-done.8.refs_2_
  55.2 0.0 collective-permute-done.6.refs_0_
  55.3 9.0 %pairs_far.1 = (f32[4,16,512]{2,1,0:T(8,128)S(1)}, bf16[4,16,512]{2,1,0:T(8,128)(2,1)S(1)}, bf16[4,16,512]{2,1,0:T(8,128)(2,1)S(1)}, bf16[4,16,512]{2,1,0:T(8,128)(2,1)S(1)}) custom-call(s32[776]{0:T(1024)S(1)} %get-tuple-element.23.keys_ref, bf16[1008,512]{1,0:T(8,128)(2,1)} %collective-permute-done.6.refs_0_, ...), custom_call_target="tpu_custom_call" | custom-call | flops 1677721600 | bytes 2752512 | tf_op jit(solution)/shard_map/pairs_far/pallas_call | solution.py:266
  64.2 6.2 %collective-permute-start.10 = (bf16[4,16,512]{2,1,0:T(8,128)(2,1)S(1)}, bf16[4,16,512]{2,1,0:T(8,128)(2,1)S(1)}, u32[]{:S(2)}, u32[]{:S(2)}) collective-permute-start(bf16[4,16,512]{2,1,0:T(8,128)(2,1)S(1)} %get-tuple-element.28), channel_id=1, source_target_pairs={{0,3},{1,0},{2,1},{3,2},{4,7},{5,4},{6,5},{7,6},{8,11},{9,8},{10,9... | collective-permute-start | bytes 196616 | tf_op jit(solution)/shard_map/ppermute | solution.py:34
  70.4 0.0 collective-permute-start.11
  70.4 1.6 %collective-permute-start.12 = (bf16[4,16,512]{2,1,0:T(8,128)(2,1)S(1)}, bf16[4,16,512]{2,1,0:T(8,128)(2,1)S(1)}, u32[]{:S(2)}, u32[]{:S(2)}) collective-permute-start(bf16[4,16,512]{2,1,0:T(8,128)(2,1)S(1)} %get-tuple-element.30), channel_id=1, source_target_pairs={{0,2},{1,3},{2,0},{3,1},{4,6},{5,7},{6,4},{7,5},{8,10},{9,11},{10,... | collective-permute-start | bytes 196616 | tf_op jit(solution)/shard_map/ppermute | solution.py:34
  72.0 0.4 collective-permute-done.10
  72.3 4.3 %collective-permute-done.11 = bf16[4,16,512]{2,1,0:T(8,128)(2,1)S(1)} collective-permute-done((bf16[4,16,512]{2,1,0:T(8,128)(2,1)S(1)}, bf16[4,16,512]{2,1,0:T(8,128)(2,1)S(1)}, u32[]{:S(2)}, u32[]{:S(2)}) %collective-permute-start.11) | collective-permute-done | bytes 65568 | tf_op jit(solution)/shard_map/ppermute | solution.py:34
  76.6 0.0 collective-permute-done.12
  76.6 0.7 convert_add_fusion
Async XLA Ops:
  1.1 9.9 %collective-permute-start.5 = (bf16[336,512]{1,0:T(8,128)(2,1)S(1)}, bf16[336,512]{1,0:T(8,128)(2,1)S(1)}, u32[]{:S(2)}, u32[]{:S(2)}) collective-permute-start(bf16[336,512]{1,0:T(8,128)(2,1)S(1)} %get-tuple-element.18.a.refs_0_), channel_id=1, source_target_pairs={{0,12},{1,13},{2,14},{3,15},{4,0},{5,1},{6,2},{7,3},{8,4},{9,5},{1... | collective-permute-start | bytes 1032200 | tf_op jit(solution)/shard_map/ppermute | solution.py:34
  1.6 9.5 %collective-permute-start.4 = (bf16[336,512]{1,0:T(8,128)(2,1)S(1)}, bf16[336,512]{1,0:T(8,128)(2,1)S(1)}, u32[]{:S(2)}, u32[]{:S(2)}) collective-permute-start(bf16[336,512]{1,0:T(8,128)(2,1)S(1)} %get-tuple-element.18.a.refs_0_), channel_id=1, source_target_pairs={{0,4},{1,5},{2,6},{3,7},{4,8},{5,9},{6,10},{7,11},{8,12},{9,13},{1... | collective-permute-start | bytes 1032200 | tf_op jit(solution)/shard_map/ppermute | solution.py:34
  11.2 44.0 %collective-permute-start.8 = (bf16[1008,512]{1,0:T(8,128)(2,1)S(1)}, bf16[1008,512]{1,0:T(8,128)(2,1)}, u32[]{:S(2)}, u32[]{:S(2)}) collective-permute-start(bf16[1008,512]{1,0:T(8,128)(2,1)S(1)} %join.1), channel_id=1, source_target_pairs={{16,0},{32,16},{48,32},{64,48},{80,64},{96,80},{112,96},{128,112},... | collective-permute-start | bytes 3096584 | tf_op jit(solution)/shard_map/ppermute | solution.py:343
  15.5 39.7 %collective-permute-start.6 = (bf16[1008,512]{1,0:T(8,128)(2,1)S(1)}, bf16[1008,512]{1,0:T(8,128)(2,1)}, u32[]{:S(2)}, u32[]{:S(2)}) collective-permute-start(bf16[1008,512]{1,0:T(8,128)(2,1)S(1)} %join.1), channel_id=1, source_target_pairs={{0,16},{16,32},{32,48},{48,64},{64,80},{80,96},{96,112},{112,128},... | collective-permute-start | bytes 3096584 | tf_op jit(solution)/shard_map/ppermute | solution.py:343
  15.5 12.8 %collective-permute-start.3 = (bf16[272,512]{1,0:T(8,128)(2,1)S(1)}, bf16[272,512]{1,0:T(8,128)(2,1)S(1)}, u32[]{:S(2)}, u32[]{:S(2)}) collective-permute-start(bf16[272,512]{1,0:T(8,128)(2,1)S(1)} %get-tuple-element.19.refs_0_), channel_id=1, source_target_pairs={{0,3},{1,0},{2,1},{3,2},{4,7},{5,4},{6,5},{7,6},{8,11},{9,8},{10,9... | collective-permute-start | bytes 835592 | tf_op jit(solution)/shard_map/ppermute | solution.py:34
  18.3 22.4 %collective-permute-start = (bf16[336,512]{1,0:T(8,128)(2,1)S(1)}, bf16[336,512]{1,0:T(8,128)(2,1)S(1)}, u32[]{:S(2)}, u32[]{:S(2)}) collective-permute-start(bf16[336,512]{1,0:T(8,128)(2,1)S(1)} %get-tuple-element.18.a.refs_0_), channel_id=1, source_target_pairs={{0,8},{1,9},{2,10},{3,11},{4,12},{5,13},{6,14},{7,15},{8,0},{9,1},... | collective-permute-start | bytes 1032200 | tf_op jit(solution)/shard_map/ppermute | solution.py:34
  22.3 10.4 %collective-permute-start.2 = (bf16[272,512]{1,0:T(8,128)(2,1)S(1)}, bf16[272,512]{1,0:T(8,128)(2,1)S(1)}, u32[]{:S(2)}, u32[]{:S(2)}) collective-permute-start(bf16[272,512]{1,0:T(8,128)(2,1)S(1)} %get-tuple-element.19.refs_0_), channel_id=1, source_target_pairs={{0,2},{1,3},{2,0},{3,1},{4,6},{5,7},{6,4},{7,5},{8,10},{9,11},{10,... | collective-permute-start | bytes 835592 | tf_op jit(solution)/shard_map/ppermute | solution.py:34
  28.3 8.2 %collective-permute-start.1 = (bf16[272,512]{1,0:T(8,128)(2,1)S(1)}, bf16[272,512]{1,0:T(8,128)(2,1)S(1)}, u32[]{:S(2)}, u32[]{:S(2)}) collective-permute-start(bf16[272,512]{1,0:T(8,128)(2,1)S(1)} %get-tuple-element.19.refs_0_), channel_id=1, source_target_pairs={{0,1},{1,2},{2,3},{3,0},{4,5},{5,6},{6,7},{7,4},{8,9},{9,10},{10,1... | collective-permute-start | bytes 835592 | tf_op jit(solution)/shard_map/ppermute | solution.py:34
  40.7 14.6 %collective-permute-start.9 = (bf16[336,512]{1,0:T(8,128)(2,1)S(1)}, bf16[336,512]{1,0:T(8,128)(2,1)S(1)}, u32[]{:S(2)}, u32[]{:S(2)}) collective-permute-start(bf16[336,512]{1,0:T(8,128)(2,1)S(1)} %collective-permute-done.refs_2_), channel_id=1, source_target_pairs={{16,0},{32,16},{48,32},{64,48},{80,64},{96,80},{112,96},{128,112},... | collective-permute-start | bytes 1032200 | tf_op jit(solution)/shard_map/ppermute | solution.py:369
  47.2 8.0 %collective-permute-start.7 = (bf16[336,512]{1,0:T(8,128)(2,1)S(1)}, bf16[336,512]{1,0:T(8,128)(2,1)S(1)}, u32[]{:S(2)}, u32[]{:S(2)}) collective-permute-start(bf16[336,512]{1,0:T(8,128)(2,1)S(1)} %collective-permute-done.refs_2_), channel_id=1, source_target_pairs={{0,16},{16,32},{32,48},{48,64},{64,80},{80,96},{96,112},{112,128},... | collective-permute-start | bytes 1032200 | tf_op jit(solution)/shard_map/ppermute | solution.py:369
  64.2 8.1 %collective-permute-start.10 = (bf16[4,16,512]{2,1,0:T(8,128)(2,1)S(1)}, bf16[4,16,512]{2,1,0:T(8,128)(2,1)S(1)}, u32[]{:S(2)}, u32[]{:S(2)}) collective-permute-start(bf16[4,16,512]{2,1,0:T(8,128)(2,1)S(1)} %get-tuple-element.28), channel_id=1, source_target_pairs={{0,3},{1,0},{2,1},{3,2},{4,7},{5,4},{6,5},{7,6},{8,11},{9,8},{10,9... | collective-permute-start | bytes 196616 | tf_op jit(solution)/shard_map/ppermute | solution.py:34
  70.4 6.2 %collective-permute-start.11 = (bf16[4,16,512]{2,1,0:T(8,128)(2,1)S(1)}, bf16[4,16,512]{2,1,0:T(8,128)(2,1)S(1)}, u32[]{:S(2)}, u32[]{:S(2)}) collective-permute-start(bf16[4,16,512]{2,1,0:T(8,128)(2,1)S(1)} %get-tuple-element.29), channel_id=1, source_target_pairs={{0,1},{1,2},{2,3},{3,0},{4,5},{5,6},{6,7},{7,4},{8,9},{9,10},{10,1... | collective-permute-start | bytes 196616 | tf_op jit(solution)/shard_map/ppermute | solution.py:34
  70.4 6.2 %collective-permute-start.12 = (bf16[4,16,512]{2,1,0:T(8,128)(2,1)S(1)}, bf16[4,16,512]{2,1,0:T(8,128)(2,1)S(1)}, u32[]{:S(2)}, u32[]{:S(2)}) collective-permute-start(bf16[4,16,512]{2,1,0:T(8,128)(2,1)S(1)} %get-tuple-element.30), channel_id=1, source_target_pairs={{0,2},{1,3},{2,0},{3,1},{4,6},{5,7},{6,4},{7,5},{8,10},{9,11},{10,... | collective-permute-start | bytes 196616 | tf_op jit(solution)/shard_map/ppermute | solution.py:34

commit v3 on v2

--- a/solution.py
+++ b/solution.py
@@ -96,10 +96,10 @@
         copy.wait()
 
 
-def join_kernel(a, b, c, out):
+def join_kernel(a, b, out):
     rows = a.shape[0]
-    for i, ref in enumerate((a, b, c)):
-        out[i * rows : (i + 1) * rows] = ref[...]
+    out[:rows] = a[...]
+    out[rows:] = b[...]
 
 
 def target_kernel(slots, me_ref, *refs):
@@ -331,16 +331,18 @@
         column[d] = moved(source, d, 0)
     join = pl.pallas_call(
         join_kernel,
-        out_shape=jax.ShapeDtypeStruct((3 * rows, width), jnp.bfloat16),
-        in_specs=[VMEM] * 3,
+        out_shape=jax.ShapeDtypeStruct((2 * rows, width), jnp.bfloat16),
+        in_specs=[VMEM] * 2,
         out_specs=VMEM,
         compiler_params=pltpu.CompilerParams(vmem_limit_bytes=4 << 20),
         name="join",
     )
-    near = join(source, column[1], column[3])
     sides = []
     for ring in (up, down):
-        sides.append([lax.ppermute(near, "owner", ring)])
+        sides.append([lax.ppermute(source, "owner", ring)])
+    near = join(column[1], column[3])
+    for ring, side in zip((up, down), sides):
+        side.append(lax.ppermute(near, "owner", ring))
 
     room = SIDE * local * slots + 8
     me = jnp.stack([helper // SIDE, helper % SIDE]).astype(jnp.int32)
@@ -377,7 +379,7 @@
     )
     places = []
     for s in range(2):
-        places += [(2 * s, 0), (2 * s, rows), (2 * s + 1, 0), (2 * s, 2 * rows)]
+        places += [(3 * s, 0), (3 * s + 1, 0), (3 * s + 2, 0), (3 * s + 1, rows)]
     parts = pair_sums(far, sides[0] + sides[1], tuple(places), tgt, vectors, total)
     result = parts[0]
     for d in order:

time: 77.5 us -> 70.9 us (0.915)
  waiting for transfers between devices: 26 us -> 20.8 us
  starting transfers between devices: 28.2 us -> 26.6 us
    ppermute x9, waiting for transfers between devices: 25.9 us -> 20.8 us  [moved(): return lax.ppermute(value, 'helper', pairs)]
    ppermute x2, starting transfers between devices: 6.55 us -> 2.82 us  [potentials(): side.append(lax.ppermute(opposite, 'owner', ring))]
    ppermute x9, starting transfers between devices: 17.4 us -> 20.7 us  [moved(): return lax.ppermute(value, 'helper', pairs)]
    ppermute x2 -> x4, starting transfers between devices: 4.29 us -> 3.16 us  [the longest x2 2.97 us: potentials(): side.append(lax.ppermute(near, 'owner', ring))]
  transfers between devices with their start and end apart: 13 -> 15, of which waited for: 7 -> 4; matrix products, arithmetic and copies ran while one was open for 0% -> 0% of each run, Pallas kernels for 16% -> 18%
where the time goes in v3:
time: 70.9 us; the launch traced here: 70.6 us
  starting transfers between devices  26.6 us (38%)
  Pallas kernels  22.3 us (31%)
  waiting for transfers between devices  20.8 us (29%)
  other arithmetic  0.76 us (1%)
    ppermute x9, waiting for transfers between devices, moved(): return lax.ppermute(value, 'helper', pairs)  20.8 us
    ppermute x9, starting transfers between devices, moved(): return lax.ppermute(value, 'helper', pairs)  20.7 us
    pallas_call x2, Pallas kernels, pair_sums(): pl.pallas_call(functools.partial(pair_kernel, places, last), out_shape=ou...  17.1 us
    pallas_call x1, Pallas kernels, potentials(): tgt, own, far = make_targets(me, *[row[d] for d in range(SIDE)])  4.13 us
    ppermute x2, starting transfers between devices, potentials(): side.append(lax.ppermute(near, 'owner', ring))  2.97 us
    ppermute x2, starting transfers between devices, potentials(): side.append(lax.ppermute(opposite, 'owner', ring))  2.82 us
  transfers between devices with their start and end apart: 15, of which 4 were waited for; matrix products, arithmetic and copies ran while one was open for 0% of the time, Pallas kernels for 18%

profile of v3, /device:TPU:16, one launch (start us, length us, event | category | flops | bytes accessed | tf_op | source)
XLA Modules:
  0.0 70.6 jit_solution(365923544178498755)
XLA Ops:
  0.0 1.1 %pack.1 = (bf16[336,512]{1,0:T(8,128)(2,1)S(1)}, bf16[272,512]{1,0:T(8,128)(2,1)S(1)}) custom-call(s32[1]{0:T(128)} %bitcast.first_ref, s32[4]{0:T(128)} %counts_hbm.1, bf16[4,64,512]{2,1,0:T(8,128)(2,1)} %points.1, bf16[4,16,512]{2,1,0:T(8,128)(2,1)} %weights.1, s32[4,48]{1,0:T(4,128)} %lists.1), custom_call_target="tpu_custom_call" | custom-call | tf_op jit(solution)/shard_map/pack/pallas_call | solution.py:301
  1.1 1.4 %collective-permute-start.5 = (bf16[336,512]{1,0:T(8,128)(2,1)S(1)}, bf16[336,512]{1,0:T(8,128)(2,1)S(1)}, u32[]{:S(2)}, u32[]{:S(2)}) collective-permute-start(bf16[336,512]{1,0:T(8,128)(2,1)S(1)} %get-tuple-element.18.refs_0_), channel_id=1, source_target_pairs={{0,4},{1,5},{2,6},{3,7},{4,8},{5,9},{6,10},{7,11},{8,12},{9,13},{1... | collective-permute-start | bytes 1032200 | tf_op jit(solution)/shard_map/ppermute | solution.py:34
  2.5 0.7 %collective-permute-start.6 = (bf16[336,512]{1,0:T(8,128)(2,1)S(1)}, bf16[336,512]{1,0:T(8,128)(2,1)S(1)}, u32[]{:S(2)}, u32[]{:S(2)}) collective-permute-start(bf16[336,512]{1,0:T(8,128)(2,1)S(1)} %get-tuple-element.18.refs_0_), channel_id=1, source_target_pairs={{0,12},{1,13},{2,14},{3,15},{4,0},{5,1},{6,2},{7,3},{8,4},{9,5},{1... | collective-permute-start | bytes 1032200 | tf_op jit(solution)/shard_map/ppermute | solution.py:34
  3.2 1.5 %collective-permute-start.1 = (bf16[272,512]{1,0:T(8,128)(2,1)S(1)}, bf16[272,512]{1,0:T(8,128)(2,1)S(1)}, u32[]{:S(2)}, u32[]{:S(2)}) collective-permute-start(bf16[272,512]{1,0:T(8,128)(2,1)S(1)} %get-tuple-element.19.refs_0_), channel_id=1, source_target_pairs={{0,1},{1,2},{2,3},{3,0},{4,5},{5,6},{6,7},{7,4},{8,9},{9,10},{10,1... | collective-permute-start | bytes 835592 | tf_op jit(solution)/shard_map/ppermute | solution.py:34
  4.7 2.7 %collective-permute-start.2 = (bf16[272,512]{1,0:T(8,128)(2,1)S(1)}, bf16[272,512]{1,0:T(8,128)(2,1)S(1)}, u32[]{:S(2)}, u32[]{:S(2)}) collective-permute-start(bf16[272,512]{1,0:T(8,128)(2,1)S(1)} %get-tuple-element.19.refs_0_), channel_id=1, source_target_pairs={{0,2},{1,3},{2,0},{3,1},{4,6},{5,7},{6,4},{7,5},{8,10},{9,11},{10,... | collective-permute-start | bytes 835592 | tf_op jit(solution)/shard_map/ppermute | solution.py:34
  7.4 1.5 %collective-permute-start = (bf16[336,512]{1,0:T(8,128)(2,1)S(1)}, bf16[336,512]{1,0:T(8,128)(2,1)}, u32[]{:S(2)}, u32[]{:S(2)}) collective-permute-start(bf16[336,512]{1,0:T(8,128)(2,1)S(1)} %get-tuple-element.18.refs_0_), channel_id=1, source_target_pairs={{0,8},{1,9},{2,10},{3,11},{4,12},{5,13},{6,14},{7,15},{8,0},{9,1},... | collective-permute-start | bytes 1032200 | tf_op jit(solution)/shard_map/ppermute | solution.py:34
  9.0 9.4 %collective-permute-done.5.a.refs_1_ = bf16[336,512]{1,0:T(8,128)(2,1)S(1)} collective-permute-done((bf16[336,512]{1,0:T(8,128)(2,1)S(1)}, bf16[336,512]{1,0:T(8,128)(2,1)S(1)}, u32[]{:S(2)}, u32[]{:S(2)}) %collective-permute-start.5) | collective-permute-done | bytes 344096 | tf_op jit(solution)/shard_map/ppermute | solution.py:34
  18.3 0.0 collective-permute-start.4
  18.4 0.0 collective-permute-done.6.b.refs_3_
  18.4 3.0 %collective-permute-start.10 = (bf16[672,512]{1,0:T(8,128)(2,1)S(1)}, bf16[672,512]{1,0:T(8,128)(2,1)S(1)}, u32[]{:S(2)}, u32[]{:S(2)}) collective-permute-start(bf16[672,512]{1,0:T(8,128)(2,1)S(1)} %join.1), channel_id=1, source_target_pairs={{16,0},{32,16},{48,32},{64,48},{80,64},{96,80},{112,96},{128,112},... | collective-permute-start | bytes 2064392 | tf_op jit(solution)/shard_map/ppermute | solution.py:345
  21.4 0.0 collective-permute-done.1.refs_1_
  21.4 0.0 collective-permute-start.7
  21.4 0.0 collective-permute-done.2.refs_2_
  21.4 2.8 %collective-permute-start.3 = (bf16[272,512]{1,0:T(8,128)(2,1)S(1)}, bf16[272,512]{1,0:T(8,128)(2,1)S(1)}, u32[]{:S(2)}, u32[]{:S(2)}) collective-permute-start(bf16[272,512]{1,0:T(8,128)(2,1)S(1)} %get-tuple-element.19.refs_0_), channel_id=1, source_target_pairs={{0,3},{1,0},{2,1},{3,2},{4,7},{5,4},{6,5},{7,6},{8,11},{9,8},{10,9... | collective-permute-start | bytes 835592 | tf_op jit(solution)/shard_map/ppermute | solution.py:34
  24.2 0.1 pad_add_fusion.me_ref
  24.3 6.7 %collective-permute-done.3.refs_3_ = bf16[272,512]{1,0:T(8,128)(2,1)S(1)} collective-permute-done((bf16[272,512]{1,0:T(8,128)(2,1)S(1)}, bf16[272,512]{1,0:T(8,128)(2,1)S(1)}, u32[]{:S(2)}, u32[]{:S(2)}) %collective-permute-start.3) | collective-permute-done | bytes 278560 | tf_op jit(solution)/shard_map/ppermute | solution.py:34
  31.0 0.2 collective-permute-start.9
  31.2 4.1 %targets.1 = (bf16[16,80,512]{2,1,0:T(8,128)(2,1)S(1)}, s32[776]{0:T(1024)S(1)}, s32[776]{0:T(1024)S(1)}) custom-call(s32[2]{0:T(128)S(1)} %pad_add_fusion.me_ref, bf16[272,512]{1,0:T(8,128)(2,1)S(1)} %get-tuple-element.19.refs_0_, bf16[272,512]{1,0:T(8,128)(2,1)S(1)} %collective-permute-done.1.refs_1_, bf16[272,512]{1,0:T(8,128)(2,1)S(1)} %collective-permute-done.2.refs_2_, ...), custom_call_target="tpu_custom_call" | custom-call | tf_op jit(solution)/shard_map/targets/pallas_call | solution.py:368
  35.4 0.0 collective-permute-done.refs_2_
  35.4 2.8 %collective-permute-start.11 = (bf16[336,512]{1,0:T(8,128)(2,1)}, bf16[336,512]{1,0:T(8,128)(2,1)S(1)}, u32[]{:S(2)}, u32[]{:S(2)}) collective-permute-start(bf16[336,512]{1,0:T(8,128)(2,1)} %collective-permute-done.refs_2_), channel_id=1, source_target_pairs={{16,0},{32,16},{48,32},{64,48},{80,64},{96,80},{112,96},{128,112},... | collective-permute-start | bytes 1032200 | tf_op jit(solution)/shard_map/ppermute | solution.py:371
  38.2 0.0 collective-permute-done.4.refs_0_
  38.2 0.0 collective-permute-start.8
  38.2 8.4 %pairs_own.1.refs_7_ = f32[16,16,512]{2,1,0:T(8,128)S(1)} custom-call(s32[776]{0:T(1024)S(1)} %get-tuple-element.26.keys_ref, bf16[336,512]{1,0:T(8,128)(2,1)S(1)} %get-tuple-element.18.refs_0_, bf16[336,512]{1,0:T(8,128)(2,1)S(1)} %collective-permute-done.5.a.refs_1_, bf16[336,512]{1,0:T(8,128)(2,1)} %collective-permute-done.refs_2_, ...), custom_call_target="tpu_custom_call" | custom-call | flops 1677721600 | bytes 1376256 | tf_op jit(solution)/shard_map/pairs_own/pallas_call | solution.py:266
  46.6 0.0 collective-permute-done.9.refs_3_
  46.6 0.0 collective-permute-done.11.refs_5_
  46.6 0.0 collective-permute-done.8.refs_2_
  46.6 0.0 collective-permute-done.10.refs_4_
  46.6 0.0 collective-permute-done.7.refs_1_
  46.7 8.7 %pairs_far.1 = (f32[4,16,512]{2,1,0:T(8,128)S(1)}, bf16[4,16,512]{2,1,0:T(8,128)(2,1)S(1)}, bf16[4,16,512]{2,1,0:T(8,128)(2,1)S(1)}, bf16[4,16,512]{2,1,0:T(8,128)(2,1)S(1)}) custom-call(s32[776]{0:T(1024)S(1)} %get-tuple-element.23.keys_ref, bf16[336,512]{1,0:T(8,128)(2,1)} %collective-permute-done.4.refs_0_, ...), custom_call_target="tpu_custom_call" | custom-call | flops 1677721600 | bytes 2752512 | tf_op jit(solution)/shard_map/pairs_far/pallas_call | solution.py:266
  55.3 8.4 %collective-permute-start.12 = (bf16[4,16,512]{2,1,0:T(8,128)(2,1)S(1)}, bf16[4,16,512]{2,1,0:T(8,128)(2,1)S(1)}, u32[]{:S(2)}, u32[]{:S(2)}) collective-permute-start(bf16[4,16,512]{2,1,0:T(8,128)(2,1)S(1)} %get-tuple-element.28), channel_id=1, source_target_pairs={{0,3},{1,0},{2,1},{3,2},{4,7},{5,4},{6,5},{7,6},{8,11},{9,8},{10,9... | collective-permute-start | bytes 196616 | tf_op jit(solution)/shard_map/ppermute | solution.py:34
  63.7 0.0 collective-permute-start.13
  63.7 1.6 %collective-permute-start.14 = (bf16[4,16,512]{2,1,0:T(8,128)(2,1)S(1)}, bf16[4,16,512]{2,1,0:T(8,128)(2,1)S(1)}, u32[]{:S(2)}, u32[]{:S(2)}) collective-permute-start(bf16[4,16,512]{2,1,0:T(8,128)(2,1)S(1)} %get-tuple-element.30), channel_id=1, source_target_pairs={{0,2},{1,3},{2,0},{3,1},{4,6},{5,7},{6,4},{7,5},{8,10},{9,11},{10,... | collective-permute-start | bytes 196616 | tf_op jit(solution)/shard_map/ppermute | solution.py:34
  65.3 0.4 collective-permute-done.12
  65.6 4.3 %collective-permute-done.13 = bf16[4,16,512]{2,1,0:T(8,128)(2,1)S(1)} collective-permute-done((bf16[4,16,512]{2,1,0:T(8,128)(2,1)S(1)}, bf16[4,16,512]{2,1,0:T(8,128)(2,1)S(1)}, u32[]{:S(2)}, u32[]{:S(2)}) %collective-permute-start.13) | collective-permute-done | bytes 65568 | tf_op jit(solution)/shard_map/ppermute | solution.py:34
  69.9 0.0 collective-permute-done.14
  69.9 0.7 convert_add_fusion
  (1 shorter events, 0.0 us)
Async XLA Ops:
  1.1 17.3 %collective-permute-start.5 = (bf16[336,512]{1,0:T(8,128)(2,1)S(1)}, bf16[336,512]{1,0:T(8,128)(2,1)S(1)}, u32[]{:S(2)}, u32[]{:S(2)}) collective-permute-start(bf16[336,512]{1,0:T(8,128)(2,1)S(1)} %get-tuple-element.18.refs_0_), channel_id=1, source_target_pairs={{0,4},{1,5},{2,6},{3,7},{4,8},{5,9},{6,10},{7,11},{8,12},{9,13},{1... | collective-permute-start | bytes 1032200 | tf_op jit(solution)/shard_map/ppermute | solution.py:34
  2.5 15.9 %collective-permute-start.6 = (bf16[336,512]{1,0:T(8,128)(2,1)S(1)}, bf16[336,512]{1,0:T(8,128)(2,1)S(1)}, u32[]{:S(2)}, u32[]{:S(2)}) collective-permute-start(bf16[336,512]{1,0:T(8,128)(2,1)S(1)} %get-tuple-element.18.refs_0_), channel_id=1, source_target_pairs={{0,12},{1,13},{2,14},{3,15},{4,0},{5,1},{6,2},{7,3},{8,4},{9,5},{1... | collective-permute-start | bytes 1032200 | tf_op jit(solution)/shard_map/ppermute | solution.py:34
  3.2 18.2 %collective-permute-start.1 = (bf16[272,512]{1,0:T(8,128)(2,1)S(1)}, bf16[272,512]{1,0:T(8,128)(2,1)S(1)}, u32[]{:S(2)}, u32[]{:S(2)}) collective-permute-start(bf16[272,512]{1,0:T(8,128)(2,1)S(1)} %get-tuple-element.19.refs_0_), channel_id=1, source_target_pairs={{0,1},{1,2},{2,3},{3,0},{4,5},{5,6},{6,7},{7,4},{8,9},{9,10},{10,1... | collective-permute-start | bytes 835592 | tf_op jit(solution)/shard_map/ppermute | solution.py:34
  4.7 16.7 %collective-permute-start.2 = (bf16[272,512]{1,0:T(8,128)(2,1)S(1)}, bf16[272,512]{1,0:T(8,128)(2,1)S(1)}, u32[]{:S(2)}, u32[]{:S(2)}) collective-permute-start(bf16[272,512]{1,0:T(8,128)(2,1)S(1)} %get-tuple-element.19.refs_0_), channel_id=1, source_target_pairs={{0,2},{1,3},{2,0},{3,1},{4,6},{5,7},{6,4},{7,5},{8,10},{9,11},{10,... | collective-permute-start | bytes 835592 | tf_op jit(solution)/shard_map/ppermute | solution.py:34
  7.4 27.9 %collective-permute-start = (bf16[336,512]{1,0:T(8,128)(2,1)S(1)}, bf16[336,512]{1,0:T(8,128)(2,1)}, u32[]{:S(2)}, u32[]{:S(2)}) collective-permute-start(bf16[336,512]{1,0:T(8,128)(2,1)S(1)} %get-tuple-element.18.refs_0_), channel_id=1, source_target_pairs={{0,8},{1,9},{2,10},{3,11},{4,12},{5,13},{6,14},{7,15},{8,0},{9,1},... | collective-permute-start | bytes 1032200 | tf_op jit(solution)/shard_map/ppermute | solution.py:34
  18.3 19.8 %collective-permute-start.4 = (bf16[336,512]{1,0:T(8,128)(2,1)S(1)}, bf16[336,512]{1,0:T(8,128)(2,1)}, u32[]{:S(2)}, u32[]{:S(2)}) collective-permute-start(bf16[336,512]{1,0:T(8,128)(2,1)S(1)} %get-tuple-element.18.refs_0_), channel_id=1, source_target_pairs={{0,16},{16,32},{32,48},{48,64},{64,80},{80,96},{96,112},{112,128},... | collective-permute-start | bytes 1032200 | tf_op jit(solution)/shard_map/ppermute | solution.py:342
  18.4 28.2 %collective-permute-start.10 = (bf16[672,512]{1,0:T(8,128)(2,1)S(1)}, bf16[672,512]{1,0:T(8,128)(2,1)S(1)}, u32[]{:S(2)}, u32[]{:S(2)}) collective-permute-start(bf16[672,512]{1,0:T(8,128)(2,1)S(1)} %join.1), channel_id=1, source_target_pairs={{16,0},{32,16},{48,32},{64,48},{80,64},{96,80},{112,96},{128,112},... | collective-permute-start | bytes 2064392 | tf_op jit(solution)/shard_map/ppermute | solution.py:345
  21.4 25.3 %collective-permute-start.7 = (bf16[672,512]{1,0:T(8,128)(2,1)S(1)}, bf16[672,512]{1,0:T(8,128)(2,1)}, u32[]{:S(2)}, u32[]{:S(2)}) collective-permute-start(bf16[672,512]{1,0:T(8,128)(2,1)S(1)} %join.1), channel_id=1, source_target_pairs={{0,16},{16,32},{32,48},{48,64},{64,80},{80,96},{96,112},{112,128},... | collective-permute-start | bytes 2064392 | tf_op jit(solution)/shard_map/ppermute | solution.py:345
  21.4 9.7 %collective-permute-start.3 = (bf16[272,512]{1,0:T(8,128)(2,1)S(1)}, bf16[272,512]{1,0:T(8,128)(2,1)S(1)}, u32[]{:S(2)}, u32[]{:S(2)}) collective-permute-start(bf16[272,512]{1,0:T(8,128)(2,1)S(1)} %get-tuple-element.19.refs_0_), channel_id=1, source_target_pairs={{0,3},{1,0},{2,1},{3,2},{4,7},{5,4},{6,5},{7,6},{8,11},{9,8},{10,9... | collective-permute-start | bytes 835592 | tf_op jit(solution)/shard_map/ppermute | solution.py:34
  31.0 15.6 %collective-permute-start.9 = (bf16[336,512]{1,0:T(8,128)(2,1)S(1)}, bf16[336,512]{1,0:T(8,128)(2,1)S(1)}, u32[]{:S(2)}, u32[]{:S(2)}) collective-permute-start(bf16[336,512]{1,0:T(8,128)(2,1)S(1)} %get-tuple-element.18.refs_0_), channel_id=1, source_target_pairs={{16,0},{32,16},{48,32},{64,48},{80,64},{96,80},{112,96},{128,112},... | collective-permute-start | bytes 1032200 | tf_op jit(solution)/shard_map/ppermute | solution.py:342
  35.4 11.2 %collective-permute-start.11 = (bf16[336,512]{1,0:T(8,128)(2,1)}, bf16[336,512]{1,0:T(8,128)(2,1)S(1)}, u32[]{:S(2)}, u32[]{:S(2)}) collective-permute-start(bf16[336,512]{1,0:T(8,128)(2,1)} %collective-permute-done.refs_2_), channel_id=1, source_target_pairs={{16,0},{32,16},{48,32},{64,48},{80,64},{96,80},{112,96},{128,112},... | collective-permute-start | bytes 1032200 | tf_op jit(solution)/shard_map/ppermute | solution.py:371
  38.2 8.4 %collective-permute-start.8 = (bf16[336,512]{1,0:T(8,128)(2,1)}, bf16[336,512]{1,0:T(8,128)(2,1)S(1)}, u32[]{:S(2)}, u32[]{:S(2)}) collective-permute-start(bf16[336,512]{1,0:T(8,128)(2,1)} %collective-permute-done.refs_2_), channel_id=1, source_target_pairs={{0,16},{16,32},{32,48},{48,64},{64,80},{80,96},{96,112},{112,128},... | collective-permute-start | bytes 1032200 | tf_op jit(solution)/shard_map/ppermute | solution.py:371
  55.3 10.3 %collective-permute-start.12 = (bf16[4,16,512]{2,1,0:T(8,128)(2,1)S(1)}, bf16[4,16,512]{2,1,0:T(8,128)(2,1)S(1)}, u32[]{:S(2)}, u32[]{:S(2)}) collective-permute-start(bf16[4,16,512]{2,1,0:T(8,128)(2,1)S(1)} %get-tuple-element.28), channel_id=1, source_target_pairs={{0,3},{1,0},{2,1},{3,2},{4,7},{5,4},{6,5},{7,6},{8,11},{9,8},{10,9... | collective-permute-start | bytes 196616 | tf_op jit(solution)/shard_map/ppermute | solution.py:34
  63.7 6.2 %collective-permute-start.13 = (bf16[4,16,512]{2,1,0:T(8,128)(2,1)S(1)}, bf16[4,16,512]{2,1,0:T(8,128)(2,1)S(1)}, u32[]{:S(2)}, u32[]{:S(2)}) collective-permute-start(bf16[4,16,512]{2,1,0:T(8,128)(2,1)S(1)} %get-tuple-element.29), channel_id=1, source_target_pairs={{0,1},{1,2},{2,3},{3,0},{4,5},{5,6},{6,7},{7,4},{8,9},{9,10},{10,1... | collective-permute-start | bytes 196616 | tf_op jit(solution)/shard_map/ppermute | solution.py:34
  63.7 6.2 %collective-permute-start.14 = (bf16[4,16,512]{2,1,0:T(8,128)(2,1)S(1)}, bf16[4,16,512]{2,1,0:T(8,128)(2,1)S(1)}, u32[]{:S(2)}, u32[]{:S(2)}) collective-permute-start(bf16[4,16,512]{2,1,0:T(8,128)(2,1)S(1)} %get-tuple-element.30), channel_id=1, source_target_pairs={{0,2},{1,3},{2,0},{3,1},{4,6},{5,7},{6,4},{7,5},{8,10},{9,11},{10,... | collective-permute-start | bytes 196616 | tf_op jit(solution)/shard_map/ppermute | solution.py:34

commit v4 on v3

--- a/solution.py
+++ b/solution.py
@@ -340,9 +340,9 @@
     sides = []
     for ring in (up, down):
         sides.append([lax.ppermute(source, "owner", ring)])
-    near = join(column[1], column[3])
-    for ring, side in zip((up, down), sides):
-        side.append(lax.ppermute(near, "owner", ring))
+    for d in order[:2]:
+        for ring, side in zip((up, down), sides):
+            side.append(lax.ppermute(column[d], "owner", ring))
 
     room = SIDE * local * slots + 8
     me = jnp.stack([helper // SIDE, helper % SIDE]).astype(jnp.int32)
@@ -379,7 +379,7 @@
     )
     places = []
     for s in range(2):
-        places += [(3 * s, 0), (3 * s + 1, 0), (3 * s + 2, 0), (3 * s + 1, rows)]
+        places += [(4 * s, 0), (4 * s + 1, 0), (4 * s + 3, 0), (4 * s + 2, 0)]
     parts = pair_sums(far, sides[0] + sides[1], tuple(places), tgt, vectors, total)
     result = parts[0]
     for d in order:

time: 70.9 us -> 63.7 us (0.90)
  waiting for transfers between devices: 20.8 us -> 12.2 us
  starting transfers between devices: 26.6 us -> 29.3 us
  Pallas kernels: 22.3 us -> 21.2 us
    ppermute x9, waiting for transfers between devices: 20.8 us -> 10.8 us  [moved(): return lax.ppermute(value, 'helper', pairs)]
    ppermute x9, starting transfers between devices: 20.7 us -> 16 us  [moved(): return lax.ppermute(value, 'helper', pairs)]
    ppermute x2, starting transfers between devices: 0.19 us -> 4.19 us  [potentials(): sides.append([lax.ppermute(source, 'owner', ring)])]
    ppermute x2 -> x4, starting transfers between devices: 2.97 us -> 5.91 us  [potentials(): side.append(lax.ppermute(column[d], 'owner', ring))]
    ppermute x2 -> x4, waiting for transfers between devices: 0.01 us -> 1.3 us  [potentials(): side.append(lax.ppermute(column[d], 'owner', ring))]
    pallas_call x2, Pallas kernels: 17.1 us -> 16 us  [pair_sums(): pl.pallas_call(functools.partial(pair_kernel, places, last), out_shape=ou...]
  transfers between devices with their start and end apart: 15 -> 17, of which waited for: 4 -> 5; matrix products, arithmetic and copies ran while one was open for 0% -> 0% of each run, Pallas kernels for 18% -> 19%
where the time goes in v4:
time: 63.7 us; the launch traced here: 63.5 us
  starting transfers between devices  29.3 us (46%)
  Pallas kernels  21.2 us (33%)
  waiting for transfers between devices  12.2 us (19%)
  other arithmetic  0.76 us (1%)
    ppermute x9, starting transfers between devices, moved(): return lax.ppermute(value, 'helper', pairs)  16 us
    pallas_call x2, Pallas kernels, pair_sums(): pl.pallas_call(functools.partial(pair_kernel, places, last), out_shape=ou...  16 us
    ppermute x9, waiting for transfers between devices, moved(): return lax.ppermute(value, 'helper', pairs)  10.8 us
    ppermute x4, starting transfers between devices, potentials(): side.append(lax.ppermute(column[d], 'owner', ring))  5.91 us
    ppermute x2, starting transfers between devices, potentials(): sides.append([lax.ppermute(source, 'owner', ring)])  4.19 us
    pallas_call x1, Pallas kernels, potentials(): tgt, own, far = make_targets(me, *[row[d] for d in range(SIDE)])  4.13 us
    ppermute x2, starting transfers between devices, potentials(): side.append(lax.ppermute(opposite, 'owner', ring))  3.17 us
    ppermute x4, waiting for transfers between devices, potentials(): side.append(lax.ppermute(column[d], 'owner', ring))  1.3 us
  transfers between devices with their start and end apart: 17, of which 5 were waited for; matrix products, arithmetic and copies ran while one was open for 0% of the time, Pallas kernels for 19%

profile of v4, /device:TPU:16, one launch (start us, length us, event | category | flops | bytes accessed | tf_op | source)
XLA Modules:
  0.0 63.5 jit_solution(11816894919449021832)
XLA Ops:
  0.0 1.1 %pack.1 = (bf16[336,512]{1,0:T(8,128)(2,1)S(1)}, bf16[272,512]{1,0:T(8,128)(2,1)S(1)}) custom-call(s32[1]{0:T(128)} %bitcast.first_ref, s32[4]{0:T(128)} %counts_hbm.1, bf16[4,64,512]{2,1,0:T(8,128)(2,1)} %points.1, bf16[4,16,512]{2,1,0:T(8,128)(2,1)} %weights.1, s32[4,48]{1,0:T(4,128)} %lists.1), custom_call_target="tpu_custom_call" | custom-call | tf_op jit(solution)/shard_map/pack/pallas_call | solution.py:301
  1.1 2.1 %collective-permute-start = (bf16[336,512]{1,0:T(8,128)(2,1)S(1)}, bf16[336,512]{1,0:T(8,128)(2,1)S(1)}, u32[]{:S(2)}, u32[]{:S(2)}) collective-permute-start(bf16[336,512]{1,0:T(8,128)(2,1)S(1)} %get-tuple-element.18.refs_0_), channel_id=1, source_target_pairs={{0,8},{1,9},{2,10},{3,11},{4,12},{5,13},{6,14},{7,15},{8,0},{9,1},... | collective-permute-start | bytes 1032200 | tf_op jit(solution)/shard_map/ppermute | solution.py:34
  3.2 0.0 collective-permute-start.1
  3.2 2.5 %collective-permute-start.2 = (bf16[272,512]{1,0:T(8,128)(2,1)S(1)}, bf16[272,512]{1,0:T(8,128)(2,1)S(1)}, u32[]{:S(2)}, u32[]{:S(2)}) collective-permute-start(bf16[272,512]{1,0:T(8,128)(2,1)S(1)} %get-tuple-element.19.refs_0_), channel_id=1, source_target_pairs={{0,2},{1,3},{2,0},{3,1},{4,6},{5,7},{6,4},{7,5},{8,10},{9,11},{10,... | collective-permute-start | bytes 835592 | tf_op jit(solution)/shard_map/ppermute | solution.py:34
  5.7 1.4 %collective-permute-start.3 = (bf16[272,512]{1,0:T(8,128)(2,1)S(1)}, bf16[272,512]{1,0:T(8,128)(2,1)S(1)}, u32[]{:S(2)}, u32[]{:S(2)}) collective-permute-start(bf16[272,512]{1,0:T(8,128)(2,1)S(1)} %get-tuple-element.19.refs_0_), channel_id=1, source_target_pairs={{0,3},{1,0},{2,1},{3,2},{4,7},{5,4},{6,5},{7,6},{8,11},{9,8},{10,9... | collective-permute-start | bytes 835592 | tf_op jit(solution)/shard_map/ppermute | solution.py:34
  7.2 2.2 %collective-permute-start.5 = (bf16[336,512]{1,0:T(8,128)(2,1)S(1)}, bf16[336,512]{1,0:T(8,128)(2,1)S(1)}, u32[]{:S(2)}, u32[]{:S(2)}) collective-permute-start(bf16[336,512]{1,0:T(8,128)(2,1)S(1)} %get-tuple-element.18.refs_0_), channel_id=1, source_target_pairs={{0,4},{1,5},{2,6},{3,7},{4,8},{5,9},{6,10},{7,11},{8,12},{9,13},{1... | collective-permute-start | bytes 1032200 | tf_op jit(solution)/shard_map/ppermute | solution.py:34
  9.4 0.1 pad_add_fusion.me_ref
  9.4 2.0 %collective-permute-done.1.refs_1_ = bf16[272,512]{1,0:T(8,128)(2,1)S(1)} collective-permute-done((bf16[272,512]{1,0:T(8,128)(2,1)S(1)}, bf16[272,512]{1,0:T(8,128)(2,1)S(1)}, u32[]{:S(2)}, u32[]{:S(2)}) %collective-permute-start.1) | collective-permute-done | bytes 278560 | tf_op jit(solution)/shard_map/ppermute | solution.py:34
  11.5 2.2 %collective-permute-start.7 = (bf16[336,512]{1,0:T(8,128)(2,1)S(1)}, bf16[336,512]{1,0:T(8,128)(2,1)S(1)}, u32[]{:S(2)}, u32[]{:S(2)}) collective-permute-start(bf16[336,512]{1,0:T(8,128)(2,1)S(1)} %get-tuple-element.18.refs_0_), channel_id=1, source_target_pairs={{0,12},{1,13},{2,14},{3,15},{4,0},{5,1},{6,2},{7,3},{8,4},{9,5},{1... | collective-permute-start | bytes 1032200 | tf_op jit(solution)/shard_map/ppermute | solution.py:34
  13.7 4.2 %collective-permute-done.2.refs_2_ = bf16[272,512]{1,0:T(8,128)(2,1)S(1)} collective-permute-done((bf16[272,512]{1,0:T(8,128)(2,1)S(1)}, bf16[272,512]{1,0:T(8,128)(2,1)S(1)}, u32[]{:S(2)}, u32[]{:S(2)}) %collective-permute-start.2) | collective-permute-done | bytes 278560 | tf_op jit(solution)/shard_map/ppermute | solution.py:34
  17.8 4.2 %collective-permute-start.10 = (bf16[336,512]{1,0:T(8,128)(2,1)S(1)}, bf16[336,512]{1,0:T(8,128)(2,1)S(1)}, u32[]{:S(2)}, u32[]{:S(2)}) collective-permute-start(bf16[336,512]{1,0:T(8,128)(2,1)S(1)} %get-tuple-element.18.refs_0_), channel_id=1, source_target_pairs={{16,0},{32,16},{48,32},{64,48},{80,64},{96,80},{112,96},{128,112},... | collective-permute-start | bytes 1032200 | tf_op jit(solution)/shard_map/ppermute | solution.py:342
  22.0 0.0 collective-permute-done.3.refs_3_
  22.0 0.0 collective-permute-start.4
  22.0 4.1 %targets.1 = (bf16[16,80,512]{2,1,0:T(8,128)(2,1)S(1)}, s32[776]{0:T(1024)S(1)}, s32[776]{0:T(1024)S(1)}) custom-call(s32[2]{0:T(128)S(1)} %pad_add_fusion.me_ref, bf16[272,512]{1,0:T(8,128)(2,1)S(1)} %get-tuple-element.19.refs_0_, bf16[272,512]{1,0:T(8,128)(2,1)S(1)} %collective-permute-done.1.refs_1_, bf16[272,512]{1,0:T(8,128)(2,1)S(1)} %collective-permute-done.2.refs_2_, ...), custom_call_target="tpu_custom_call" | custom-call | tf_op jit(solution)/shard_map/targets/pallas_call | solution.py:368
  26.2 0.0 collective-permute-done.refs_2_
  26.2 3.2 %collective-permute-start.13 = (bf16[336,512]{1,0:T(8,128)(2,1)S(1)}, bf16[336,512]{1,0:T(8,128)(2,1)S(1)}, u32[]{:S(2)}, u32[]{:S(2)}) collective-permute-start(bf16[336,512]{1,0:T(8,128)(2,1)S(1)} %collective-permute-done.refs_2_), channel_id=1, source_target_pairs={{16,0},{32,16},{48,32},{64,48},{80,64},{96,80},{112,96},{128,112},... | collective-permute-start | bytes 1032200 | tf_op jit(solution)/shard_map/ppermute | solution.py:371
  29.4 0.0 collective-permute-done.5.refs_1_
  29.4 0.0 collective-permute-start.9
  29.4 0.0 collective-permute-done.7.refs_3_
  29.4 3.0 %collective-permute-start.11 = (bf16[336,512]{1,0:T(8,128)(2,1)S(1)}, bf16[336,512]{1,0:T(8,128)(2,1)S(1)}, u32[]{:S(2)}, u32[]{:S(2)}) collective-permute-start(bf16[336,512]{1,0:T(8,128)(2,1)S(1)} %collective-permute-done.5.refs_1_), channel_id=1, source_target_pairs={{16,0},{32,16},{48,32},{64,48},{80,64},{96,80},{112,96},{128,112},... | collective-permute-start | bytes 1032200 | tf_op jit(solution)/shard_map/ppermute | solution.py:345
  32.3 0.0 collective-permute-done.10.refs_4_
  32.3 0.0 collective-permute-start.6
  32.3 0.0 collective-permute-done.4.refs_0_
  32.3 3.0 %collective-permute-start.12 = (bf16[336,512]{1,0:T(8,128)(2,1)S(1)}, bf16[336,512]{1,0:T(8,128)(2,1)S(1)}, u32[]{:S(2)}, u32[]{:S(2)}) collective-permute-start(bf16[336,512]{1,0:T(8,128)(2,1)S(1)} %collective-permute-done.7.refs_3_), channel_id=1, source_target_pairs={{16,0},{32,16},{48,32},{64,48},{80,64},{96,80},{112,96},{128,112},... | collective-permute-start | bytes 1032200 | tf_op jit(solution)/shard_map/ppermute | solution.py:345
  35.3 0.0 collective-permute-done.13.refs_7_
  35.3 0.0 collective-permute-start.8
  35.3 8.0 %pairs_own.1.refs_9_ = f32[16,16,512]{2,1,0:T(8,128)S(1)} custom-call(s32[776]{0:T(1024)S(1)} %get-tuple-element.26.keys_ref, bf16[336,512]{1,0:T(8,128)(2,1)S(1)} %get-tuple-element.18.refs_0_, bf16[336,512]{1,0:T(8,128)(2,1)S(1)} %collective-permute-done.5.refs_1_, bf16[336,512]{1,0:T(8,128)(2,1)S(1)} %collective-permute-done.refs_2_, ...), custom_call_target="tpu_custom_call" | custom-call | flops 1677721600 | bytes 1376256 | tf_op jit(solution)/shard_map/pairs_own/pallas_call | solution.py:266
  43.3 0.0 collective-permute-done.9.refs_3_
  43.3 0.0 collective-permute-done.11.refs_5_
  43.3 0.0 collective-permute-done.12.refs_6_
  43.3 0.0 collective-permute-done.6.refs_1_
  43.3 1.3 %collective-permute-done.8.refs_2_ = bf16[336,512]{1,0:T(8,128)(2,1)S(1)} collective-permute-done((bf16[336,512]{1,0:T(8,128)(2,1)S(1)}, bf16[336,512]{1,0:T(8,128)(2,1)S(1)}, u32[]{:S(2)}, u32[]{:S(2)}) %collective-permute-start.8) | collective-permute-done | bytes 344096 | tf_op jit(solution)/shard_map/ppermute | solution.py:345
  44.6 8.0 %pairs_far.1 = (f32[4,16,512]{2,1,0:T(8,128)S(1)}, bf16[4,16,512]{2,1,0:T(8,128)(2,1)S(1)}, bf16[4,16,512]{2,1,0:T(8,128)(2,1)S(1)}, bf16[4,16,512]{2,1,0:T(8,128)(2,1)S(1)}) custom-call(s32[776]{0:T(1024)S(1)} %get-tuple-element.23.keys_ref, bf16[336,512]{1,0:T(8,128)(2,1)S(1)} %collective-permute-done.4.refs_0_, ...), custom_call_target="tpu_custom_call" | custom-call | flops 1677721600 | bytes 2752512 | tf_op jit(solution)/shard_map/pairs_far/pallas_call | solution.py:266
  52.7 4.0 %collective-permute-start.14 = (bf16[4,16,512]{2,1,0:T(8,128)(2,1)S(1)}, bf16[4,16,512]{2,1,0:T(8,128)(2,1)S(1)}, u32[]{:S(2)}, u32[]{:S(2)}) collective-permute-start(bf16[4,16,512]{2,1,0:T(8,128)(2,1)S(1)} %get-tuple-element.28), channel_id=1, source_target_pairs={{0,3},{1,0},{2,1},{3,2},{4,7},{5,4},{6,5},{7,6},{8,11},{9,8},{10,9... | collective-permute-start | bytes 196616 | tf_op jit(solution)/shard_map/ppermute | solution.py:34
  56.7 0.0 collective-permute-start.15
  56.7 1.6 %collective-permute-start.16 = (bf16[4,16,512]{2,1,0:T(8,128)(2,1)S(1)}, bf16[4,16,512]{2,1,0:T(8,128)(2,1)S(1)}, u32[]{:S(2)}, u32[]{:S(2)}) collective-permute-start(bf16[4,16,512]{2,1,0:T(8,128)(2,1)S(1)} %get-tuple-element.30), channel_id=1, source_target_pairs={{0,2},{1,3},{2,0},{3,1},{4,6},{5,7},{6,4},{7,5},{8,10},{9,11},{10,... | collective-permute-start | bytes 196616 | tf_op jit(solution)/shard_map/ppermute | solution.py:34
  58.2 0.4 collective-permute-done.14
  58.6 4.3 %collective-permute-done.15 = bf16[4,16,512]{2,1,0:T(8,128)(2,1)S(1)} collective-permute-done((bf16[4,16,512]{2,1,0:T(8,128)(2,1)S(1)}, bf16[4,16,512]{2,1,0:T(8,128)(2,1)S(1)}, u32[]{:S(2)}, u32[]{:S(2)}) %collective-permute-start.15) | collective-permute-done | bytes 65568 | tf_op jit(solution)/shard_map/ppermute | solution.py:34
  62.9 0.0 collective-permute-done.16
  62.9 0.7 %convert_add_fusion = f32[4,16,512]{2,1,0:T(8,128)} fusion(bf16[4,16,512]{2,1,0:T(8,128)(2,1)S(1)} %collective-permute-done.16, bf16[4,16,512]{2,1,0:T(8,128)(2,1)S(1)} %collective-permute-done.15, f32[4,16,512]{2,1,0:T(8,128)S(1)} %get-tuple-element.27, bf16[4,16,512]{2,1,0:T(8,128)(2,1)S(1)} %collective-permute-done.14), kind=kLoop, calls=%fused_computation | loop fusion | flops 196608 | bytes 458752 | tf_op jit(solution)/shard_map/add | solution.py:386
Async XLA Ops:
  1.1 25.1 %collective-permute-start = (bf16[336,512]{1,0:T(8,128)(2,1)S(1)}, bf16[336,512]{1,0:T(8,128)(2,1)S(1)}, u32[]{:S(2)}, u32[]{:S(2)}) collective-permute-start(bf16[336,512]{1,0:T(8,128)(2,1)S(1)} %get-tuple-element.18.refs_0_), channel_id=1, source_target_pairs={{0,8},{1,9},{2,10},{3,11},{4,12},{5,13},{6,14},{7,15},{8,0},{9,1},... | collective-permute-start | bytes 1032200 | tf_op jit(solution)/shard_map/ppermute | solution.py:34
  3.2 8.3 %collective-permute-start.1 = (bf16[272,512]{1,0:T(8,128)(2,1)S(1)}, bf16[272,512]{1,0:T(8,128)(2,1)S(1)}, u32[]{:S(2)}, u32[]{:S(2)}) collective-permute-start(bf16[272,512]{1,0:T(8,128)(2,1)S(1)} %get-tuple-element.19.refs_0_), channel_id=1, source_target_pairs={{0,1},{1,2},{2,3},{3,0},{4,5},{5,6},{6,7},{7,4},{8,9},{9,10},{10,1... | collective-permute-start | bytes 835592 | tf_op jit(solution)/shard_map/ppermute | solution.py:34
  3.2 14.6 %collective-permute-start.2 = (bf16[272,512]{1,0:T(8,128)(2,1)S(1)}, bf16[272,512]{1,0:T(8,128)(2,1)S(1)}, u32[]{:S(2)}, u32[]{:S(2)}) collective-permute-start(bf16[272,512]{1,0:T(8,128)(2,1)S(1)} %get-tuple-element.19.refs_0_), channel_id=1, source_target_pairs={{0,2},{1,3},{2,0},{3,1},{4,6},{5,7},{6,4},{7,5},{8,10},{9,11},{10,... | collective-permute-start | bytes 835592 | tf_op jit(solution)/shard_map/ppermute | solution.py:34
  5.7 16.3 %collective-permute-start.3 = (bf16[272,512]{1,0:T(8,128)(2,1)S(1)}, bf16[272,512]{1,0:T(8,128)(2,1)S(1)}, u32[]{:S(2)}, u32[]{:S(2)}) collective-permute-start(bf16[272,512]{1,0:T(8,128)(2,1)S(1)} %get-tuple-element.19.refs_0_), channel_id=1, source_target_pairs={{0,3},{1,0},{2,1},{3,2},{4,7},{5,4},{6,5},{7,6},{8,11},{9,8},{10,9... | collective-permute-start | bytes 835592 | tf_op jit(solution)/shard_map/ppermute | solution.py:34
  7.2 22.2 %collective-permute-start.5 = (bf16[336,512]{1,0:T(8,128)(2,1)S(1)}, bf16[336,512]{1,0:T(8,128)(2,1)S(1)}, u32[]{:S(2)}, u32[]{:S(2)}) collective-permute-start(bf16[336,512]{1,0:T(8,128)(2,1)S(1)} %get-tuple-element.18.refs_0_), channel_id=1, source_target_pairs={{0,4},{1,5},{2,6},{3,7},{4,8},{5,9},{6,10},{7,11},{8,12},{9,13},{1... | collective-permute-start | bytes 1032200 | tf_op jit(solution)/shard_map/ppermute | solution.py:34
  11.5 17.9 %collective-permute-start.7 = (bf16[336,512]{1,0:T(8,128)(2,1)S(1)}, bf16[336,512]{1,0:T(8,128)(2,1)S(1)}, u32[]{:S(2)}, u32[]{:S(2)}) collective-permute-start(bf16[336,512]{1,0:T(8,128)(2,1)S(1)} %get-tuple-element.18.refs_0_), channel_id=1, source_target_pairs={{0,12},{1,13},{2,14},{3,15},{4,0},{5,1},{6,2},{7,3},{8,4},{9,5},{1... | collective-permute-start | bytes 1032200 | tf_op jit(solution)/shard_map/ppermute | solution.py:34
  17.8 14.5 %collective-permute-start.10 = (bf16[336,512]{1,0:T(8,128)(2,1)S(1)}, bf16[336,512]{1,0:T(8,128)(2,1)S(1)}, u32[]{:S(2)}, u32[]{:S(2)}) collective-permute-start(bf16[336,512]{1,0:T(8,128)(2,1)S(1)} %get-tuple-element.18.refs_0_), channel_id=1, source_target_pairs={{16,0},{32,16},{48,32},{64,48},{80,64},{96,80},{112,96},{128,112},... | collective-permute-start | bytes 1032200 | tf_op jit(solution)/shard_map/ppermute | solution.py:342
  22.0 10.3 %collective-permute-start.4 = (bf16[336,512]{1,0:T(8,128)(2,1)S(1)}, bf16[336,512]{1,0:T(8,128)(2,1)S(1)}, u32[]{:S(2)}, u32[]{:S(2)}) collective-permute-start(bf16[336,512]{1,0:T(8,128)(2,1)S(1)} %get-tuple-element.18.refs_0_), channel_id=1, source_target_pairs={{0,16},{16,32},{32,48},{48,64},{64,80},{80,96},{96,112},{112,128},... | collective-permute-start | bytes 1032200 | tf_op jit(solution)/shard_map/ppermute | solution.py:342
  26.2 9.1 %collective-permute-start.13 = (bf16[336,512]{1,0:T(8,128)(2,1)S(1)}, bf16[336,512]{1,0:T(8,128)(2,1)S(1)}, u32[]{:S(2)}, u32[]{:S(2)}) collective-permute-start(bf16[336,512]{1,0:T(8,128)(2,1)S(1)} %collective-permute-done.refs_2_), channel_id=1, source_target_pairs={{16,0},{32,16},{48,32},{64,48},{80,64},{96,80},{112,96},{128,112},... | collective-permute-start | bytes 1032200 | tf_op jit(solution)/shard_map/ppermute | solution.py:371
  29.4 13.9 %collective-permute-start.9 = (bf16[336,512]{1,0:T(8,128)(2,1)S(1)}, bf16[336,512]{1,0:T(8,128)(2,1)S(1)}, u32[]{:S(2)}, u32[]{:S(2)}) collective-permute-start(bf16[336,512]{1,0:T(8,128)(2,1)S(1)} %collective-permute-done.refs_2_), channel_id=1, source_target_pairs={{0,16},{16,32},{32,48},{48,64},{64,80},{80,96},{96,112},{112,128},... | collective-permute-start | bytes 1032200 | tf_op jit(solution)/shard_map/ppermute | solution.py:371
  29.4 13.9 %collective-permute-start.11 = (bf16[336,512]{1,0:T(8,128)(2,1)S(1)}, bf16[336,512]{1,0:T(8,128)(2,1)S(1)}, u32[]{:S(2)}, u32[]{:S(2)}) collective-permute-start(bf16[336,512]{1,0:T(8,128)(2,1)S(1)} %collective-permute-done.5.refs_1_), channel_id=1, source_target_pairs={{16,0},{32,16},{48,32},{64,48},{80,64},{96,80},{112,96},{128,112},... | collective-permute-start | bytes 1032200 | tf_op jit(solution)/shard_map/ppermute | solution.py:345
  32.3 11.0 %collective-permute-start.6 = (bf16[336,512]{1,0:T(8,128)(2,1)S(1)}, bf16[336,512]{1,0:T(8,128)(2,1)S(1)}, u32[]{:S(2)}, u32[]{:S(2)}) collective-permute-start(bf16[336,512]{1,0:T(8,128)(2,1)S(1)} %collective-permute-done.5.refs_1_), channel_id=1, source_target_pairs={{0,16},{16,32},{32,48},{48,64},{64,80},{80,96},{96,112},{112,128},... | collective-permute-start | bytes 1032200 | tf_op jit(solution)/shard_map/ppermute | solution.py:345
  32.3 11.0 %collective-permute-start.12 = (bf16[336,512]{1,0:T(8,128)(2,1)S(1)}, bf16[336,512]{1,0:T(8,128)(2,1)S(1)}, u32[]{:S(2)}, u32[]{:S(2)}) collective-permute-start(bf16[336,512]{1,0:T(8,128)(2,1)S(1)} %collective-permute-done.7.refs_3_), channel_id=1, source_target_pairs={{16,0},{32,16},{48,32},{64,48},{80,64},{96,80},{112,96},{128,112},... | collective-permute-start | bytes 1032200 | tf_op jit(solution)/shard_map/ppermute | solution.py:345
  35.3 9.3 %collective-permute-start.8 = (bf16[336,512]{1,0:T(8,128)(2,1)S(1)}, bf16[336,512]{1,0:T(8,128)(2,1)S(1)}, u32[]{:S(2)}, u32[]{:S(2)}) collective-permute-start(bf16[336,512]{1,0:T(8,128)(2,1)S(1)} %collective-permute-done.7.refs_3_), channel_id=1, source_target_pairs={{0,16},{16,32},{32,48},{48,64},{64,80},{80,96},{96,112},{112,128},... | collective-permute-start | bytes 1032200 | tf_op jit(solution)/shard_map/ppermute | solution.py:345
  52.7 5.9 %collective-permute-start.14 = (bf16[4,16,512]{2,1,0:T(8,128)(2,1)S(1)}, bf16[4,16,512]{2,1,0:T(8,128)(2,1)S(1)}, u32[]{:S(2)}, u32[]{:S(2)}) collective-permute-start(bf16[4,16,512]{2,1,0:T(8,128)(2,1)S(1)} %get-tuple-element.28), channel_id=1, source_target_pairs={{0,3},{1,0},{2,1},{3,2},{4,7},{5,4},{6,5},{7,6},{8,11},{9,8},{10,9... | collective-permute-start | bytes 196616 | tf_op jit(solution)/shard_map/ppermute | solution.py:34
  56.7 6.2 %collective-permute-start.15 = (bf16[4,16,512]{2,1,0:T(8,128)(2,1)S(1)}, bf16[4,16,512]{2,1,0:T(8,128)(2,1)S(1)}, u32[]{:S(2)}, u32[]{:S(2)}) collective-permute-start(bf16[4,16,512]{2,1,0:T(8,128)(2,1)S(1)} %get-tuple-element.29), channel_id=1, source_target_pairs={{0,1},{1,2},{2,3},{3,0},{4,5},{5,6},{6,7},{7,4},{8,9},{9,10},{10,1... | collective-permute-start | bytes 196616 | tf_op jit(solution)/shard_map/ppermute | solution.py:34
  56.7 6.2 %collective-permute-start.16 = (bf16[4,16,512]{2,1,0:T(8,128)(2,1)S(1)}, bf16[4,16,512]{2,1,0:T(8,128)(2,1)S(1)}, u32[]{:S(2)}, u32[]{:S(2)}) collective-permute-start(bf16[4,16,512]{2,1,0:T(8,128)(2,1)S(1)} %get-tuple-element.30), channel_id=1, source_target_pairs={{0,2},{1,3},{2,0},{3,1},{4,6},{5,7},{6,4},{7,5},{8,10},{9,11},{10,... | collective-permute-start | bytes 196616 | tf_op jit(solution)/shard_map/ppermute | solution.py:34

commit v5 on v4

--- a/solution.py
+++ b/solution.py
@@ -47,7 +47,18 @@
 
 
 def pack_kernel(
-    first_ref, counts_hbm, points, weights, lists, s_out, t_out, tile, near, counts, sems
+    first_ref,
+    counts_hbm,
+    points,
+    weights,
+    lists,
+    s_out,
+    t_out,
+    l_out,
+    tile,
+    near,
+    counts,
+    sems,
 ):
     dims = points.shape[1]
     vectors = weights.shape[1]
@@ -80,18 +91,16 @@
     tile[LISTS : LISTS + 3] = jnp.ones((3, tile.shape[1]), jnp.float32)
     tile[LISTS + 3 :] = jnp.zeros((1, tile.shape[1]), jnp.float32)
     s_out[top : top + TILE] = tile[...].astype(jnp.bfloat16)
-    tile[LISTS:] = jnp.zeros((LOCAL, tile.shape[1]), jnp.float32)
+    t_out[top:] = tile[...].astype(jnp.bfloat16)
+    l_out[...] = jnp.zeros_like(l_out)
     copies[2 * LOCAL].wait()
     copies[2 * LOCAL + 1].wait()
     slot = lax.broadcasted_iota(jnp.int32, (1, slots), 1)
     for i in range(LOCAL):
         size = counts[i]
         place = jnp.where(slot < size, near[i : i + 1] - first_ref[0], UNUSED)
-        tile[LISTS + i : LISTS + i + 1, :slots] = place.astype(jnp.float32)
-        tile[LISTS + i : LISTS + i + 1, slots : slots + 1] = jnp.full(
-            (1, 1), size, jnp.int32
-        ).astype(jnp.float32)
-    t_out[top:] = tile[...].astype(jnp.bfloat16)
+        l_out[i : i + 1, :slots] = place
+        l_out[i : i + 1, slots : slots + 1] = jnp.full((1, 1), size, jnp.int32)
     for copy in copies[LOCAL : 2 * LOCAL]:
         copy.wait()
 
@@ -102,16 +111,11 @@
     out[rows:] = b[...]
 
 
-def target_kernel(slots, me_ref, *refs):
+def list_kernel(slots, me_ref, *refs):
     blocks, refs = refs[:SIDE], refs[SIDE:]
-    tgt, own_ref, far_ref, tile, norm, keys, keys_s, sem = refs
-    dims = tgt.shape[1] - TILE
-    top = LOCAL * dims
-    norm[...] = jnp.full(norm.shape, -0.5, jnp.float32)
-    norm[LISTS + 3 :] = jnp.zeros((1, norm.shape[1]), jnp.float32)
+    own_ref, far_ref, keys, keys_s, sem = refs
     for b, ref in enumerate(blocks):
-        tile[...] = ref[top:].astype(jnp.float32)
-        keys[b * LOCAL : (b + 1) * LOCAL] = tile[LISTS:, :128].astype(jnp.int32)
+        keys[b * LOCAL : (b + 1) * LOCAL] = ref[...]
     s = keys[...]
     g, h, i = s >> 6, (s >> 2) & 15, s & 3
     used = s < UNUSED
@@ -125,12 +129,6 @@
     keys[...] = jnp.where(lane == slots, s, key)
     copy = pltpu.make_async_copy(keys, keys_s, sem)
     copy.start()
-    for b, ref in enumerate(blocks):
-        tile[...] = ref[top:].astype(jnp.float32)
-        for j in range(LOCAL):
-            tgt[b * LOCAL + j, :dims] = ref[j * dims : (j + 1) * dims]
-            norm[LISTS : LISTS + 3] = -0.5 * tile[3 * j : 3 * j + 3]
-            tgt[b * LOCAL + j, dims:] = norm[...].astype(jnp.bfloat16)
     copy.wait()
 
     def per_target(t, carry):
@@ -155,6 +153,20 @@
     for u in range(1, TAIL + 3):
         own_ref[own + u] = jnp.int32(targets << 16)
         far_ref[far + u] = jnp.int32(targets << 16)
+
+
+def target_kernel(*refs):
+    blocks, (tgt, tile, norm) = refs[:SIDE], refs[SIDE:]
+    dims = tgt.shape[1] - TILE
+    top = LOCAL * dims
+    norm[...] = jnp.full(norm.shape, -0.5, jnp.float32)
+    norm[LISTS + 3 :] = jnp.zeros((1, norm.shape[1]), jnp.float32)
+    for b, ref in enumerate(blocks):
+        tile[...] = ref[top:].astype(jnp.float32)
+        for j in range(LOCAL):
+            tgt[b * LOCAL + j, :dims] = ref[j * dims : (j + 1) * dims]
+            norm[LISTS : LISTS + 3] = -0.5 * tile[3 * j : 3 * j + 3]
+            tgt[b * LOCAL + j, dims:] = norm[...].astype(jnp.bfloat16)
 
 
 def pair_kernel(places, last, keys_ref, *refs):
@@ -298,14 +310,15 @@
     down = [(j, i) for i, j in up]
 
     rows = local * (dims + vectors) + TILE
-    source, target = pl.pallas_call(
+    source, target, listed = pl.pallas_call(
         pack_kernel,
         out_shape=(
             jax.ShapeDtypeStruct((rows, width), jnp.bfloat16),
             jax.ShapeDtypeStruct((local * dims + TILE, width), jnp.bfloat16),
+            jax.ShapeDtypeStruct((local, 128), jnp.int32),
         ),
         in_specs=[SMEM] + [HBM] * 4,
-        out_specs=(VMEM, VMEM),
+        out_specs=(VMEM, VMEM, VMEM),
         scratch_shapes=[
             pltpu.VMEM((TILE, width), jnp.float32),
             pltpu.VMEM((local, slots), jnp.int32),
@@ -326,6 +339,9 @@
     row = {0: target}
     for d in order:
         row[d] = moved(target, d, 1)
+    lists = {0: listed}
+    for d in order:
+        lists[d] = moved(listed, d, 1)
     column = {0: source}
     for d in order:
         column[d] = moved(source, d, 0)
@@ -346,26 +362,37 @@
 
     room = SIDE * local * slots + 8
     me = jnp.stack([helper // SIDE, helper % SIDE]).astype(jnp.int32)
-    make_targets = pl.pallas_call(
-        functools.partial(target_kernel, slots),
+    make_lists = pl.pallas_call(
+        functools.partial(list_kernel, slots),
         out_shape=(
-            jax.ShapeDtypeStruct((SIDE * local, dims + TILE, width), jnp.bfloat16),
             jax.ShapeDtypeStruct((room,), jnp.int32),
             jax.ShapeDtypeStruct((room,), jnp.int32),
         ),
         in_specs=[SMEM] + [VMEM] * SIDE,
-        out_specs=(VMEM, SMEM, SMEM),
+        out_specs=(SMEM, SMEM),
         scratch_shapes=[
-            pltpu.VMEM((TILE, width), jnp.float32),
-            pltpu.VMEM((TILE, width), jnp.float32),
             pltpu.VMEM((SIDE * local, 128), jnp.int32),
             pltpu.SMEM((SIDE * local, 128), jnp.int32),
             pltpu.SemaphoreType.DMA,
         ],
+        compiler_params=pltpu.CompilerParams(vmem_limit_bytes=4 << 20),
+        name="lists",
+    )
+    own, far = make_lists(me, *[lists[d] for d in range(SIDE)])
+    row[1], own, far = lax.optimization_barrier((row[1], own, far))
+    make_targets = pl.pallas_call(
+        target_kernel,
+        out_shape=jax.ShapeDtypeStruct((SIDE * local, dims + TILE, width), jnp.bfloat16),
+        in_specs=[VMEM] * SIDE,
+        out_specs=VMEM,
+        scratch_shapes=[
+            pltpu.VMEM((TILE, width), jnp.float32),
+            pltpu.VMEM((TILE, width), jnp.float32),
+        ],
         compiler_params=pltpu.CompilerParams(vmem_limit_bytes=8 << 20),
         name="targets",
     )
-    tgt, own, far = make_targets(me, *[row[d] for d in range(SIDE)])
+    tgt = make_targets(*[row[d] for d in range(SIDE)])
     opposite, tgt, own, far = lax.optimization_barrier((column[2], tgt, own, far))
     for ring, side in zip((up, down), sides):
         side.append(lax.ppermute(opposite, "owner", ring))

time: 63.7 us -> 76.9 us (1.21)
  starting transfers between devices: 29.3 us -> 36.1 us
  waiting for transfers between devices: 12.2 us -> 18.3 us
    ppermute x9 -> x12, starting transfers between devices: 16 us -> 25.4 us  [moved(): return lax.ppermute(value, 'helper', pairs)]
    ppermute x9 -> x12, waiting for transfers between devices: 10.8 us -> 16.7 us  [moved(): return lax.ppermute(value, 'helper', pairs)]
    ppermute x2, starting transfers between devices: 4.19 us -> 2.07 us  [potentials(): sides.append([lax.ppermute(source, 'owner', ring)])]
    ppermute x2, waiting for transfers between devices: 0.01 us -> 1.4 us  [potentials(): side.append(lax.ppermute(opposite, 'owner', ring))]
    ppermute x4, waiting for transfers between devices: 1.3 us -> 0.01 us  [potentials(): side.append(lax.ppermute(column[d], 'owner', ring))]
    pallas_call x1 -> x2, Pallas kernels: 4.13 us -> 4.23 us  [the longest x1 4.08 us: potentials(): own, far = make_lists(me, *[lists[d] for d in range(SIDE)])]
  transfers between devices with their start and end apart: 17 -> 20, of which waited for: 5 -> 8; matrix products, arithmetic and copies ran while one was open for 0% -> 0% of each run, Pallas kernels for 19% -> 16%
where the time goes in v5:
time: 76.9 us; the launch traced here: 76.7 us
  starting transfers between devices  36.1 us (47%)
  Pallas kernels  21.3 us (28%)
  waiting for transfers between devices  18.3 us (24%)
    ppermute x12, starting transfers between devices, moved(): return lax.ppermute(value, 'helper', pairs)  25.4 us
    ppermute x12, waiting for transfers between devices, moved(): return lax.ppermute(value, 'helper', pairs)  16.7 us
    pallas_call x2, Pallas kernels, pair_sums(): pl.pallas_call(functools.partial(pair_kernel, places, last), out_shape=ou...  16 us
    ppermute x4, starting transfers between devices, potentials(): side.append(lax.ppermute(column[d], 'owner', ring))  5.25 us
    pallas_call x1, Pallas kernels, potentials(): own, far = make_lists(me, *[lists[d] for d in range(SIDE)])  4.08 us
    ppermute x2, starting transfers between devices, potentials(): side.append(lax.ppermute(opposite, 'owner', ring))  3.45 us
    ppermute x2, starting transfers between devices, potentials(): sides.append([lax.ppermute(source, 'owner', ring)])  2.07 us
  transfers between devices with their start and end apart: 20, of which 8 were waited for; matrix products, arithmetic and copies ran while one was open for 0% of the time, Pallas kernels for 16%

profile of v5, /device:TPU:16, one launch (start us, length us, event | category | flops | bytes accessed | tf_op | source)
XLA Modules:
  0.0 76.7 jit_solution(2645201199179788676)
XLA Ops:
  0.0 1.1 %pack.1 = (bf16[336,512]{1,0:T(8,128)(2,1)S(1)}, bf16[272,512]{1,0:T(8,128)(2,1)S(1)}, s32[4,128]{1,0:T(4,128)S(1)}) custom-call(s32[1]{0:T(128)} %bitcast.first_ref, s32[4]{0:T(128)} %counts_hbm.1, bf16[4,64,512]{2,1,0:T(8,128)(2,1)} %points.1, bf16[4,16,512]{2,1,0:T(8,128)(2,1)} %weights.1, s32[4,48]{1,0:T(4,128)} %lists.2), custom_call_target="tpu_custom_call" | custom-call | tf_op jit(solution)/shard_map/pack/pallas_call | solution.py:313
  1.1 2.1 %collective-permute-start = (bf16[336,512]{1,0:T(8,128)(2,1)S(1)}, bf16[336,512]{1,0:T(8,128)(2,1)S(1)}, u32[]{:S(2)}, u32[]{:S(2)}) collective-permute-start(bf16[336,512]{1,0:T(8,128)(2,1)S(1)} %get-tuple-element.21.refs_0_), channel_id=1, source_target_pairs={{0,8},{1,9},{2,10},{3,11},{4,12},{5,13},{6,14},{7,15},{8,0},{9,1},... | collective-permute-start | bytes 1032200 | tf_op jit(solution)/shard_map/ppermute | solution.py:34
  3.2 0.0 collective-permute-start.1
  3.2 2.5 %collective-permute-start.5 = (bf16[272,512]{1,0:T(8,128)(2,1)S(1)}, bf16[272,512]{1,0:T(8,128)(2,1)S(1)}, u32[]{:S(2)}, u32[]{:S(2)}) collective-permute-start(bf16[272,512]{1,0:T(8,128)(2,1)S(1)} %get-tuple-element.22.refs_0_), channel_id=1, source_target_pairs={{0,2},{1,3},{2,0},{3,1},{4,6},{5,7},{6,4},{7,5},{8,10},{9,11},{10,... | collective-permute-start | bytes 835592 | tf_op jit(solution)/shard_map/ppermute | solution.py:34
  5.7 1.4 %collective-permute-start.6 = (bf16[272,512]{1,0:T(8,128)(2,1)S(1)}, bf16[272,512]{1,0:T(8,128)(2,1)S(1)}, u32[]{:S(2)}, u32[]{:S(2)}) collective-permute-start(bf16[272,512]{1,0:T(8,128)(2,1)S(1)} %get-tuple-element.22.refs_0_), channel_id=1, source_target_pairs={{0,3},{1,0},{2,1},{3,2},{4,7},{5,4},{6,5},{7,6},{8,11},{9,8},{10,9... | collective-permute-start | bytes 835592 | tf_op jit(solution)/shard_map/ppermute | solution.py:34
  7.2 0.6 collective-permute-start.2
  7.8 6.9 %collective-permute-done.2.refs_1_ = s32[4,128]{1,0:T(4,128)S(1)} collective-permute-done((s32[4,128]{1,0:T(4,128)S(1)}, s32[4,128]{1,0:T(4,128)S(1)}, u32[]{:S(2)}, u32[]{:S(2)}) %collective-permute-start.2) | collective-permute-done | bytes 2080 | tf_op jit(solution)/shard_map/ppermute | solution.py:34
  14.7 2.7 %collective-permute-start.3 = (s32[4,128]{1,0:T(4,128)S(1)}, s32[4,128]{1,0:T(4,128)S(1)}, u32[]{:S(2)}, u32[]{:S(2)}) collective-permute-start(s32[4,128]{1,0:T(4,128)S(1)} %get-tuple-element.23.refs_0_), channel_id=1, source_target_pairs={{0,2},{1,3},{2,0},{3,1},{4,6},{5,7},{6,4},{7,5},{8,10},{9,11},{10,... | collective-permute-start | bytes 6152 | tf_op jit(solution)/shard_map/ppermute | solution.py:34
  17.4 2.4 %collective-permute-done.3.refs_2_ = s32[4,128]{1,0:T(4,128)S(1)} collective-permute-done((s32[4,128]{1,0:T(4,128)S(1)}, s32[4,128]{1,0:T(4,128)S(1)}, u32[]{:S(2)}, u32[]{:S(2)}) %collective-permute-start.3) | collective-permute-done | bytes 2080 | tf_op jit(solution)/shard_map/ppermute | solution.py:34
  19.8 3.8 %collective-permute-start.4 = (s32[4,128]{1,0:T(4,128)S(1)}, s32[4,128]{1,0:T(4,128)S(1)}, u32[]{:S(2)}, u32[]{:S(2)}) collective-permute-start(s32[4,128]{1,0:T(4,128)S(1)} %get-tuple-element.23.refs_0_), channel_id=1, source_target_pairs={{0,3},{1,0},{2,1},{3,2},{4,7},{5,4},{6,5},{7,6},{8,11},{9,8},{10,9... | collective-permute-start | bytes 6152 | tf_op jit(solution)/shard_map/ppermute | solution.py:34
  23.5 0.1 pad_add_fusion.me_ref
  23.6 1.2 %collective-permute-done.4.refs_3_ = s32[4,128]{1,0:T(4,128)S(1)} collective-permute-done((s32[4,128]{1,0:T(4,128)S(1)}, s32[4,128]{1,0:T(4,128)S(1)}, u32[]{:S(2)}, u32[]{:S(2)}) %collective-permute-start.4) | collective-permute-done | bytes 2080 | tf_op jit(solution)/shard_map/ppermute | solution.py:34
  24.9 2.4 %collective-permute-start.10 = (bf16[336,512]{1,0:T(8,128)(2,1)S(1)}, bf16[336,512]{1,0:T(8,128)(2,1)S(1)}, u32[]{:S(2)}, u32[]{:S(2)}) collective-permute-start(bf16[336,512]{1,0:T(8,128)(2,1)S(1)} %get-tuple-element.21.refs_0_), channel_id=1, source_target_pairs={{0,12},{1,13},{2,14},{3,15},{4,0},{5,1},{6,2},{7,3},{8,4},{9,5},{1... | collective-permute-start | bytes 1032200 | tf_op jit(solution)/shard_map/ppermute | solution.py:34
  27.2 4.1 %lists.3 = (s32[776]{0:T(1024)S(1)}, s32[776]{0:T(1024)S(1)}) custom-call(s32[2]{0:T(128)S(1)} %pad_add_fusion.me_ref, s32[4,128]{1,0:T(4,128)S(1)} %get-tuple-element.23.refs_0_, s32[4,128]{1,0:T(4,128)S(1)} %collective-permute-done.2.refs_1_, s32[4,128]{1,0:T(4,128)S(1)} %collective-permute-done.3.refs_2_, s32[4,128]{1,0:T(4,128)S(1)} %collective-permute-done.4.refs_3_), custom_call_target="tpu_custom_call" | custom-call | tf_op jit(solution)/shard_map/lists/pallas_call | solution.py:381
  31.3 0.0 collective-permute-done.1.refs_1_
  31.3 0.1 collective-permute-start.8
  31.4 0.0 collective-permute-done.5.refs_2_
  31.4 2.1 %collective-permute-start.13 = (bf16[336,512]{1,0:T(8,128)(2,1)S(1)}, bf16[336,512]{1,0:T(8,128)(2,1)S(1)}, u32[]{:S(2)}, u32[]{:S(2)}) collective-permute-start(bf16[336,512]{1,0:T(8,128)(2,1)S(1)} %get-tuple-element.21.refs_0_), channel_id=1, source_target_pairs={{16,0},{32,16},{48,32},{64,48},{80,64},{96,80},{112,96},{128,112},... | collective-permute-start | bytes 1032200 | tf_op jit(solution)/shard_map/ppermute | solution.py:358
  33.5 0.0 collective-permute-done.6.refs_3_
  33.5 0.0 collective-permute-start.7
  33.5 0.2 targets.1.refs_4_.refs_8_
  33.7 0.0 collective-permute-done.refs_2_
  33.7 0.0 collective-permute-start.12
  33.7 0.0 collective-permute-done.10.refs_3_
  33.7 3.4 %collective-permute-start.16 = (bf16[336,512]{1,0:T(8,128)(2,1)S(1)}, bf16[336,512]{1,0:T(8,128)(2,1)S(1)}, u32[]{:S(2)}, u32[]{:S(2)}) collective-permute-start(bf16[336,512]{1,0:T(8,128)(2,1)S(1)} %collective-permute-done.refs_2_), channel_id=1, source_target_pairs={{16,0},{32,16},{48,32},{64,48},{80,64},{96,80},{112,96},{128,112},... | collective-permute-start | bytes 1032200 | tf_op jit(solution)/shard_map/ppermute | solution.py:398
  37.1 1.5 %collective-permute-done.8.refs_1_ = bf16[336,512]{1,0:T(8,128)(2,1)S(1)} collective-permute-done((bf16[336,512]{1,0:T(8,128)(2,1)S(1)}, bf16[336,512]{1,0:T(8,128)(2,1)S(1)}, u32[]{:S(2)}, u32[]{:S(2)}) %collective-permute-start.8) | collective-permute-done | bytes 344096 | tf_op jit(solution)/shard_map/ppermute | solution.py:34
  38.7 0.0 collective-permute-start.11
  38.7 0.0 collective-permute-done.13.refs_4_
  38.7 3.0 %collective-permute-start.15 = (bf16[336,512]{1,0:T(8,128)(2,1)S(1)}, bf16[336,512]{1,0:T(8,128)(2,1)S(1)}, u32[]{:S(2)}, u32[]{:S(2)}) collective-permute-start(bf16[336,512]{1,0:T(8,128)(2,1)S(1)} %collective-permute-done.10.refs_3_), channel_id=1, source_target_pairs={{16,0},{32,16},{48,32},{64,48},{80,64},{96,80},{112,96},{128,112},... | collective-permute-start | bytes 1032200 | tf_op jit(solution)/shard_map/ppermute | solution.py:361
  41.6 0.2 collective-permute-done.7.refs_0_
  41.9 2.3 %collective-permute-start.14 = (bf16[336,512]{1,0:T(8,128)(2,1)S(1)}, bf16[336,512]{1,0:T(8,128)(2,1)S(1)}, u32[]{:S(2)}, u32[]{:S(2)}) collective-permute-start(bf16[336,512]{1,0:T(8,128)(2,1)S(1)} %collective-permute-done.8.refs_1_), channel_id=1, source_target_pairs={{16,0},{32,16},{48,32},{64,48},{80,64},{96,80},{112,96},{128,112},... | collective-permute-start | bytes 1032200 | tf_op jit(solution)/shard_map/ppermute | solution.py:361
  44.1 1.4 %collective-permute-done.12.refs_3_ = bf16[336,512]{1,0:T(8,128)(2,1)S(1)} collective-permute-done((bf16[336,512]{1,0:T(8,128)(2,1)S(1)}, bf16[336,512]{1,0:T(8,128)(2,1)S(1)}, u32[]{:S(2)}, u32[]{:S(2)}) %collective-permute-start.12) | collective-permute-done | bytes 344096 | tf_op jit(solution)/shard_map/ppermute | solution.py:398
  45.5 0.0 collective-permute-start.9
  45.5 8.0 %pairs_own.1.refs_9_ = f32[16,16,512]{2,1,0:T(8,128)S(1)} custom-call(s32[776]{0:T(1024)S(1)} %get-tuple-element.32.keys_ref, bf16[336,512]{1,0:T(8,128)(2,1)S(1)} %get-tuple-element.21.refs_0_, bf16[336,512]{1,0:T(8,128)(2,1)S(1)} %collective-permute-done.8.refs_1_, bf16[336,512]{1,0:T(8,128)(2,1)S(1)} %collective-permute-done.refs_2_, ...), custom_call_target="tpu_custom_call" | custom-call | flops 1677721600 | bytes 1376256 | tf_op jit(solution)/shard_map/pairs_own/pallas_call | solution.py:278
  53.5 0.0 collective-permute-done.16.refs_7_
  53.6 0.0 collective-permute-done.11.refs_2_
  53.6 0.0 collective-permute-done.14.refs_5_
  53.6 0.0 collective-permute-done.15.refs_6_
  53.6 0.0 collective-permute-done.9.refs_1_
  53.6 8.0 %pairs_far.1 = (f32[4,16,512]{2,1,0:T(8,128)S(1)}, bf16[4,16,512]{2,1,0:T(8,128)(2,1)S(1)}, bf16[4,16,512]{2,1,0:T(8,128)(2,1)S(1)}, bf16[4,16,512]{2,1,0:T(8,128)(2,1)S(1)}) custom-call(s32[776]{0:T(1024)S(1)} %get-tuple-element.29.keys_ref, bf16[336,512]{1,0:T(8,128)(2,1)S(1)} %collective-permute-done.7.refs_0_, ...), custom_call_target="tpu_custom_call" | custom-call | flops 1677721600 | bytes 2752512 | tf_op jit(solution)/shard_map/pairs_far/pallas_call | solution.py:278
  61.6 8.2 %collective-permute-start.17 = (bf16[4,16,512]{2,1,0:T(8,128)(2,1)S(1)}, bf16[4,16,512]{2,1,0:T(8,128)(2,1)S(1)}, u32[]{:S(2)}, u32[]{:S(2)}) collective-permute-start(bf16[4,16,512]{2,1,0:T(8,128)(2,1)S(1)} %get-tuple-element.34), channel_id=1, source_target_pairs={{0,3},{1,0},{2,1},{3,2},{4,7},{5,4},{6,5},{7,6},{8,11},{9,8},{10,9... | collective-permute-start | bytes 196616 | tf_op jit(solution)/shard_map/ppermute | solution.py:34
  69.8 0.0 collective-permute-start.18
  69.8 1.6 %collective-permute-start.19 = (bf16[4,16,512]{2,1,0:T(8,128)(2,1)S(1)}, bf16[4,16,512]{2,1,0:T(8,128)(2,1)S(1)}, u32[]{:S(2)}, u32[]{:S(2)}) collective-permute-start(bf16[4,16,512]{2,1,0:T(8,128)(2,1)S(1)} %get-tuple-element.36), channel_id=1, source_target_pairs={{0,2},{1,3},{2,0},{3,1},{4,6},{5,7},{6,4},{7,5},{8,10},{9,11},{10,... | collective-permute-start | bytes 196616 | tf_op jit(solution)/shard_map/ppermute | solution.py:34
  71.4 0.4 collective-permute-done.17
  71.7 4.3 %collective-permute-done.18 = bf16[4,16,512]{2,1,0:T(8,128)(2,1)S(1)} collective-permute-done((bf16[4,16,512]{2,1,0:T(8,128)(2,1)S(1)}, bf16[4,16,512]{2,1,0:T(8,128)(2,1)S(1)}, u32[]{:S(2)}, u32[]{:S(2)}) %collective-permute-start.18) | collective-permute-done | bytes 65568 | tf_op jit(solution)/shard_map/ppermute | solution.py:34
  76.0 0.0 collective-permute-done.19
  76.0 0.7 convert_add_fusion
Async XLA Ops:
  1.1 32.6 %collective-permute-start = (bf16[336,512]{1,0:T(8,128)(2,1)S(1)}, bf16[336,512]{1,0:T(8,128)(2,1)S(1)}, u32[]{:S(2)}, u32[]{:S(2)}) collective-permute-start(bf16[336,512]{1,0:T(8,128)(2,1)S(1)} %get-tuple-element.21.refs_0_), channel_id=1, source_target_pairs={{0,8},{1,9},{2,10},{3,11},{4,12},{5,13},{6,14},{7,15},{8,0},{9,1},... | collective-permute-start | bytes 1032200 | tf_op jit(solution)/shard_map/ppermute | solution.py:34
  3.2 28.1 %collective-permute-start.1 = (bf16[272,512]{1,0:T(8,128)(2,1)S(1)}, bf16[272,512]{1,0:T(8,128)(2,1)S(1)}, u32[]{:S(2)}, u32[]{:S(2)}) collective-permute-start(bf16[272,512]{1,0:T(8,128)(2,1)S(1)} %get-tuple-element.22.refs_0_), channel_id=1, source_target_pairs={{0,1},{1,2},{2,3},{3,0},{4,5},{5,6},{6,7},{7,4},{8,9},{9,10},{10,1... | collective-permute-start | bytes 835592 | tf_op jit(solution)/shard_map/ppermute | solution.py:34
  3.2 28.2 %collective-permute-start.5 = (bf16[272,512]{1,0:T(8,128)(2,1)S(1)}, bf16[272,512]{1,0:T(8,128)(2,1)S(1)}, u32[]{:S(2)}, u32[]{:S(2)}) collective-permute-start(bf16[272,512]{1,0:T(8,128)(2,1)S(1)} %get-tuple-element.22.refs_0_), channel_id=1, source_target_pairs={{0,2},{1,3},{2,0},{3,1},{4,6},{5,7},{6,4},{7,5},{8,10},{9,11},{10,... | collective-permute-start | bytes 835592 | tf_op jit(solution)/shard_map/ppermute | solution.py:34
  5.7 27.8 %collective-permute-start.6 = (bf16[272,512]{1,0:T(8,128)(2,1)S(1)}, bf16[272,512]{1,0:T(8,128)(2,1)S(1)}, u32[]{:S(2)}, u32[]{:S(2)}) collective-permute-start(bf16[272,512]{1,0:T(8,128)(2,1)S(1)} %get-tuple-element.22.refs_0_), channel_id=1, source_target_pairs={{0,3},{1,0},{2,1},{3,2},{4,7},{5,4},{6,5},{7,6},{8,11},{9,8},{10,9... | collective-permute-start | bytes 835592 | tf_op jit(solution)/shard_map/ppermute | solution.py:34
  7.2 7.5 %collective-permute-start.2 = (s32[4,128]{1,0:T(4,128)S(1)}, s32[4,128]{1,0:T(4,128)S(1)}, u32[]{:S(2)}, u32[]{:S(2)}) collective-permute-start(s32[4,128]{1,0:T(4,128)S(1)} %get-tuple-element.23.refs_0_), channel_id=1, source_target_pairs={{0,1},{1,2},{2,3},{3,0},{4,5},{5,6},{6,7},{7,4},{8,9},{9,10},{10,1... | collective-permute-start | bytes 6152 | tf_op jit(solution)/shard_map/ppermute | solution.py:34
  14.7 5.1 %collective-permute-start.3 = (s32[4,128]{1,0:T(4,128)S(1)}, s32[4,128]{1,0:T(4,128)S(1)}, u32[]{:S(2)}, u32[]{:S(2)}) collective-permute-start(s32[4,128]{1,0:T(4,128)S(1)} %get-tuple-element.23.refs_0_), channel_id=1, source_target_pairs={{0,2},{1,3},{2,0},{3,1},{4,6},{5,7},{6,4},{7,5},{8,10},{9,11},{10,... | collective-permute-start | bytes 6152 | tf_op jit(solution)/shard_map/ppermute | solution.py:34
  19.8 5.1 %collective-permute-start.4 = (s32[4,128]{1,0:T(4,128)S(1)}, s32[4,128]{1,0:T(4,128)S(1)}, u32[]{:S(2)}, u32[]{:S(2)}) collective-permute-start(s32[4,128]{1,0:T(4,128)S(1)} %get-tuple-element.23.refs_0_), channel_id=1, source_target_pairs={{0,3},{1,0},{2,1},{3,2},{4,7},{5,4},{6,5},{7,6},{8,11},{9,8},{10,9... | collective-permute-start | bytes 6152 | tf_op jit(solution)/shard_map/ppermute | solution.py:34
  24.9 8.8 %collective-permute-start.10 = (bf16[336,512]{1,0:T(8,128)(2,1)S(1)}, bf16[336,512]{1,0:T(8,128)(2,1)S(1)}, u32[]{:S(2)}, u32[]{:S(2)}) collective-permute-start(bf16[336,512]{1,0:T(8,128)(2,1)S(1)} %get-tuple-element.21.refs_0_), channel_id=1, source_target_pairs={{0,12},{1,13},{2,14},{3,15},{4,0},{5,1},{6,2},{7,3},{8,4},{9,5},{1... | collective-permute-start | bytes 1032200 | tf_op jit(solution)/shard_map/ppermute | solution.py:34
  31.3 7.3 %collective-permute-start.8 = (bf16[336,512]{1,0:T(8,128)(2,1)S(1)}, bf16[336,512]{1,0:T(8,128)(2,1)S(1)}, u32[]{:S(2)}, u32[]{:S(2)}) collective-permute-start(bf16[336,512]{1,0:T(8,128)(2,1)S(1)} %get-tuple-element.21.refs_0_), channel_id=1, source_target_pairs={{0,4},{1,5},{2,6},{3,7},{4,8},{5,9},{6,10},{7,11},{8,12},{9,13},{1... | collective-permute-start | bytes 1032200 | tf_op jit(solution)/shard_map/ppermute | solution.py:34
  31.4 7.2 %collective-permute-start.13 = (bf16[336,512]{1,0:T(8,128)(2,1)S(1)}, bf16[336,512]{1,0:T(8,128)(2,1)S(1)}, u32[]{:S(2)}, u32[]{:S(2)}) collective-permute-start(bf16[336,512]{1,0:T(8,128)(2,1)S(1)} %get-tuple-element.21.refs_0_), channel_id=1, source_target_pairs={{16,0},{32,16},{48,32},{64,48},{80,64},{96,80},{112,96},{128,112},... | collective-permute-start | bytes 1032200 | tf_op jit(solution)/shard_map/ppermute | solution.py:358
  33.5 8.4 %collective-permute-start.7 = (bf16[336,512]{1,0:T(8,128)(2,1)S(1)}, bf16[336,512]{1,0:T(8,128)(2,1)S(1)}, u32[]{:S(2)}, u32[]{:S(2)}) collective-permute-start(bf16[336,512]{1,0:T(8,128)(2,1)S(1)} %get-tuple-element.21.refs_0_), channel_id=1, source_target_pairs={{0,16},{16,32},{32,48},{48,64},{64,80},{80,96},{96,112},{112,128},... | collective-permute-start | bytes 1032200 | tf_op jit(solution)/shard_map/ppermute | solution.py:358
  33.7 11.9 %collective-permute-start.12 = (bf16[336,512]{1,0:T(8,128)(2,1)S(1)}, bf16[336,512]{1,0:T(8,128)(2,1)S(1)}, u32[]{:S(2)}, u32[]{:S(2)}) collective-permute-start(bf16[336,512]{1,0:T(8,128)(2,1)S(1)} %collective-permute-done.refs_2_), channel_id=1, source_target_pairs={{0,16},{16,32},{32,48},{48,64},{64,80},{80,96},{96,112},{112,128},... | collective-permute-start | bytes 1032200 | tf_op jit(solution)/shard_map/ppermute | solution.py:398
  33.7 19.8 %collective-permute-start.16 = (bf16[336,512]{1,0:T(8,128)(2,1)S(1)}, bf16[336,512]{1,0:T(8,128)(2,1)S(1)}, u32[]{:S(2)}, u32[]{:S(2)}) collective-permute-start(bf16[336,512]{1,0:T(8,128)(2,1)S(1)} %collective-permute-done.refs_2_), channel_id=1, source_target_pairs={{16,0},{32,16},{48,32},{64,48},{80,64},{96,80},{112,96},{128,112},... | collective-permute-start | bytes 1032200 | tf_op jit(solution)/shard_map/ppermute | solution.py:398
  38.7 14.9 %collective-permute-start.11 = (bf16[336,512]{1,0:T(8,128)(2,1)S(1)}, bf16[336,512]{1,0:T(8,128)(2,1)S(1)}, u32[]{:S(2)}, u32[]{:S(2)}) collective-permute-start(bf16[336,512]{1,0:T(8,128)(2,1)S(1)} %collective-permute-done.10.refs_3_), channel_id=1, source_target_pairs={{0,16},{16,32},{32,48},{48,64},{64,80},{80,96},{96,112},{112,128},... | collective-permute-start | bytes 1032200 | tf_op jit(solution)/shard_map/ppermute | solution.py:361
  38.7 14.9 %collective-permute-start.15 = (bf16[336,512]{1,0:T(8,128)(2,1)S(1)}, bf16[336,512]{1,0:T(8,128)(2,1)S(1)}, u32[]{:S(2)}, u32[]{:S(2)}) collective-permute-start(bf16[336,512]{1,0:T(8,128)(2,1)S(1)} %collective-permute-done.10.refs_3_), channel_id=1, source_target_pairs={{16,0},{32,16},{48,32},{64,48},{80,64},{96,80},{112,96},{128,112},... | collective-permute-start | bytes 1032200 | tf_op jit(solution)/shard_map/ppermute | solution.py:361
  41.9 11.7 %collective-permute-start.14 = (bf16[336,512]{1,0:T(8,128)(2,1)S(1)}, bf16[336,512]{1,0:T(8,128)(2,1)S(1)}, u32[]{:S(2)}, u32[]{:S(2)}) collective-permute-start(bf16[336,512]{1,0:T(8,128)(2,1)S(1)} %collective-permute-done.8.refs_1_), channel_id=1, source_target_pairs={{16,0},{32,16},{48,32},{64,48},{80,64},{96,80},{112,96},{128,112},... | collective-permute-start | bytes 1032200 | tf_op jit(solution)/shard_map/ppermute | solution.py:361
  45.5 8.0 %collective-permute-start.9 = (bf16[336,512]{1,0:T(8,128)(2,1)S(1)}, bf16[336,512]{1,0:T(8,128)(2,1)S(1)}, u32[]{:S(2)}, u32[]{:S(2)}) collective-permute-start(bf16[336,512]{1,0:T(8,128)(2,1)S(1)} %collective-permute-done.8.refs_1_), channel_id=1, source_target_pairs={{0,16},{16,32},{32,48},{48,64},{64,80},{80,96},{96,112},{112,128},... | collective-permute-start | bytes 1032200 | tf_op jit(solution)/shard_map/ppermute | solution.py:361
  61.6 10.1 %collective-permute-start.17 = (bf16[4,16,512]{2,1,0:T(8,128)(2,1)S(1)}, bf16[4,16,512]{2,1,0:T(8,128)(2,1)S(1)}, u32[]{:S(2)}, u32[]{:S(2)}) collective-permute-start(bf16[4,16,512]{2,1,0:T(8,128)(2,1)S(1)} %get-tuple-element.34), channel_id=1, source_target_pairs={{0,3},{1,0},{2,1},{3,2},{4,7},{5,4},{6,5},{7,6},{8,11},{9,8},{10,9... | collective-permute-start | bytes 196616 | tf_op jit(solution)/shard_map/ppermute | solution.py:34
  69.8 6.2 %collective-permute-start.18 = (bf16[4,16,512]{2,1,0:T(8,128)(2,1)S(1)}, bf16[4,16,512]{2,1,0:T(8,128)(2,1)S(1)}, u32[]{:S(2)}, u32[]{:S(2)}) collective-permute-start(bf16[4,16,512]{2,1,0:T(8,128)(2,1)S(1)} %get-tuple-element.35), channel_id=1, source_target_pairs={{0,1},{1,2},{2,3},{3,0},{4,5},{5,6},{6,7},{7,4},{8,9},{9,10},{10,1... | collective-permute-start | bytes 196616 | tf_op jit(solution)/shard_map/ppermute | solution.py:34
  69.8 6.2 %collective-permute-start.19 = (bf16[4,16,512]{2,1,0:T(8,128)(2,1)S(1)}, bf16[4,16,512]{2,1,0:T(8,128)(2,1)S(1)}, u32[]{:S(2)}, u32[]{:S(2)}) collective-permute-start(bf16[4,16,512]{2,1,0:T(8,128)(2,1)S(1)} %get-tuple-element.36), channel_id=1, source_target_pairs={{0,2},{1,3},{2,0},{3,1},{4,6},{5,7},{6,4},{7,5},{8,10},{9,11},{10,... | collective-permute-start | bytes 196616 | tf_op jit(solution)/shard_map/ppermute | solution.py:34

commit v6 on v4

--- a/solution.py
+++ b/solution.py
@@ -120,7 +120,7 @@
     block = ((me_ref[0] - (h >> 2)) & 3) * LOCAL + i
     slot = jnp.where(used, block + jnp.where(g == 2, SIDE * LOCAL, 0), 0)
     mine = used & ((h & 3) == me_ref[1])
-    kind = jnp.where(mine, jnp.where(g == 1, 0, 1), 2)
+    kind = jnp.where(mine, jnp.where(g == 1, 1, 2), 0)
     key = (kind << 24) | (t << 16) | (t << 8) | slot
     keys[...] = jnp.where(lane == slots, s, key)
     copy = pltpu.make_async_copy(keys, keys_s, sem)
@@ -138,11 +138,10 @@
             own, far = carry
             for u in range(AT_ONCE):
                 key = keys_s[t, AT_ONCE * q + u]
-                kind = key >> 24
-                own_ref[own + 1] = key & 0xFFFFFF
-                far_ref[far + 1] = key & 0xFFFFFF
-                own = own + jnp.where(kind == 0, 1, 0)
-                far = far + jnp.where(kind == 1, 1, 0)
+                own_ref[own + 1] = key
+                far_ref[far + 1] = key
+                own = own + ((key >> 24) & 1)
+                far = far + (key >> 25)
             return own, far
 
         turns = (keys_s[t, slots] + (AT_ONCE - 1)) >> 2
@@ -192,7 +191,7 @@
 
     def picked(p):
         key = keys_ref[p + 1]
-        return key & 255, (key >> 8) & 255, key >> 16
+        return key & 255, (key >> 8) & 255, (key >> 16) & 255
 
     def ahead(p, buffer):
         s, t, _ = picked(p)

time: 63.7 us -> 63.4 us (level)
  no operation moved by 1% of the time
where the time goes in v6:
time: 63.4 us; the launch traced here: 63.2 us
  starting transfers between devices  29.3 us (46%)
  Pallas kernels  20.9 us (33%)
  waiting for transfers between devices  12.2 us (19%)
  other arithmetic  0.76 us (1%)
    ppermute x9, starting transfers between devices, moved(): return lax.ppermute(value, 'helper', pairs)  16 us
    pallas_call x2, Pallas kernels, pair_sums(): pl.pallas_call(functools.partial(pair_kernel, places, last), out_shape=ou...  16 us
    ppermute x9, waiting for transfers between devices, moved(): return lax.ppermute(value, 'helper', pairs)  10.8 us
    ppermute x4, starting transfers between devices, potentials(): side.append(lax.ppermute(column[d], 'owner', ring))  5.91 us
    ppermute x2, starting transfers between devices, potentials(): sides.append([lax.ppermute(source, 'owner', ring)])  4.19 us
    pallas_call x1, Pallas kernels, potentials(): tgt, own, far = make_targets(me, *[row[d] for d in range(SIDE)])  3.82 us
    ppermute x2, starting transfers between devices, potentials(): side.append(lax.ppermute(opposite, 'owner', ring))  3.14 us
    ppermute x4, waiting for transfers between devices, potentials(): side.append(lax.ppermute(column[d], 'owner', ring))  1.32 us
  transfers between devices with their start and end apart: 17, of which 5 were waited for; matrix products, arithmetic and copies ran while one was open for 0% of the time, Pallas kernels for 19%

profile of v6, /device:TPU:16, one launch (start us, length us, event | category | flops | bytes accessed | tf_op | source)
XLA Modules:
  0.0 63.2 jit_solution(7711635375047874003)
XLA Ops:
  0.0 1.1 %pack.1 = (bf16[336,512]{1,0:T(8,128)(2,1)S(1)}, bf16[272,512]{1,0:T(8,128)(2,1)S(1)}) custom-call(s32[1]{0:T(128)} %bitcast.first_ref, s32[4]{0:T(128)} %counts_hbm.1, bf16[4,64,512]{2,1,0:T(8,128)(2,1)} %points.1, bf16[4,16,512]{2,1,0:T(8,128)(2,1)} %weights.1, s32[4,48]{1,0:T(4,128)} %lists.1), custom_call_target="tpu_custom_call" | custom-call | tf_op jit(solution)/shard_map/pack/pallas_call | solution.py:300
  1.1 2.1 %collective-permute-start = (bf16[336,512]{1,0:T(8,128)(2,1)S(1)}, bf16[336,512]{1,0:T(8,128)(2,1)S(1)}, u32[]{:S(2)}, u32[]{:S(2)}) collective-permute-start(bf16[336,512]{1,0:T(8,128)(2,1)S(1)} %get-tuple-element.18.refs_0_), channel_id=1, source_target_pairs={{0,8},{1,9},{2,10},{3,11},{4,12},{5,13},{6,14},{7,15},{8,0},{9,1},... | collective-permute-start | bytes 1032200 | tf_op jit(solution)/shard_map/ppermute | solution.py:34
  3.2 0.0 collective-permute-start.1
  3.2 2.5 %collective-permute-start.2 = (bf16[272,512]{1,0:T(8,128)(2,1)S(1)}, bf16[272,512]{1,0:T(8,128)(2,1)S(1)}, u32[]{:S(2)}, u32[]{:S(2)}) collective-permute-start(bf16[272,512]{1,0:T(8,128)(2,1)S(1)} %get-tuple-element.19.refs_0_), channel_id=1, source_target_pairs={{0,2},{1,3},{2,0},{3,1},{4,6},{5,7},{6,4},{7,5},{8,10},{9,11},{10,... | collective-permute-start | bytes 835592 | tf_op jit(solution)/shard_map/ppermute | solution.py:34
  5.7 1.4 %collective-permute-start.3 = (bf16[272,512]{1,0:T(8,128)(2,1)S(1)}, bf16[272,512]{1,0:T(8,128)(2,1)S(1)}, u32[]{:S(2)}, u32[]{:S(2)}) collective-permute-start(bf16[272,512]{1,0:T(8,128)(2,1)S(1)} %get-tuple-element.19.refs_0_), channel_id=1, source_target_pairs={{0,3},{1,0},{2,1},{3,2},{4,7},{5,4},{6,5},{7,6},{8,11},{9,8},{10,9... | collective-permute-start | bytes 835592 | tf_op jit(solution)/shard_map/ppermute | solution.py:34
  7.2 2.2 %collective-permute-start.5 = (bf16[336,512]{1,0:T(8,128)(2,1)S(1)}, bf16[336,512]{1,0:T(8,128)(2,1)S(1)}, u32[]{:S(2)}, u32[]{:S(2)}) collective-permute-start(bf16[336,512]{1,0:T(8,128)(2,1)S(1)} %get-tuple-element.18.refs_0_), channel_id=1, source_target_pairs={{0,4},{1,5},{2,6},{3,7},{4,8},{5,9},{6,10},{7,11},{8,12},{9,13},{1... | collective-permute-start | bytes 1032200 | tf_op jit(solution)/shard_map/ppermute | solution.py:34
  9.4 0.1 pad_add_fusion.me_ref
  9.4 2.0 %collective-permute-done.1.refs_1_ = bf16[272,512]{1,0:T(8,128)(2,1)S(1)} collective-permute-done((bf16[272,512]{1,0:T(8,128)(2,1)S(1)}, bf16[272,512]{1,0:T(8,128)(2,1)S(1)}, u32[]{:S(2)}, u32[]{:S(2)}) %collective-permute-start.1) | collective-permute-done | bytes 278560 | tf_op jit(solution)/shard_map/ppermute | solution.py:34
  11.5 2.2 %collective-permute-start.7 = (bf16[336,512]{1,0:T(8,128)(2,1)S(1)}, bf16[336,512]{1,0:T(8,128)(2,1)S(1)}, u32[]{:S(2)}, u32[]{:S(2)}) collective-permute-start(bf16[336,512]{1,0:T(8,128)(2,1)S(1)} %get-tuple-element.18.refs_0_), channel_id=1, source_target_pairs={{0,12},{1,13},{2,14},{3,15},{4,0},{5,1},{6,2},{7,3},{8,4},{9,5},{1... | collective-permute-start | bytes 1032200 | tf_op jit(solution)/shard_map/ppermute | solution.py:34
  13.7 4.2 %collective-permute-done.2.refs_2_ = bf16[272,512]{1,0:T(8,128)(2,1)S(1)} collective-permute-done((bf16[272,512]{1,0:T(8,128)(2,1)S(1)}, bf16[272,512]{1,0:T(8,128)(2,1)S(1)}, u32[]{:S(2)}, u32[]{:S(2)}) %collective-permute-start.2) | collective-permute-done | bytes 278560 | tf_op jit(solution)/shard_map/ppermute | solution.py:34
  17.8 4.2 %collective-permute-start.10 = (bf16[336,512]{1,0:T(8,128)(2,1)S(1)}, bf16[336,512]{1,0:T(8,128)(2,1)S(1)}, u32[]{:S(2)}, u32[]{:S(2)}) collective-permute-start(bf16[336,512]{1,0:T(8,128)(2,1)S(1)} %get-tuple-element.18.refs_0_), channel_id=1, source_target_pairs={{16,0},{32,16},{48,32},{64,48},{80,64},{96,80},{112,96},{128,112},... | collective-permute-start | bytes 1032200 | tf_op jit(solution)/shard_map/ppermute | solution.py:341
  22.0 0.0 collective-permute-done.3.refs_3_
  22.0 0.0 collective-permute-start.4
  22.0 3.8 %targets.1 = (bf16[16,80,512]{2,1,0:T(8,128)(2,1)S(1)}, s32[776]{0:T(1024)S(1)}, s32[776]{0:T(1024)S(1)}) custom-call(s32[2]{0:T(128)S(1)} %pad_add_fusion.me_ref, bf16[272,512]{1,0:T(8,128)(2,1)S(1)} %get-tuple-element.19.refs_0_, bf16[272,512]{1,0:T(8,128)(2,1)S(1)} %collective-permute-done.1.refs_1_, bf16[272,512]{1,0:T(8,128)(2,1)S(1)} %collective-permute-done.2.refs_2_, ...), custom_call_target="tpu_custom_call" | custom-call | tf_op jit(solution)/shard_map/targets/pallas_call | solution.py:367
  25.9 0.0 collective-permute-done.refs_2_
  25.9 3.1 %collective-permute-start.13 = (bf16[336,512]{1,0:T(8,128)(2,1)S(1)}, bf16[336,512]{1,0:T(8,128)(2,1)S(1)}, u32[]{:S(2)}, u32[]{:S(2)}) collective-permute-start(bf16[336,512]{1,0:T(8,128)(2,1)S(1)} %collective-permute-done.refs_2_), channel_id=1, source_target_pairs={{16,0},{32,16},{48,32},{64,48},{80,64},{96,80},{112,96},{128,112},... | collective-permute-start | bytes 1032200 | tf_op jit(solution)/shard_map/ppermute | solution.py:370
  29.0 0.0 collective-permute-done.5.refs_1_
  29.0 0.0 collective-permute-start.9
  29.0 0.0 collective-permute-done.7.refs_3_
  29.0 3.0 %collective-permute-start.11 = (bf16[336,512]{1,0:T(8,128)(2,1)S(1)}, bf16[336,512]{1,0:T(8,128)(2,1)S(1)}, u32[]{:S(2)}, u32[]{:S(2)}) collective-permute-start(bf16[336,512]{1,0:T(8,128)(2,1)S(1)} %collective-permute-done.5.refs_1_), channel_id=1, source_target_pairs={{16,0},{32,16},{48,32},{64,48},{80,64},{96,80},{112,96},{128,112},... | collective-permute-start | bytes 1032200 | tf_op jit(solution)/shard_map/ppermute | solution.py:344
  32.0 0.0 collective-permute-done.10.refs_4_
  32.0 0.0 collective-permute-start.6
  32.0 0.0 collective-permute-done.4.refs_0_
  32.0 3.0 %collective-permute-start.12 = (bf16[336,512]{1,0:T(8,128)(2,1)S(1)}, bf16[336,512]{1,0:T(8,128)(2,1)S(1)}, u32[]{:S(2)}, u32[]{:S(2)}) collective-permute-start(bf16[336,512]{1,0:T(8,128)(2,1)S(1)} %collective-permute-done.7.refs_3_), channel_id=1, source_target_pairs={{16,0},{32,16},{48,32},{64,48},{80,64},{96,80},{112,96},{128,112},... | collective-permute-start | bytes 1032200 | tf_op jit(solution)/shard_map/ppermute | solution.py:344
  34.9 0.0 collective-permute-done.13.refs_7_
  34.9 0.0 collective-permute-start.8
  35.0 8.0 %pairs_own.1.refs_9_ = f32[16,16,512]{2,1,0:T(8,128)S(1)} custom-call(s32[776]{0:T(1024)S(1)} %get-tuple-element.26.keys_ref, bf16[336,512]{1,0:T(8,128)(2,1)S(1)} %get-tuple-element.18.refs_0_, bf16[336,512]{1,0:T(8,128)(2,1)S(1)} %collective-permute-done.5.refs_1_, bf16[336,512]{1,0:T(8,128)(2,1)S(1)} %collective-permute-done.refs_2_, ...), custom_call_target="tpu_custom_call" | custom-call | flops 1677721600 | bytes 1376256 | tf_op jit(solution)/shard_map/pairs_own/pallas_call | solution.py:265
  42.9 0.0 collective-permute-done.9.refs_3_
  42.9 0.0 collective-permute-done.11.refs_5_
  42.9 0.0 collective-permute-done.12.refs_6_
  43.0 0.0 collective-permute-done.6.refs_1_
  43.0 1.3 %collective-permute-done.8.refs_2_ = bf16[336,512]{1,0:T(8,128)(2,1)S(1)} collective-permute-done((bf16[336,512]{1,0:T(8,128)(2,1)S(1)}, bf16[336,512]{1,0:T(8,128)(2,1)S(1)}, u32[]{:S(2)}, u32[]{:S(2)}) %collective-permute-start.8) | collective-permute-done | bytes 344096 | tf_op jit(solution)/shard_map/ppermute | solution.py:344
  44.3 8.0 %pairs_far.1 = (f32[4,16,512]{2,1,0:T(8,128)S(1)}, bf16[4,16,512]{2,1,0:T(8,128)(2,1)S(1)}, bf16[4,16,512]{2,1,0:T(8,128)(2,1)S(1)}, bf16[4,16,512]{2,1,0:T(8,128)(2,1)S(1)}) custom-call(s32[776]{0:T(1024)S(1)} %get-tuple-element.23.keys_ref, bf16[336,512]{1,0:T(8,128)(2,1)S(1)} %collective-permute-done.4.refs_0_, ...), custom_call_target="tpu_custom_call" | custom-call | flops 1677721600 | bytes 2752512 | tf_op jit(solution)/shard_map/pairs_far/pallas_call | solution.py:265
  52.3 4.0 %collective-permute-start.14 = (bf16[4,16,512]{2,1,0:T(8,128)(2,1)S(1)}, bf16[4,16,512]{2,1,0:T(8,128)(2,1)S(1)}, u32[]{:S(2)}, u32[]{:S(2)}) collective-permute-start(bf16[4,16,512]{2,1,0:T(8,128)(2,1)S(1)} %get-tuple-element.28), channel_id=1, source_target_pairs={{0,3},{1,0},{2,1},{3,2},{4,7},{5,4},{6,5},{7,6},{8,11},{9,8},{10,9... | collective-permute-start | bytes 196616 | tf_op jit(solution)/shard_map/ppermute | solution.py:34
  56.3 0.0 collective-permute-start.15
  56.3 1.6 %collective-permute-start.16 = (bf16[4,16,512]{2,1,0:T(8,128)(2,1)S(1)}, bf16[4,16,512]{2,1,0:T(8,128)(2,1)S(1)}, u32[]{:S(2)}, u32[]{:S(2)}) collective-permute-start(bf16[4,16,512]{2,1,0:T(8,128)(2,1)S(1)} %get-tuple-element.30), channel_id=1, source_target_pairs={{0,2},{1,3},{2,0},{3,1},{4,6},{5,7},{6,4},{7,5},{8,10},{9,11},{10,... | collective-permute-start | bytes 196616 | tf_op jit(solution)/shard_map/ppermute | solution.py:34
  57.9 0.4 collective-permute-done.14
  58.2 4.3 %collective-permute-done.15 = bf16[4,16,512]{2,1,0:T(8,128)(2,1)S(1)} collective-permute-done((bf16[4,16,512]{2,1,0:T(8,128)(2,1)S(1)}, bf16[4,16,512]{2,1,0:T(8,128)(2,1)S(1)}, u32[]{:S(2)}, u32[]{:S(2)}) %collective-permute-start.15) | collective-permute-done | bytes 65568 | tf_op jit(solution)/shard_map/ppermute | solution.py:34
  62.5 0.0 collective-permute-done.16
  62.5 0.7 %convert_add_fusion = f32[4,16,512]{2,1,0:T(8,128)} fusion(bf16[4,16,512]{2,1,0:T(8,128)(2,1)S(1)} %collective-permute-done.16, bf16[4,16,512]{2,1,0:T(8,128)(2,1)S(1)} %collective-permute-done.15, f32[4,16,512]{2,1,0:T(8,128)S(1)} %get-tuple-element.27, bf16[4,16,512]{2,1,0:T(8,128)(2,1)S(1)} %collective-permute-done.14), kind=kLoop, calls=%fused_computation | loop fusion | flops 196608 | bytes 458752 | tf_op jit(solution)/shard_map/add | solution.py:385
Async XLA Ops:
  1.1 24.8 %collective-permute-start = (bf16[336,512]{1,0:T(8,128)(2,1)S(1)}, bf16[336,512]{1,0:T(8,128)(2,1)S(1)}, u32[]{:S(2)}, u32[]{:S(2)}) collective-permute-start(bf16[336,512]{1,0:T(8,128)(2,1)S(1)} %get-tuple-element.18.refs_0_), channel_id=1, source_target_pairs={{0,8},{1,9},{2,10},{3,11},{4,12},{5,13},{6,14},{7,15},{8,0},{9,1},... | collective-permute-start | bytes 1032200 | tf_op jit(solution)/shard_map/ppermute | solution.py:34
  3.2 8.3 %collective-permute-start.1 = (bf16[272,512]{1,0:T(8,128)(2,1)S(1)}, bf16[272,512]{1,0:T(8,128)(2,1)S(1)}, u32[]{:S(2)}, u32[]{:S(2)}) collective-permute-start(bf16[272,512]{1,0:T(8,128)(2,1)S(1)} %get-tuple-element.19.refs_0_), channel_id=1, source_target_pairs={{0,1},{1,2},{2,3},{3,0},{4,5},{5,6},{6,7},{7,4},{8,9},{9,10},{10,1... | collective-permute-start | bytes 835592 | tf_op jit(solution)/shard_map/ppermute | solution.py:34
  3.2 14.6 %collective-permute-start.2 = (bf16[272,512]{1,0:T(8,128)(2,1)S(1)}, bf16[272,512]{1,0:T(8,128)(2,1)S(1)}, u32[]{:S(2)}, u32[]{:S(2)}) collective-permute-start(bf16[272,512]{1,0:T(8,128)(2,1)S(1)} %get-tuple-element.19.refs_0_), channel_id=1, source_target_pairs={{0,2},{1,3},{2,0},{3,1},{4,6},{5,7},{6,4},{7,5},{8,10},{9,11},{10,... | collective-permute-start | bytes 835592 | tf_op jit(solution)/shard_map/ppermute | solution.py:34
  5.7 16.3 %collective-permute-start.3 = (bf16[272,512]{1,0:T(8,128)(2,1)S(1)}, bf16[272,512]{1,0:T(8,128)(2,1)S(1)}, u32[]{:S(2)}, u32[]{:S(2)}) collective-permute-start(bf16[272,512]{1,0:T(8,128)(2,1)S(1)} %get-tuple-element.19.refs_0_), channel_id=1, source_target_pairs={{0,3},{1,0},{2,1},{3,2},{4,7},{5,4},{6,5},{7,6},{8,11},{9,8},{10,9... | collective-permute-start | bytes 835592 | tf_op jit(solution)/shard_map/ppermute | solution.py:34
  7.2 21.8 %collective-permute-start.5 = (bf16[336,512]{1,0:T(8,128)(2,1)S(1)}, bf16[336,512]{1,0:T(8,128)(2,1)S(1)}, u32[]{:S(2)}, u32[]{:S(2)}) collective-permute-start(bf16[336,512]{1,0:T(8,128)(2,1)S(1)} %get-tuple-element.18.refs_0_), channel_id=1, source_target_pairs={{0,4},{1,5},{2,6},{3,7},{4,8},{5,9},{6,10},{7,11},{8,12},{9,13},{1... | collective-permute-start | bytes 1032200 | tf_op jit(solution)/shard_map/ppermute | solution.py:34
  11.5 17.5 %collective-permute-start.7 = (bf16[336,512]{1,0:T(8,128)(2,1)S(1)}, bf16[336,512]{1,0:T(8,128)(2,1)S(1)}, u32[]{:S(2)}, u32[]{:S(2)}) collective-permute-start(bf16[336,512]{1,0:T(8,128)(2,1)S(1)} %get-tuple-element.18.refs_0_), channel_id=1, source_target_pairs={{0,12},{1,13},{2,14},{3,15},{4,0},{5,1},{6,2},{7,3},{8,4},{9,5},{1... | collective-permute-start | bytes 1032200 | tf_op jit(solution)/shard_map/ppermute | solution.py:34
  17.8 14.1 %collective-permute-start.10 = (bf16[336,512]{1,0:T(8,128)(2,1)S(1)}, bf16[336,512]{1,0:T(8,128)(2,1)S(1)}, u32[]{:S(2)}, u32[]{:S(2)}) collective-permute-start(bf16[336,512]{1,0:T(8,128)(2,1)S(1)} %get-tuple-element.18.refs_0_), channel_id=1, source_target_pairs={{16,0},{32,16},{48,32},{64,48},{80,64},{96,80},{112,96},{128,112},... | collective-permute-start | bytes 1032200 | tf_op jit(solution)/shard_map/ppermute | solution.py:341
  22.0 10.0 %collective-permute-start.4 = (bf16[336,512]{1,0:T(8,128)(2,1)S(1)}, bf16[336,512]{1,0:T(8,128)(2,1)S(1)}, u32[]{:S(2)}, u32[]{:S(2)}) collective-permute-start(bf16[336,512]{1,0:T(8,128)(2,1)S(1)} %get-tuple-element.18.refs_0_), channel_id=1, source_target_pairs={{0,16},{16,32},{32,48},{48,64},{64,80},{80,96},{96,112},{112,128},... | collective-permute-start | bytes 1032200 | tf_op jit(solution)/shard_map/ppermute | solution.py:341
  25.9 9.1 %collective-permute-start.13 = (bf16[336,512]{1,0:T(8,128)(2,1)S(1)}, bf16[336,512]{1,0:T(8,128)(2,1)S(1)}, u32[]{:S(2)}, u32[]{:S(2)}) collective-permute-start(bf16[336,512]{1,0:T(8,128)(2,1)S(1)} %collective-permute-done.refs_2_), channel_id=1, source_target_pairs={{16,0},{32,16},{48,32},{64,48},{80,64},{96,80},{112,96},{128,112},... | collective-permute-start | bytes 1032200 | tf_op jit(solution)/shard_map/ppermute | solution.py:370
  29.0 13.9 %collective-permute-start.9 = (bf16[336,512]{1,0:T(8,128)(2,1)S(1)}, bf16[336,512]{1,0:T(8,128)(2,1)S(1)}, u32[]{:S(2)}, u32[]{:S(2)}) collective-permute-start(bf16[336,512]{1,0:T(8,128)(2,1)S(1)} %collective-permute-done.refs_2_), channel_id=1, source_target_pairs={{0,16},{16,32},{32,48},{48,64},{64,80},{80,96},{96,112},{112,128},... | collective-permute-start | bytes 1032200 | tf_op jit(solution)/shard_map/ppermute | solution.py:370
  29.0 13.9 %collective-permute-start.11 = (bf16[336,512]{1,0:T(8,128)(2,1)S(1)}, bf16[336,512]{1,0:T(8,128)(2,1)S(1)}, u32[]{:S(2)}, u32[]{:S(2)}) collective-permute-start(bf16[336,512]{1,0:T(8,128)(2,1)S(1)} %collective-permute-done.5.refs_1_), channel_id=1, source_target_pairs={{16,0},{32,16},{48,32},{64,48},{80,64},{96,80},{112,96},{128,112},... | collective-permute-start | bytes 1032200 | tf_op jit(solution)/shard_map/ppermute | solution.py:344
  32.0 11.0 %collective-permute-start.6 = (bf16[336,512]{1,0:T(8,128)(2,1)S(1)}, bf16[336,512]{1,0:T(8,128)(2,1)S(1)}, u32[]{:S(2)}, u32[]{:S(2)}) collective-permute-start(bf16[336,512]{1,0:T(8,128)(2,1)S(1)} %collective-permute-done.5.refs_1_), channel_id=1, source_target_pairs={{0,16},{16,32},{32,48},{48,64},{64,80},{80,96},{96,112},{112,128},... | collective-permute-start | bytes 1032200 | tf_op jit(solution)/shard_map/ppermute | solution.py:344
  32.0 11.0 %collective-permute-start.12 = (bf16[336,512]{1,0:T(8,128)(2,1)S(1)}, bf16[336,512]{1,0:T(8,128)(2,1)S(1)}, u32[]{:S(2)}, u32[]{:S(2)}) collective-permute-start(bf16[336,512]{1,0:T(8,128)(2,1)S(1)} %collective-permute-done.7.refs_3_), channel_id=1, source_target_pairs={{16,0},{32,16},{48,32},{64,48},{80,64},{96,80},{112,96},{128,112},... | collective-permute-start | bytes 1032200 | tf_op jit(solution)/shard_map/ppermute | solution.py:344
  34.9 9.3 %collective-permute-start.8 = (bf16[336,512]{1,0:T(8,128)(2,1)S(1)}, bf16[336,512]{1,0:T(8,128)(2,1)S(1)}, u32[]{:S(2)}, u32[]{:S(2)}) collective-permute-start(bf16[336,512]{1,0:T(8,128)(2,1)S(1)} %collective-permute-done.7.refs_3_), channel_id=1, source_target_pairs={{0,16},{16,32},{32,48},{48,64},{64,80},{80,96},{96,112},{112,128},... | collective-permute-start | bytes 1032200 | tf_op jit(solution)/shard_map/ppermute | solution.py:344
  52.3 5.9 %collective-permute-start.14 = (bf16[4,16,512]{2,1,0:T(8,128)(2,1)S(1)}, bf16[4,16,512]{2,1,0:T(8,128)(2,1)S(1)}, u32[]{:S(2)}, u32[]{:S(2)}) collective-permute-start(bf16[4,16,512]{2,1,0:T(8,128)(2,1)S(1)} %get-tuple-element.28), channel_id=1, source_target_pairs={{0,3},{1,0},{2,1},{3,2},{4,7},{5,4},{6,5},{7,6},{8,11},{9,8},{10,9... | collective-permute-start | bytes 196616 | tf_op jit(solution)/shard_map/ppermute | solution.py:34
  56.3 6.2 %collective-permute-start.15 = (bf16[4,16,512]{2,1,0:T(8,128)(2,1)S(1)}, bf16[4,16,512]{2,1,0:T(8,128)(2,1)S(1)}, u32[]{:S(2)}, u32[]{:S(2)}) collective-permute-start(bf16[4,16,512]{2,1,0:T(8,128)(2,1)S(1)} %get-tuple-element.29), channel_id=1, source_target_pairs={{0,1},{1,2},{2,3},{3,0},{4,5},{5,6},{6,7},{7,4},{8,9},{9,10},{10,1... | collective-permute-start | bytes 196616 | tf_op jit(solution)/shard_map/ppermute | solution.py:34
  56.3 6.2 %collective-permute-start.16 = (bf16[4,16,512]{2,1,0:T(8,128)(2,1)S(1)}, bf16[4,16,512]{2,1,0:T(8,128)(2,1)S(1)}, u32[]{:S(2)}, u32[]{:S(2)}) collective-permute-start(bf16[4,16,512]{2,1,0:T(8,128)(2,1)S(1)} %get-tuple-element.30), channel_id=1, source_target_pairs={{0,2},{1,3},{2,0},{3,1},{4,6},{5,7},{6,4},{7,5},{8,10},{9,11},{10,... | collective-permute-start | bytes 196616 | tf_op jit(solution)/shard_map/ppermute | solution.py:34
